TPU v7x, 32 devices: a whole 2x2x4 slice. The times are simulated.
32 devices in a mesh: ctx: 8 (over y, x, core), head: 4 (over z).
Axes of the slice: x: 2, y: 2, z: 4, core: 2. Of those that a mesh axis runs over, the one named last changes fastest.
Arguments:
- row_query: bfloat16 [8192, 3072], P('ctx', 'head'), may hold values from -160 to 160
- row_key: bfloat16 [8192, 3072], P('ctx', 'head'), may hold values from -5 to 5
- row_value: bfloat16 [8192, 3072], P('ctx', 'head'), may hold values from -6 to 6
- row_cotangent: bfloat16 [8192, 3072], P('ctx', 'head'), may hold values from -6 to 6
- row_mask: int32 [64, 9], replicated, may hold values from 0 to 1, as said below
- col_query: bfloat16 [8192, 3072], P('ctx', 'head'), may hold values from -160 to 160
- col_key: bfloat16 [8192, 3072], P('ctx', 'head'), may hold values from -5 to 5
- col_value: bfloat16 [8192, 3072], P('ctx', 'head'), may hold values from -6 to 6
- col_cotangent: bfloat16 [8192, 3072], P('ctx', 'head'), may hold values from -6 to 6
- col_mask: int32 [64, 64], replicated, may hold values from 0 to 1, as said below
Outputs:
- row_output: bfloat16 [8192, 3072], P('ctx', 'head')
- row_dquery: bfloat16 [8192, 3072], P('ctx', 'head')
- row_dkeys: bfloat16 [8192, 3072], P('ctx', 'head')
- row_dvalues: bfloat16 [8192, 3072], P('ctx', 'head')
- col_output: bfloat16 [8192, 3072], P('ctx', 'head')
- col_dquery: bfloat16 [8192, 3072], P('ctx', 'head')
- col_dkeys: bfloat16 [8192, 3072], P('ctx', 'head')
- col_dvalues: bfloat16 [8192, 3072], P('ctx', 'head')
Inputs may be any that keep to these rules, and one draw needn't show every extreme that they name: row_mask[r, 4] = 1 for every r, row_mask[r, 3] = 1 for even r and row_mask[r, 5] = 1 for odd r; entries that point outside the grid are ignored. col_mask[r, r] = 1 for every r and col_mask[r, r - 1] = 1 for r >= 1.
All inputs are finite; a program needn't handle non-finite values.
Results may differ from a plain program's by a relative error of at most 0.022.
Values may be sent and summed in bfloat16 or wider, within the bound.
No kernel may reach another device: no remote copies, remote signals or barrier semaphores. Data moves between devices by JAX's collectives and lax.ppermute only.
A program may use at most 192 MiB of HBM per device.

v0:
```python
import jax
import jax.numpy as jnp
from jax import lax
from jax.sharding import PartitionSpec as P

HEAD_DIM = 128
GRIDC = 128


masked_score = -1e30


def padded_2(array, sides, width):
    for axis, dim in sides:
        size, length = (lax.axis_size(axis), array.shape[dim])
        up = [(i, (i + 1) % size) for i in range(size - 1)]
        down = [(j, i) for i, j in up]
        last = lax.slice_in_dim(array, length - width, length, axis=dim)
        initial = lax.slice_in_dim(array, 0, width, axis=dim)
        before = lax.ppermute(last, axis, up)
        after = lax.ppermute(initial, axis, down)
        array = jnp.concatenate([before, array, after], axis=dim)
    return array


def passed_along(block, axis, distance):
    devices = range(lax.axis_size(axis))
    route = [(i - distance, i) for i in devices if i - distance in devices]
    return lax.ppermute(block, axis, route)


def attend_block(queries, key_block, value_block, cotangent, allowed):
    scale = queries.shape[-1] ** (-0.5)
    scores = (
        jnp.einsum("bnd,bmd->bnm", queries, key_block, preferred_element_type=jnp.float32) * scale
    )
    scores = jnp.where(allowed, scores, masked_score)
    row_max = jnp.max(scores, axis=-1, keepdims=True)
    exp_terms = jnp.where(allowed, jnp.exp(scores - row_max), 0.0)
    attn_prob = exp_terms / jnp.sum(exp_terms, axis=-1, keepdims=True)
    prob_low = attn_prob.astype(jnp.bfloat16)
    output = jnp.einsum(
        "bnm,bmd->bnd", prob_low, value_block, preferred_element_type=jnp.float32
    ).astype(jnp.bfloat16)
    d_prob = jnp.einsum("bnd,bmd->bnm", cotangent, value_block, preferred_element_type=jnp.float32)
    delta_sum = jnp.sum(
        cotangent.astype(jnp.float32) * output.astype(jnp.float32), axis=-1, keepdims=True
    )
    d_scores = (attn_prob * (d_prob - delta_sum)).astype(jnp.bfloat16)
    grad_query = (
        jnp.einsum("bnm,bmd->bnd", d_scores, key_block, preferred_element_type=jnp.float32) * scale
    ).astype(jnp.bfloat16)
    grad_keys = (
        jnp.einsum("bnm,bnd->bmd", d_scores, queries, preferred_element_type=jnp.float32) * scale
    )
    grad_values = jnp.einsum(
        "bnm,bnd->bmd", prob_low, cotangent, preferred_element_type=jnp.float32
    )
    return (output, grad_query, grad_keys, grad_values)


def row_allowed(mask_rows, first, nrows, window, band, total_rows, grid_cols):
    query_rows = first + jnp.arange(nrows)[:, None]
    block_rows = query_rows + jnp.arange(window)[None, :] - band
    valid = (block_rows >= 0) & (block_rows < total_rows) & (mask_rows == 1)
    outside = (query_rows < 0) | (query_rows >= total_rows)
    valid = valid | outside
    return jnp.repeat(valid, grid_cols, axis=1)[:, None, :]


def row_pass(queries, pairs, cotangent, allowed, nrows, band, window, grid_cols):
    head_dim = HEAD_DIM
    heads = queries.shape[1] // head_dim
    head_queries = queries.reshape(nrows, grid_cols, heads, head_dim).transpose(2, 0, 1, 3)
    head_cotangent = cotangent.reshape(nrows, grid_cols, heads, head_dim).transpose(2, 0, 1, 3)
    head_pairs = pairs.reshape(2, nrows + 2 * band, grid_cols, heads, head_dim).transpose(
        3, 0, 1, 2, 4
    )

    def one_head(operands):
        head_q, head_kv, head_cot = operands
        windows = jnp.stack([head_kv[:, offset : offset + nrows] for offset in range(window)], 2)
        windows = windows.reshape(2, nrows, window * grid_cols, head_dim)
        output, grad_query, grad_keys, grad_values = attend_block(
            head_q, windows[0], windows[1], head_cot, allowed
        )
        grads = jnp.stack([grad_keys, grad_values]).reshape(2, nrows, window, grid_cols, head_dim)
        accum = jnp.zeros((2, nrows + 2 * band, grid_cols, head_dim), jnp.float32)
        for offset in range(window):
            accum = accum.at[:, offset : offset + nrows].add(grads[:, :, offset])
        return (output, grad_query, accum)

    return lax.map(one_head, (head_queries, head_pairs, head_cotangent))


def body(
    row_query,
    row_key,
    row_value,
    row_cotangent,
    row_mask,
    col_query,
    col_key,
    col_value,
    col_cotangent,
    col_mask,
):
    head_dim = HEAD_DIM
    grid_cols = GRIDC
    tokens = row_query.shape[0]
    rows_here = tokens // grid_cols
    window = row_mask.shape[1]
    band = (window - 1) // 2
    row_feat = row_query.shape[1]
    first_row = lax.axis_index("ctx") * rows_here
    total_rows = rows_here * lax.axis_size("ctx")
    key_value = jnp.stack([row_key, row_value])
    padded = padded_2(key_value, (("ctx", 1),), band * grid_cols)
    mask_rows = lax.dynamic_slice_in_dim(row_mask, first_row, rows_here, 0)
    allowed_rows = row_allowed(mask_rows, first_row, rows_here, window, band, total_rows, grid_cols)
    outputs, grad_queries, accums = row_pass(
        row_query, padded, row_cotangent, allowed_rows, rows_here, band, window, grid_cols
    )
    lower_rim = accums[:, :, :band]
    upper_rim = accums[:, :, band + rows_here :]
    own_grads = accums[:, :, band : band + rows_here]
    from_next = passed_along(lower_rim.astype(jnp.bfloat16), "ctx", -1).astype(lower_rim.dtype)
    from_prev = passed_along(upper_rim.astype(jnp.bfloat16), "ctx", 1).astype(upper_rim.dtype)
    own_grads = own_grads.at[:, :, rows_here - band :].add(from_next)
    own_grads = own_grads.at[:, :, :band].add(from_prev)
    own_grads = own_grads.transpose(1, 2, 3, 0, 4).reshape(2, tokens, row_feat).astype(jnp.bfloat16)
    row_output = outputs.transpose(1, 2, 0, 3).reshape(tokens, row_feat)
    row_dquery = grad_queries.transpose(1, 2, 0, 3).reshape(tokens, row_feat)
    row_dkeys = own_grads[0]
    row_dvalues = own_grads[1]
    col_feat = col_query.shape[1]
    n_ctx = lax.axis_size("ctx")
    grid_rows = rows_here * n_ctx
    stacked = jnp.stack([col_query, col_key, col_value, col_cotangent]).reshape(
        4, rows_here, grid_cols, col_feat
    )
    moved = lax.all_to_all(stacked, "ctx", split_axis=2, concat_axis=1, tiled=True)
    cols_here = moved.shape[2]
    all_heads = moved.shape[3] // head_dim
    batched = moved.reshape(4, grid_rows, cols_here, all_heads, head_dim).transpose(0, 2, 3, 1, 4)
    batched = batched.reshape(4, cols_here * all_heads, grid_rows, head_dim)
    allowed_cols = (col_mask == 1)[None]
    output, grad_query, grad_keys, grad_values = attend_block(
        batched[0], batched[1], batched[2], batched[3], allowed_cols
    )
    results = jnp.stack(
        [output, grad_query, grad_keys.astype(jnp.bfloat16), grad_values.astype(jnp.bfloat16)]
    )
    results = results.reshape(4, cols_here, all_heads, grid_rows, head_dim).transpose(0, 3, 1, 2, 4)
    results = results.reshape(4, grid_rows, cols_here, all_heads * head_dim)
    returned = lax.all_to_all(results, "ctx", split_axis=1, concat_axis=2, tiled=True)
    returned = returned.reshape(4, tokens, col_feat)
    return (
        row_output,
        row_dquery,
        row_dkeys,
        row_dvalues,
        returned[0],
        returned[1],
        returned[2],
        returned[3],
    )


def solution(mesh):
    return jax.shard_map(
        body,
        mesh=mesh,
        in_specs=(
            P("ctx", "head"),
            P("ctx", "head"),
            P("ctx", "head"),
            P("ctx", "head"),
            P(),
            P("ctx", "head"),
            P("ctx", "head"),
            P("ctx", "head"),
            P("ctx", "head"),
            P(),
        ),
        out_specs=(
            P("ctx", "head"),
            P("ctx", "head"),
            P("ctx", "head"),
            P("ctx", "head"),
            P("ctx", "head"),
            P("ctx", "head"),
            P("ctx", "head"),
            P("ctx", "head"),
        ),
        check_vma=False,
    )
```

profile of v0, /device:TPU:11, one launch (start us, length us, event | category | flops | bytes accessed | tf_op | source)
XLA Modules:
  0.0 450.1 jit_solution(2632079442033608553)
XLA Ops:
  0.6 3.7 pad_maximum_fusion.2
  4.4 6.3 %copy.209 = bf16[4,8,128,768]{3,1,0,2:T(8,128)(2,1)} copy(bf16[4,8,128,768]{3,2,1,0:T(8,128)(2,1)S(1)} %pad_maximum_fusion.2) | data formatting | bytes 12582912 | tf_op jit(solution)/shard_map/stack | solution.py:139
  10.6 5.8 %all-to-all-start = ((bf16[4,8,128,768]{3,1,0,2:T(8,128)(2,1)}), bf16[4,8,128,768]{3,1,0,2:T(8,128)(2,1)}, u32[]{:S(2)}, u32[]{:S(2)}) async-start(bf16[4,8,128,768]{3,1,0,2:T(8,128)(2,1)} %copy.209), calls=%async_computation | async-start | bytes 12582912 | tf_op jit(solution)/shard_map/all_to_all | solution.py:142
  16.4 1.9 fusion.67
  18.2 2.3 collective-permute-start.1
  20.5 4.4 collective-permute-start
  24.9 2.6 copy.197
  27.5 3.0 copy.263
  30.5 2.6 copy.199
  33.1 3.0 copy.265
  36.3 83.7 %collective-permute-done.1 = bf16[2,512,768]{2,1,0:T(8,128)(2,1)} collective-permute-done((bf16[2,512,768]{2,1,0:T(8,128)(2,1)}, bf16[2,512,768]{2,1,0:T(8,128)(2,1)}, u32[]{:S(2)}, u32[]{:S(2)}) %collective-permute-start.1) | collective-permute-done | bytes 1572896 | tf_op jit(solution)/shard_map/ppermute | solution.py:21
  120.0 5.1 %pad_maximum_fusion.1 = bf16[2,2048,768]{2,1,0:T(8,128)(2,1)} fusion(bf16[2,512,768]{2,1,0:T(8,128)(2,1)} %collective-permute-done.1, bf16[1,1024,768]{2,1,0:T(8,128)(2,1)S(1)} %bitcast.375, bf16[1,1024,768]{2,1,0:T(8,128)(2,1)S(1)} %bitcast.373, bf16[2,512,768]{2,1,0:T(8,128)(2,1)} %collective-permute-done), kind=kLoop, calls=%fused_computation.102 | loop fusion | flops 25165824 | bytes 12582912 | tf_op jit(solution)/shard_map/concatenate | solution.py:22
  125.2 8.7 %copy.198 = bf16[2,2048,768]{1,2,0:T(8,128)(2,1)} copy(bf16[2,2048,768]{2,1,0:T(8,128)(2,1)} %pad_maximum_fusion.1) | data formatting | bytes 12582912 | tf_op jit(solution)/shard_map/concatenate | solution.py:22
  133.8 7.7 %copy.264 = bf16[192,8,16,128]{3,2,1,0:T(8,128)(2,1)} copy(bf16[192,8,16,128]{3,1,2,0:T(8,128)(2,1)} %bitcast.366) | data formatting | bytes 12582912
  141.6 10.6 %copy.211 = bf16[4,8,8,16,768]{4,3,2,1,0:T(8,128)(2,1)} copy(bf16[4,8,8,16,768]{4,2,0,3,1:T(8,128)(2,1)} %bitcast.14) | data formatting | bytes 12582912 | tf_op jit(solution)/shard_map/all_to_all | solution.py:142
  152.2 13.6 %reshape.576 = bf16[4,64,16,6,128]{4,3,2,1,0:T(8,128)(2,1)} reshape(bf16[4,8,8,16,768]{4,3,2,1,0:T(8,128)(2,1)} %copy.211) | data formatting | bytes 12582912 | tf_op jit(solution)/shard_map/reshape | solution.py:145
  165.8 5.8 %fusion.85 = (bf16[1,16,6,64,128]{4,2,1,3,0:T(8,128)(2,1)S(1)}, bf16[1,16,6,64,128]{4,2,1,3,0:T(8,128)(2,1)S(1)}, bf16[1,16,6,64,128]{4,2,1,3,0:T(8,128)(2,1)S(1)}, bf16[1,16,6,64,128]{4,2,1,3,0:T(8,128)(2,1)S(1)}) fusion(bf16[4,16,6,64,128]{4,2,1,3,0:T(8,128)(2,1)} %bitcast.364), kind=kLoop, calls=%fused_computation.144 | loop fusion | bytes 12582912 | tf_op jit(solution)/shard_map/slice | solution.py:149
  171.6 2.2 copy.216
  175.8 2.2 copy.214
  177.9 3.2 fusion.89
  181.2 3.1 convolution_convert_fusion.1
  193.7 4.4 maximum_bitcast_fusion
  198.1 13.8 %reshape.577 = bf16[4,64,16,768]{3,2,1,0:T(8,128)(2,1)} reshape(bf16[4,64,16,6,128]{4,3,2,1,0:T(8,128)(2,1)} %maximum_bitcast_fusion) | data formatting | bytes 12582912 | tf_op jit(solution)/shard_map/reshape | solution.py:155
  211.9 6.3 %copy.223 = bf16[4,64,16,768]{3,2,0,1:T(8,128)(2,1)} copy(bf16[4,64,16,768]{3,2,1,0:T(8,128)(2,1)} %reshape.577) | data formatting | bytes 12582912 | tf_op jit(solution)/shard_map/reshape | solution.py:155
  218.2 4.7 %all-to-all-start.1 = ((bf16[4,64,16,768]{3,2,0,1:T(8,128)(2,1)}), bf16[4,64,16,768]{3,2,0,1:T(8,128)(2,1)}, u32[]{:S(2)}, u32[]{:S(2)}) async-start(bf16[4,64,16,768]{3,2,0,1:T(8,128)(2,1)} %copy.223), calls=%async_computation.1 | async-start | bytes 12582912 | tf_op jit(solution)/shard_map/all_to_all | solution.py:156
  222.9 160.0 %while.29 = (s32[]{:T(128)}, bf16[6,8,128,128]{2,3,1,0:T(8,128)(2,1)}, bf16[6,8,128,128]{3,2,1,0:T(8,128)(2,1)}, f32[6,2,16,128,128]{4,3,2,1,0:T(8,128)}, bf16[6...) while((s32[]{:T(128)}, ...), condition=%wide.region_4.5_spmd.clone, body=%wide.region_0.4_spmd.clone.sunk | while | flops 1831469184 | bytes 216832256 | solution.py:93
  226.0 2.4 fusion.165
  229.8 5.7 %fusion.166 = (f32[8,128]{1,0:T(8,128)S(1)}, f32[8,128,1152]{2,1,0:T(8,128)}) fusion(bf16[8,1152,128]{2,1,0:T(8,128)(2,1)} %bitcast.362, pred[8,1152]{1,0:T(8,128)(4,1)S(1)} %broadcast_bitcast_fusion.2, bf16[1,8,128,128]{3,2,1,0:T(8,128)(2,1)S(1)} %copy.288), kind=kOutput, calls=%fused_computation.143.clone.1 | convolution fusion | flops 307889280 | bytes 7353344 | tf_op jit(solution)/shard_map/while/body/eval_jaxpr/sub | solution.py:39
  235.5 2.8 fusion.167
  238.4 1.7 bitcast_dynamic-update-slice_fusion.2
  252.7 2.4 fusion.165
  256.4 5.7 %fusion.166 = (f32[8,128]{1,0:T(8,128)S(1)}, f32[8,128,1152]{2,1,0:T(8,128)}) fusion(bf16[8,1152,128]{2,1,0:T(8,128)(2,1)} %bitcast.362, pred[8,1152]{1,0:T(8,128)(4,1)S(1)} %broadcast_bitcast_fusion.2, bf16[1,8,128,128]{3,2,1,0:T(8,128)(2,1)S(1)} %copy.288), kind=kOutput, calls=%fused_computation.143.clone.1 | convolution fusion | flops 307889280 | bytes 7353344 | tf_op jit(solution)/shard_map/while/body/eval_jaxpr/sub | solution.py:39
  262.1 2.8 fusion.167
  265.0 1.7 bitcast_dynamic-update-slice_fusion.2
  279.3 2.4 fusion.165
  283.0 5.7 %fusion.166 = (f32[8,128]{1,0:T(8,128)S(1)}, f32[8,128,1152]{2,1,0:T(8,128)}) fusion(bf16[8,1152,128]{2,1,0:T(8,128)(2,1)} %bitcast.362, pred[8,1152]{1,0:T(8,128)(4,1)S(1)} %broadcast_bitcast_fusion.2, bf16[1,8,128,128]{3,2,1,0:T(8,128)(2,1)S(1)} %copy.288), kind=kOutput, calls=%fused_computation.143.clone.1 | convolution fusion | flops 307889280 | bytes 7353344 | tf_op jit(solution)/shard_map/while/body/eval_jaxpr/sub | solution.py:39
  288.7 2.8 fusion.167
  291.6 1.7 bitcast_dynamic-update-slice_fusion.2
  301.4 1.5 constant_dynamic-update-slice_fusion.2
  305.9 2.4 fusion.165
  309.7 5.7 %fusion.166 = (f32[8,128]{1,0:T(8,128)S(1)}, f32[8,128,1152]{2,1,0:T(8,128)}) fusion(bf16[8,1152,128]{2,1,0:T(8,128)(2,1)} %bitcast.362, pred[8,1152]{1,0:T(8,128)(4,1)S(1)} %broadcast_bitcast_fusion.2, bf16[1,8,128,128]{3,2,1,0:T(8,128)(2,1)S(1)} %copy.288), kind=kOutput, calls=%fused_computation.143.clone.1 | convolution fusion | flops 307889280 | bytes 7353344 | tf_op jit(solution)/shard_map/while/body/eval_jaxpr/sub | solution.py:39
  315.4 2.8 fusion.167
  318.2 1.7 bitcast_dynamic-update-slice_fusion.2
  332.6 2.4 fusion.165
  336.3 5.7 %fusion.166 = (f32[8,128]{1,0:T(8,128)S(1)}, f32[8,128,1152]{2,1,0:T(8,128)}) fusion(bf16[8,1152,128]{2,1,0:T(8,128)(2,1)} %bitcast.362, pred[8,1152]{1,0:T(8,128)(4,1)S(1)} %broadcast_bitcast_fusion.2, bf16[1,8,128,128]{3,2,1,0:T(8,128)(2,1)S(1)} %copy.288), kind=kOutput, calls=%fused_computation.143.clone.1 | convolution fusion | flops 307889280 | bytes 7353344 | tf_op jit(solution)/shard_map/while/body/eval_jaxpr/sub | solution.py:39
  342.0 2.8 fusion.167
  344.9 1.7 bitcast_dynamic-update-slice_fusion.2
  354.7 1.5 constant_dynamic-update-slice_fusion.2
  359.2 2.4 fusion.165
  363.0 5.7 %fusion.166 = (f32[8,128]{1,0:T(8,128)S(1)}, f32[8,128,1152]{2,1,0:T(8,128)}) fusion(bf16[8,1152,128]{2,1,0:T(8,128)(2,1)} %bitcast.362, pred[8,1152]{1,0:T(8,128)(4,1)S(1)} %broadcast_bitcast_fusion.2, bf16[1,8,128,128]{3,2,1,0:T(8,128)(2,1)S(1)} %copy.288), kind=kOutput, calls=%fused_computation.143.clone.1 | convolution fusion | flops 307889280 | bytes 7353344 | tf_op jit(solution)/shard_map/while/body/eval_jaxpr/sub | solution.py:39
  368.7 2.8 fusion.167
  371.6 1.7 bitcast_dynamic-update-slice_fusion.2
  383.0 6.2 %convert.4 = bf16[6,2,16,128,128]{4,3,2,1,0:T(8,128)(2,1)S(1)} convert(f32[6,2,16,128,128]{4,3,2,1,0:T(8,128)} %get-tuple-element.300) | non-fusion elementwise | flops 3145728 | bytes 18874368 | tf_op jit(solution)/shard_map/convert.1
  389.2 1.9 fusion.87
  391.0 1.9 collective-permute-start.2
  393.0 4.7 %collective-permute-start.3 = (bf16[6,2,4,128,128]{4,3,2,1,0:T(8,128)(2,1)}, bf16[6,2,4,128,128]{4,3,2,1,0:T(8,128)(2,1)}, u32[]{:S(2)}, u32[]{:S(2)}) collective-permute-start(bf16[6,2,4,128,128]{4,3,2,1,0:T(8,128)(2,1)} %get-tuple-element.424), channel_id=1, source_target_pairs={{0,4},{4,8},{8,12},{12,16},{16,20},{20,24},{24,28},{1,5},{5,9},{9,... | collective-permute-start | bytes 4718600 | tf_op jit(solution)/shard_map/ppermute | solution.py:29
  397.7 6.3 %slice.552 = f32[6,2,8,128,128]{4,3,2,1,0:T(8,128)} slice(f32[6,2,16,128,128]{4,3,2,1,0:T(8,128)} %get-tuple-element.300), slice={[0:6], [0:2], [4:12], [0:128], [0:128]} | slice | bytes 12582912 | tf_op jit(solution)/shard_map/slice | solution.py:126
  405.1 3.9 copy.241
  409.0 4.4 copy_bitcast_fusion.5
  413.3 16.9 %collective-permute-done.2 = bf16[6,2,4,128,128]{4,3,2,1,0:T(8,128)(2,1)} collective-permute-done((bf16[6,2,4,128,128]{4,3,2,1,0:T(8,128)(2,1)}, bf16[6,2,4,128,128]{4,3,2,1,0:T(8,128)(2,1)}, u32[]{:S(2)}, u32[]{:S(2)}) %collective-permute-start.2) | collective-permute-done | bytes 1572896 | tf_op jit(solution)/shard_map/ppermute | solution.py:29
  430.2 2.8 add_dynamic-update-slice_fusion
  433.0 2.2 fusion.65
  438.4 2.6 copy_bitcast_fusion.3
  441.0 3.4 copy.224
  (258 shorter events, 101.4 us)
Async XLA Ops:
  10.6 5.8 %copy-start.3 = (bf16[1024,768]{1,0:T(8,128)(2,1)S(1)}, bf16[1024,768]{1,0:T(8,128)(2,1)}, u32[]{:S(2)}) copy-start(bf16[1024,768]{1,0:T(8,128)(2,1)} %param.35) | copy-start | bytes 4718596
  10.6 5.8 %copy-start.4 = (bf16[1024,768]{1,0:T(8,128)(2,1)S(1)}, bf16[1024,768]{1,0:T(8,128)(2,1)}, u32[]{:S(2)}) copy-start(bf16[1024,768]{1,0:T(8,128)(2,1)} %param.36) | copy-start | bytes 4718596
  10.6 130.9 %all-to-all-start = ((bf16[4,8,128,768]{3,1,0,2:T(8,128)(2,1)}), bf16[4,8,128,768]{3,1,0,2:T(8,128)(2,1)}, u32[]{:S(2)}, u32[]{:S(2)}) async-start(bf16[4,8,128,768]{3,1,0,2:T(8,128)(2,1)} %copy.209), calls=%async_computation | async-start | bytes 12582912 | tf_op jit(solution)/shard_map/all_to_all | solution.py:142
  18.2 101.8 %collective-permute-start.1 = (bf16[2,512,768]{2,1,0:T(8,128)(2,1)}, bf16[2,512,768]{2,1,0:T(8,128)(2,1)}, u32[]{:S(2)}, u32[]{:S(2)}) collective-permute-start(bf16[2,512,768]{2,1,0:T(8,128)(2,1)} %get-tuple-element.429), channel_id=1, source_target_pairs={{4,0},{8,4},{12,8},{16,12},{20,16},{24,20},{28,24},{5,1},{9,5},{13... | collective-permute-start | bytes 4718600 | tf_op jit(solution)/shard_map/ppermute | solution.py:21
  20.5 99.5 %collective-permute-start = (bf16[2,512,768]{2,1,0:T(8,128)(2,1)}, bf16[2,512,768]{2,1,0:T(8,128)(2,1)}, u32[]{:S(2)}, u32[]{:S(2)}) collective-permute-start(bf16[2,512,768]{2,1,0:T(8,128)(2,1)} %get-tuple-element.428), channel_id=1, source_target_pairs={{0,4},{4,8},{8,12},{12,16},{16,20},{20,24},{24,28},{1,5},{5,9},{9,... | collective-permute-start | bytes 4718600 | tf_op jit(solution)/shard_map/ppermute | solution.py:20
  33.1 3.0 copy-start.8
  33.1 3.2 copy-start.9
  181.2 3.1 copy-start.6
  181.2 3.3 copy-start.7
  181.2 4.3 copy-start.10
  218.2 222.7 %all-to-all-start.1 = ((bf16[4,64,16,768]{3,2,0,1:T(8,128)(2,1)}), bf16[4,64,16,768]{3,2,0,1:T(8,128)(2,1)}, u32[]{:S(2)}, u32[]{:S(2)}) async-start(bf16[4,64,16,768]{3,2,0,1:T(8,128)(2,1)} %copy.223), calls=%async_computation.1 | async-start | bytes 12582912 | tf_op jit(solution)/shard_map/all_to_all | solution.py:156
  238.3 2.4 copy-start
  240.8 1.7 copy-start.1
  265.0 2.4 copy-start
  267.4 1.7 copy-start.1
  291.6 2.4 copy-start
  294.0 1.7 copy-start.1
  318.2 2.4 copy-start
  320.7 1.7 copy-start.1
  344.9 2.4 copy-start
  347.3 1.7 copy-start.1
  371.5 2.4 copy-start
  374.0 1.7 copy-start.1
  391.0 39.2 %collective-permute-start.2 = (bf16[6,2,4,128,128]{4,3,2,1,0:T(8,128)(2,1)}, bf16[6,2,4,128,128]{4,3,2,1,0:T(8,128)(2,1)}, u32[]{:S(2)}, u32[]{:S(2)}) collective-permute-start(bf16[6,2,4,128,128]{4,3,2,1,0:T(8,128)(2,1)} %get-tuple-element.425), channel_id=1, source_target_pairs={{4,0},{8,4},{12,8},{16,12},{20,16},{24,20},{28,24},{5,1},{9,5},{13... | collective-permute-start | bytes 4718600 | tf_op jit(solution)/shard_map/ppermute | solution.py:29
  393.0 11.0 %copy-start.5 = (bf16[6,8,128,128]{3,2,1,0:T(8,128)(2,1)S(1)}, bf16[6,8,128,128]{3,2,1,0:T(8,128)(2,1)}, u32[]{:S(2)}) copy-start(bf16[6,8,128,128]{3,2,1,0:T(8,128)(2,1)} %get-tuple-element.299) | copy-start | bytes 4718596
  393.0 40.0 %collective-permute-start.3 = (bf16[6,2,4,128,128]{4,3,2,1,0:T(8,128)(2,1)}, bf16[6,2,4,128,128]{4,3,2,1,0:T(8,128)(2,1)}, u32[]{:S(2)}, u32[]{:S(2)}) collective-permute-start(bf16[6,2,4,128,128]{4,3,2,1,0:T(8,128)(2,1)} %get-tuple-element.424), channel_id=1, source_target_pairs={{0,4},{4,8},{8,12},{12,16},{16,20},{20,24},{24,28},{1,5},{5,9},{9,... | collective-permute-start | bytes 4718600 | tf_op jit(solution)/shard_map/ppermute | solution.py:29
  409.0 21.2 %copy-start.2 = (f32[6,2,8,128,128]{4,3,2,1,0:T(8,128)S(1)}, f32[6,2,8,128,128]{4,3,2,1,0:T(8,128)}, u32[]{:S(2)}) copy-start(f32[6,2,8,128,128]{4,3,2,1,0:T(8,128)} %slice.552) | copy-start | bytes 18874372
where the time goes:
time: 457 us; the launch traced here: 450 us
  local copies, waits for them, and re-layouts  185 us (40%)
  waiting for transfers between devices  101 us (22%)
  matrix products  82.3 us (18%)
  other arithmetic  56.6 us (12%)
  starting transfers between devices  23.7 us (5%)
    ppermute x1, waiting for transfers between devices, padded_2(): after = lax.ppermute(initial, axis, down)  83.7 us
    sub x7, matrix products, attend_block(): exp_terms = jnp.where(allowed, jnp.exp(scores - row_max), 0.0)  37.6 us
    unnamed x29, local copies, waits for them, and re-layouts  34.3 us
    dynamic_slice x24, local copies, waits for them, and re-layouts, row_pass(): return lax.map(one_head, (head_queries, head_pairs, head_cotangent))  22.1 us
    reshape x2, local copies, waits for them, and re-layouts, body(): results = results.reshape(4, grid_rows, cols_here, all_heads * head_dim)  20.1 us
    convert_element_type x6, other arithmetic, attend_block(): prob_low = attn_prob.astype(jnp.bfloat16)  17.1 us
    ppermute x2, waiting for transfers between devices, passed_along(): return lax.ppermute(block, axis, route)  16.9 us
    slice x6, local copies, waits for them, and re-layouts, one_head(): windows[1]  14.1 us
  transfers between devices with their start and end apart: 6, of which 2 were waited for; matrix products, arithmetic and copies ran while one was open for 49% of the time, Pallas kernels for 0%

commit v1 on v0

v1 whole, which is shorter than its diff:
```python
import functools

import jax
import jax.numpy as jnp
import numpy as np
from jax import lax
from jax.experimental import pallas as pl
from jax.experimental.pallas import tpu as pltpu
from jax.sharding import PartitionSpec as P

HEAD_DIM = 128
GRIDC = 128
GROUP = 8
MASKED = -1e30
SCALE = HEAD_DIM**-0.5
EXP2_SCALE = SCALE * float(np.log2(np.e))
VMEM = 48 << 20


def contract(a, b, dim_a, dim_b):
    return lax.dot_general(
        a, b, (((dim_a,), (dim_b,)), ((), ())), preferred_element_type=jnp.float32
    )


def attend(queries, cotangent, keys, values, add_bias):
    n_keys, n_queries = keys.shape[0], queries.shape[0]
    scores = add_bias(contract(keys, queries, 1, 1))
    top = jnp.max(scores, axis=0, keepdims=True)
    terms = jnp.exp2((scores - top) * EXP2_SCALE)
    prob = terms * (1.0 / jnp.sum(terms, axis=0, keepdims=True))
    prob_low = prob.astype(jnp.bfloat16)
    output = contract(prob_low, values, 0, 0).astype(jnp.bfloat16)
    product = cotangent.astype(jnp.float32) * output.astype(jnp.float32)
    delta = jnp.sum(product.T, axis=0, keepdims=True)
    d_prob = contract(values, cotangent, 1, 1)
    d_scores = (prob * (d_prob - delta)).astype(jnp.bfloat16)
    grad_query = (contract(d_scores, keys, 0, 0) * SCALE).astype(jnp.bfloat16)
    grad_keys = contract(d_scores, queries, 1, 0)
    grad_values = contract(prob_low, cotangent, 1, 0)
    return output, grad_query, grad_keys, grad_values


def row_kernel(
    band, bias, q, k, v, d, k_lo, v_lo, k_hi, v_hi,
    out, dq, dk, dv, lo, hi, keys, values, acc_k, acc_v,
):
    tokens = q.shape[0]
    rim = k_lo.shape[0]
    for whole, before, own, after in ((keys, k_lo, k, k_hi), (values, v_lo, v, v_hi)):
        whole[:rim] = before[...]
        whole[rim : rim + tokens] = own[...]
        whole[rim + tokens :] = after[...]
    acc_k[...] = jnp.zeros_like(acc_k)
    acc_v[...] = jnp.zeros_like(acc_v)
    blocks = 2 * band + 2
    for pair in range(tokens // (2 * GRIDC)):
        here = pl.ds(pair * 2 * GRIDC, 2 * GRIDC)
        window = pl.ds(pair * 2 * GRIDC, blocks * GRIDC)

        def add_bias(scores):
            shaped = scores.reshape(blocks, GRIDC, 2 * GRIDC)
            return (shaped + bias[pair][:, None, :]).reshape(scores.shape)

        output, grad_query, grad_keys, grad_values = attend(
            q[here], d[here], keys[window], values[window], add_bias
        )
        out[here] = output
        dq[here] = grad_query
        acc_k[window] += grad_keys
        acc_v[window] += grad_values
    for at, (acc, own, factor) in enumerate(((acc_k, dk, SCALE), (acc_v, dv, 1.0))):
        own[...] = acc[rim : rim + tokens] * factor
        lo[at] = (acc[:rim] * factor).astype(lo.dtype)
        hi[at] = (acc[rim + tokens :] * factor).astype(hi.dtype)


def row_attention(bias, q, k, v, d, before, after, band):
    tokens, feat = q.shape
    heads = feat // HEAD_DIM
    rim = band * GRIDC
    tall = pl.BlockSpec((tokens, HEAD_DIM), lambda h: (0, h))
    rims = [pl.BlockSpec((None, rim, HEAD_DIM), lambda h, a=a: (a, 0, h)) for a in range(2)]
    both = pl.BlockSpec((2, rim, HEAD_DIM), lambda h: (0, 0, h))
    padded = tokens + 2 * rim
    pairs = tokens * (2 * band + 2) * GRIDC * heads
    return pl.pallas_call(
        functools.partial(row_kernel, band),
        grid=(heads,),
        in_specs=[pl.BlockSpec(bias.shape, lambda h: (0, 0, 0)), tall, tall, tall, tall, *rims, *rims],
        out_specs=[tall, tall, tall, tall, both, both],
        out_shape=[
            jax.ShapeDtypeStruct(q.shape, jnp.bfloat16),
            jax.ShapeDtypeStruct(q.shape, jnp.bfloat16),
            jax.ShapeDtypeStruct(q.shape, jnp.float32),
            jax.ShapeDtypeStruct(q.shape, jnp.float32),
            jax.ShapeDtypeStruct((2, rim, feat), jnp.bfloat16),
            jax.ShapeDtypeStruct((2, rim, feat), jnp.bfloat16),
        ],
        scratch_shapes=[
            pltpu.VMEM((padded, HEAD_DIM), jnp.bfloat16),
            pltpu.VMEM((padded, HEAD_DIM), jnp.bfloat16),
            pltpu.VMEM((padded, HEAD_DIM), jnp.float32),
            pltpu.VMEM((padded, HEAD_DIM), jnp.float32),
        ],
        compiler_params=pltpu.CompilerParams(vmem_limit_bytes=VMEM),
        cost_estimate=pl.CostEstimate(
            flops=24 * pairs * HEAD_DIM, bytes_accessed=30 * tokens * feat, transcendentals=pairs
        ),
        name="row_heads",
    )(bias, q, k, v, d, before, before, after, after)


def col_kernel(bias, x, first, second):
    shape = (x.shape[0], *x.shape[2:])
    tokens = shape[0] * shape[1] * shape[2]
    q, k, v, d = (x[:, a].reshape(tokens, HEAD_DIM) for a in range(4))
    chunk = min(tokens, 256)
    grad_keys, grad_values = 0.0, 0.0
    outputs, grads = [], []
    for start in range(0, tokens, chunk):
        here = slice(start, start + chunk)
        output, grad_query, more_keys, more_values = attend(
            q[here], d[here], k, v, lambda s: s + bias[:, here]
        )
        grad_keys += more_keys
        grad_values += more_values
        outputs.append(output)
        grads.append(grad_query)
    first[:, 0] = jnp.concatenate(outputs, 0).reshape(shape)
    first[:, 1] = jnp.concatenate(grads, 0).reshape(shape)
    second[:, 0] = (grad_keys * SCALE).astype(jnp.bfloat16).reshape(shape)
    second[:, 1] = grad_values.astype(jnp.bfloat16).reshape(shape)


def col_attention(bias, x):
    n, _, rows, cols, feat = x.shape
    heads = feat // HEAD_DIM
    tokens = n * rows * GROUP
    spec = lambda k: pl.BlockSpec((n, k, rows, GROUP, HEAD_DIM), lambda h, g: (0, 0, 0, g, h))
    half = jax.ShapeDtypeStruct((n, 2, rows, cols, feat), jnp.bfloat16)
    pairs = tokens * tokens * heads * (cols // GROUP)
    return pl.pallas_call(
        col_kernel,
        grid=(heads, cols // GROUP),
        in_specs=[pl.BlockSpec(bias.shape, lambda h, g: (0, 0)), spec(4)],
        out_specs=[spec(2), spec(2)],
        out_shape=[half, half],
        compiler_params=pltpu.CompilerParams(vmem_limit_bytes=VMEM),
        cost_estimate=pl.CostEstimate(
            flops=12 * pairs * HEAD_DIM, bytes_accessed=4 * x.size, transcendentals=pairs
        ),
        name="col_heads",
    )(bias, x)


def pack_kernel(*refs):
    *parts, out = refs
    for a, part in enumerate(parts):
        out[a] = part[...]


def packed(arrays, n):
    tokens, feat = arrays[0].shape
    rows, cols, k = tokens // GRIDC, GRIDC // n, len(arrays)
    return pl.pallas_call(
        pack_kernel,
        grid=(n,),
        in_specs=[pl.BlockSpec((rows, cols, feat), lambda j: (0, j, 0))] * k,
        out_specs=pl.BlockSpec((None, k, rows, cols, feat), lambda j: (j, 0, 0, 0, 0)),
        out_shape=jax.ShapeDtypeStruct((n, k, rows, cols, feat), jnp.bfloat16),
        compiler_params=pltpu.CompilerParams(vmem_limit_bytes=VMEM),
        cost_estimate=pl.CostEstimate(
            flops=0, bytes_accessed=4 * k * tokens * feat, transcendentals=0
        ),
        name="pack",
    )(*(a.reshape(rows, GRIDC, feat) for a in arrays))


def unpack_kernel(x, *parts):
    for a, part in enumerate(parts):
        part[...] = x[a]


def unpacked(x):
    n, k, rows, cols, feat = x.shape
    outs = pl.pallas_call(
        unpack_kernel,
        grid=(n,),
        in_specs=[pl.BlockSpec((None, k, rows, cols, feat), lambda j: (j, 0, 0, 0, 0))],
        out_specs=[pl.BlockSpec((rows, cols, feat), lambda j: (0, j, 0))] * k,
        out_shape=[jax.ShapeDtypeStruct((rows, n * cols, feat), jnp.bfloat16)] * k,
        compiler_params=pltpu.CompilerParams(vmem_limit_bytes=VMEM),
        cost_estimate=pl.CostEstimate(flops=0, bytes_accessed=4 * x.size, transcendentals=0),
        name="unpack",
    )(x)
    return [o.reshape(rows * n * cols, feat) for o in outs]


def passed_along(block, distance):
    devices = range(lax.axis_size("ctx"))
    route = [(i - distance, i) for i in devices if i - distance in devices]
    return lax.ppermute(block, "ctx", route)


def exchanged(x):
    return lax.all_to_all(x, "ctx", 0, 0, tiled=True)


def row_bias(mask, first, rows, band, total):
    mask_rows = lax.dynamic_slice_in_dim(mask, first, rows, 0)
    key_rows = (first + jnp.arange(rows))[:, None] + jnp.arange(2 * band + 1)[None, :] - band
    seen = (key_rows >= 0) & (key_rows < total) & (mask_rows == 1)
    seen = seen.reshape(rows // 2, 2, 2 * band + 1)
    even = jnp.pad(seen[:, 0], ((0, 0), (0, 1)))
    odd = jnp.pad(seen[:, 1], ((0, 0), (1, 0)))
    both = jnp.stack([even, odd], axis=-1)
    return jnp.repeat(jnp.where(both, 0.0, MASKED).astype(jnp.float32), GRIDC, axis=2)


def col_bias(mask):
    seen = (mask.T == 1)[:, None, :, None] & jnp.eye(GROUP, dtype=bool)[None, :, None, :]
    size = mask.shape[0] * GROUP
    return jnp.where(seen, 0.0, MASKED).astype(jnp.float32).reshape(size, size)


def body(
    row_query, row_key, row_value, row_cotangent, row_mask,
    col_query, col_key, col_value, col_cotangent, col_mask,
):
    n = lax.axis_size("ctx")
    tokens = row_query.shape[0]
    rows = tokens // GRIDC
    band = (row_mask.shape[1] - 1) // 2
    rim = band * GRIDC
    first_row = lax.axis_index("ctx") * rows

    after = passed_along(jnp.stack([row_key[:rim], row_value[:rim]]), -1)
    before = passed_along(jnp.stack([row_key[tokens - rim :], row_value[tokens - rim :]]), 1)
    moved = exchanged(packed([col_query, col_key, col_value, col_cotangent], n))

    bias = row_bias(row_mask, first_row, rows, band, rows * n)
    row_output, row_dquery, own_k, own_v, lo, hi = row_attention(
        bias, row_query, row_key, row_value, row_cotangent, before, after, band
    )
    from_next = passed_along(lo, -1).astype(jnp.float32)
    from_prev = passed_along(hi, 1).astype(jnp.float32)

    first, second = col_attention(col_bias(col_mask), moved)
    col_output, col_dquery = unpacked(exchanged(first))
    col_dkeys, col_dvalues = unpacked(exchanged(second))

    row_grads = []
    for at, own in enumerate((own_k, own_v)):
        own = own.at[tokens - rim :].add(from_next[at])
        own = own.at[:rim].add(from_prev[at])
        row_grads.append(own.astype(jnp.bfloat16))
    return (
        row_output, row_dquery, *row_grads,
        col_output, col_dquery, col_dkeys, col_dvalues,
    )


def solution(mesh):
    tokens, whole = P("ctx", "head"), P()
    return jax.shard_map(
        body,
        mesh=mesh,
        in_specs=(tokens,) * 4 + (whole,) + (tokens,) * 4 + (whole,),
        out_specs=(tokens,) * 8,
        check_vma=False,
    )
```

time: 457 us -> 300 us (0.66); the launches traced: 450 us -> 299 us
  local copies, waits for them, and re-layouts: 185 us -> 27.1 us
  Pallas kernels: 0 us -> 92.2 us
  matrix products: 82.3 us -> 0 us
  other arithmetic: 56.6 us -> 13.5 us
  waiting for transfers between devices: 101 us -> 136 us
  starting transfers between devices: 23.7 us -> 29.5 us
    pallas_call x0 -> x5, Pallas kernels: none -> 92.2 us  [the longest x1 49.4 us: row_attention(): pl.pallas_call(functools.partial(row_kernel, band), grid=(heads,), in_spe...]
    all_to_all x2 -> x3, waiting for transfers between devices: 0.01 us -> 74.6 us  [exchanged(): return lax.all_to_all(x, 'ctx', 0, 0, tiled=True)]
    dot_general x35 -> x0, matrix products: 44.7 us -> none  [the longest x7 11.6 us: attend_block(): jnp.einsum('bnm,bmd->bnd', prob_low, value_block, preferred_element_type=...]
    slice x19 -> x1, local copies, waits for them, and re-layouts: 40.1 us -> 0.01 us  [row_bias(): even = jnp.pad(seen[:, 0], ((0, 0), (0, 1)))]
    ppermute x4, waiting for transfers between devices: 101 us -> 61.3 us  [passed_along(): return lax.ppermute(block, 'ctx', route)]
    sub x7 -> x0, matrix products: 37.6 us -> none  [attend_block(): exp_terms = jnp.where(allowed, jnp.exp(scores - row_max), 0.0)]
    reshape x3, local copies, waits for them, and re-layouts: 33.8 us -> 0.07 us  [the longest x2 0.06 us: row_bias(): jnp.repeat(jnp.where(both, 0.0, MASKED).astype(jnp.float32), GRIDC, axis=2)]
    unnamed x29 -> x24, local copies, waits for them, and re-layouts: 34.3 us -> 11 us
  transfers between devices with their start and end apart: 6 -> 7, of which waited for: 2 -> 4; matrix products, arithmetic and copies ran while one was open for 49% -> 10% of each run, Pallas kernels for 0% -> 18%
where the time goes in v1:
time: 300 us; the launch traced here: 299 us
  waiting for transfers between devices  136 us (45%)
  Pallas kernels  92.2 us (31%)
  starting transfers between devices  29.5 us (10%)
  local copies, waits for them, and re-layouts  27.1 us (9%)
  other arithmetic  13.5 us (4%)
    all_to_all x3, waiting for transfers between devices, exchanged(): return lax.all_to_all(x, 'ctx', 0, 0, tiled=True)  74.6 us
    ppermute x4, waiting for transfers between devices, passed_along(): return lax.ppermute(block, 'ctx', route)  61.3 us
    pallas_call x1, Pallas kernels, row_attention(): pl.pallas_call(functools.partial(row_kernel, band), grid=(heads,), in_spe...  49.4 us
    pallas_call x1, Pallas kernels, col_attention(): pl.pallas_call(col_kernel, grid=(heads, cols // GROUP), in_specs=[pl.Bloc...  27.1 us
    all_to_all x3, starting transfers between devices, exchanged(): return lax.all_to_all(x, 'ctx', 0, 0, tiled=True)  16.6 us
    select_n x1, local copies, waits for them, and re-layouts, col_bias(): return jnp.where(seen, 0.0, MASKED).astype(jnp.float32).reshape(size, size)  13.4 us
    ppermute x4, starting transfers between devices, passed_along(): return lax.ppermute(block, 'ctx', route)  12.9 us
    unnamed x24, local copies, waits for them, and re-layouts  11 us
  transfers between devices with their start and end apart: 7, of which 4 were waited for; matrix products, arithmetic and copies ran while one was open for 10% of the time, Pallas kernels for 18%

profile of v1, /device:TPU:11, one launch (start us, length us, event | category | flops | bytes accessed | tf_op | source)
XLA Modules:
  0.0 299.0 jit_solution(3443611316742914263)
XLA Ops:
  0.6 0.0 copy-start
  0.7 0.0 copy-start.3
  0.7 1.4 copy-done.3
  2.1 0.0 copy-start.4
  2.1 1.4 copy-done.4
  3.5 0.0 copy-start.5
  3.5 1.4 copy-done.5
  4.9 6.5 %pack.1 = bf16[8,4,8,16,768]{4,3,2,1,0:T(8,128)(2,1)} custom-call(bf16[8,128,768]{2,1,0:T(8,128)(2,1)S(1)} %bitcast.54, bf16[8,128,768]{2,1,0:T(8,128)(2,1)S(1)} %bitcast.55, bf16[8,128,768]{2,1,0:T(8,128)(2,1)S(1)} %bitcast.56, bf16[8,128,768]{2,1,0:T(8,128)(2,1)} %bitcast.57), custom_call_target="tpu_custom_call" | custom-call | bytes 12582912 | tf_op jit(solution)/shard_map/pack/pallas_call | solution.py:166
  11.3 0.0 copy-start.10
  11.3 5.6 %all-to-all-start = ((bf16[8,4,8,16,768]{4,3,2,1,0:T(8,128)(2,1)}), bf16[8,4,8,16,768]{4,3,2,1,0:T(8,128)(2,1)}, u32[]{:S(2)}, u32[]{:S(2)}) async-start(bf16[8,4,8,16,768]{4,3,2,1,0:T(8,128)(2,1)} %pack.1), calls=%async_computation | async-start | bytes 12582912 | tf_op jit(solution)/shard_map/all_to_all | solution.py:207
  17.0 0.0 copy-done.10
  17.0 0.1 copy.28
  17.1 6.6 %and_select_fusion = f32[64,8,64,8]{3,2,1,0:T(8,128)} fusion(pred[8,8]{1,0:T(8,128)(4,1)S(1)} %iota_compare_fusion, pred[64,64]{1,0:T(8,128)(4,1)S(1)} %copy.28), kind=kLoop, calls=%fused_computation | loop fusion | flops 524288 | bytes 1052736 | tf_op jit(solution)/shard_map/jit(_where)/select_n | solution.py:224
  23.7 13.4 %select_n.18.bias = f32[512,512]{1,0:T(8,128)} reshape(f32[64,8,64,8]{3,2,1,0:T(8,128)} %and_select_fusion) | data formatting | bytes 2097152 | tf_op jit(solution)/shard_map/jit(_where)/select_n | solution.py:224
  37.1 50.0 %all-to-all-done.x = bf16[8,4,8,16,768]{4,3,2,1,0:T(8,128)(2,1)} async-done(((bf16[8,4,8,16,768]{4,3,2,1,0:T(8,128)(2,1)}), bf16[8,4,8,16,768]{4,3,2,1,0:T(8,128)(2,1)}, u32[]{:S(2)}, u32[]{:S(2)}) %all-to-all-start) | async-done | bytes 6291488 | tf_op jit(solution)/shard_map/all_to_all | solution.py:207
  87.1 0.0 copy-start.6
  87.1 1.2 copy-done.6
  88.3 27.1 %col_heads.1 = (bf16[8,2,8,16,768]{4,3,2,1,0:T(8,128)(2,1)S(1)}, bf16[8,2,8,16,768]{4,3,2,1,0:T(8,128)(2,1)}) custom-call(f32[512,512]{1,0:T(8,128)S(1)} %copy-done.6, bf16[8,4,8,16,768]{4,3,2,1,0:T(8,128)(2,1)} %all-to-all-done.x), custom_call_target="tpu_custom_call" | custom-call | flops 4831838208 | bytes 12582912 | tf_op jit(solution)/shard_map/col_heads/pallas_call | solution.py:143
  115.4 0.0 copy-start.2
  115.4 1.7 copy-done.2
  117.0 5.2 %all-to-all-start.1 = ((bf16[8,2,8,16,768]{4,3,2,1,0:T(8,128)(2,1)}), bf16[8,2,8,16,768]{4,3,2,1,0:T(8,128)(2,1)S(1)}, u32[]{:S(2)}, u32[]{:S(2)}) async-start(bf16[8,2,8,16,768]{4,3,2,1,0:T(8,128)(2,1)} %copy-done.2), calls=%async_computation.1 | async-start | bytes 6291456 | tf_op jit(solution)/shard_map/all_to_all | solution.py:207
  122.2 2.0 slice_bitcast_fusion.4
  124.2 1.3 pad_maximum_fusion.1
  125.5 2.3 collective-permute-start.1
  127.8 1.3 pad_maximum_fusion
  129.1 4.2 %collective-permute-start = (bf16[2,512,768]{2,1,0:T(8,128)(2,1)}, bf16[2,512,768]{2,1,0:T(8,128)(2,1)}, u32[]{:S(2)}, u32[]{:S(2)}) collective-permute-start(bf16[2,512,768]{2,1,0:T(8,128)(2,1)} %pad_maximum_fusion), channel_id=1, source_target_pairs={{0,4},{4,8},{8,12},{12,16},{16,20},{20,24},{24,28},{1,5},{5,9},{9,... | collective-permute-start | bytes 4718600 | tf_op jit(solution)/shard_map/ppermute | solution.py:203
  133.3 0.0 copy-done
  133.3 0.1 constant_dynamic-slice_fusion
  133.4 0.1 copy.31
  133.4 0.1 fusion.11
  133.6 0.1 pad_bitcast_fusion
  133.7 0.1 copy.26
  133.8 0.1 broadcast_in_dim.25
  133.9 24.7 %all-to-all-done.1.x = bf16[8,2,8,16,768]{4,3,2,1,0:T(8,128)(2,1)S(1)} async-done(((bf16[8,2,8,16,768]{4,3,2,1,0:T(8,128)(2,1)}), bf16[8,2,8,16,768]{4,3,2,1,0:T(8,128)(2,1)S(1)}, u32[]{:S(2)}, u32[]{:S(2)}) %all-to-all-start.1) | async-done | bytes 3145760 | tf_op jit(solution)/shard_map/all_to_all | solution.py:207
  158.6 5.8 %all-to-all-start.2 = ((bf16[8,2,8,16,768]{4,3,2,1,0:T(8,128)(2,1)}), bf16[8,2,8,16,768]{4,3,2,1,0:T(8,128)(2,1)}, u32[]{:S(2)}, u32[]{:S(2)}) async-start(bf16[8,2,8,16,768]{4,3,2,1,0:T(8,128)(2,1)} %get-tuple-element.77), calls=%async_computation.2 | async-start | bytes 6291456 | tf_op jit(solution)/shard_map/all_to_all | solution.py:207
  164.4 28.3 %collective-permute-done.1.k_hi.v_hi = bf16[2,512,768]{2,1,0:T(8,128)(2,1)} collective-permute-done((bf16[2,512,768]{2,1,0:T(8,128)(2,1)}, bf16[2,512,768]{2,1,0:T(8,128)(2,1)}, u32[]{:S(2)}, u32[]{:S(2)}) %collective-permute-start.1) | collective-permute-done | bytes 1572896 | tf_op jit(solution)/shard_map/ppermute | solution.py:203
  192.7 0.0 collective-permute-done.k_lo.v_lo
  192.7 0.0 copy-start.7
  192.7 1.4 copy-done.7
  194.1 49.4 %row_heads.1 = (bf16[1024,768]{1,0:T(8,128)(2,1)}, bf16[1024,768]{1,0:T(8,128)(2,1)}, f32[1024,768]{1,0:T(8,128)}, f32[1024,768]{1,0:T(8,128)}, bf16[2,512,768]{...) custom-call(f32[4,10,256]{2,1,0:T(8,128)S(1)} %copy.27.bias, bf16[1024,768]{1,0:T(8,128)(2,1)S(1)} %copy-done.7, ...), custom_call_target="tpu_custom_call" | custom-call | flops 24159191040 | bytes 23592960 | tf_op jit(solution)/shard_map/row_heads/pallas_call | solution.py:87
  243.5 1.9 collective-permute-start.2
  245.4 4.5 %collective-permute-start.3 = (bf16[2,512,768]{2,1,0:T(8,128)(2,1)S(1)}, bf16[2,512,768]{2,1,0:T(8,128)(2,1)S(1)}, u32[]{:S(2)}, u32[]{:S(2)}) collective-permute-start(bf16[2,512,768]{2,1,0:T(8,128)(2,1)S(1)} %get-tuple-element.72), channel_id=1, source_target_pairs={{0,4},{4,8},{8,12},{12,16},{16,20},{20,24},{24,28},{1,5},{5,9},{9,... | collective-permute-start | bytes 4718600 | tf_op jit(solution)/shard_map/ppermute | solution.py:203
  250.0 33.0 %collective-permute-done.2 = bf16[2,512,768]{2,1,0:T(8,128)(2,1)S(1)} collective-permute-done((bf16[2,512,768]{2,1,0:T(8,128)(2,1)S(1)}, bf16[2,512,768]{2,1,0:T(8,128)(2,1)S(1)}, u32[]{:S(2)}, u32[]{:S(2)}) %collective-permute-start.2) | collective-permute-done | bytes 1572896 | tf_op jit(solution)/shard_map/ppermute | solution.py:203
  282.9 0.0 copy-start.9
  283.0 0.2 convert_element_type.16
  283.2 0.0 copy-start.8
  283.2 0.0 collective-permute-done.3
  283.2 0.2 convert_element_type.17
  283.5 1.4 copy-done.9
  284.8 1.0 copy-done.8
  285.9 0.6 fusion.3
  286.5 0.6 fusion.1
  287.1 1.3 convert_element_type.18
  288.4 1.3 convert_element_type.19
  289.7 0.0 copy-start.1
  289.7 3.2 %unpack.2 = (bf16[8,128,768]{2,1,0:T(8,128)(2,1)}, bf16[8,128,768]{2,1,0:T(8,128)(2,1)}) custom-call(bf16[8,2,8,16,768]{4,3,2,1,0:T(8,128)(2,1)S(1)} %all-to-all-done.1.x), custom_call_target="tpu_custom_call" | custom-call | bytes 6291456 | tf_op jit(solution)/shard_map/unpack/pallas_call | solution.py:187
  292.9 0.0 all-to-all-done.2.x
  292.9 6.1 %unpack.3 = (bf16[8,128,768]{2,1,0:T(8,128)(2,1)}, bf16[8,128,768]{2,1,0:T(8,128)(2,1)}) custom-call(bf16[8,2,8,16,768]{4,3,2,1,0:T(8,128)(2,1)} %all-to-all-done.2.x), custom_call_target="tpu_custom_call" | custom-call | bytes 6291456 | tf_op jit(solution)/shard_map/unpack/pallas_call | solution.py:187
  299.0 0.0 copy-done.1
  (10 shorter events, 0.1 us)
Async XLA Ops:
  0.6 132.6 %copy-start = (s32[64,9]{0,1:T(8,128)S(1)}, s32[64,9]{0,1:T(8,128)}, u32[]{:S(2)}) copy-start(s32[64,9]{0,1:T(8,128)} %param.22) | copy-start | bytes 6916
  0.7 1.4 copy-start.3
  2.1 1.4 copy-start.4
  3.5 1.4 copy-start.5
  11.3 5.6 %copy-start.10 = (s32[64,64]{1,0:T(8,128)S(1)}, s32[64,64]{1,0:T(8,128)}, u32[]{:S(2)}) copy-start(s32[64,64]{1,0:T(8,128)} %param.27) | copy-start | bytes 49156
  11.3 75.7 %all-to-all-start = ((bf16[8,4,8,16,768]{4,3,2,1,0:T(8,128)(2,1)}), bf16[8,4,8,16,768]{4,3,2,1,0:T(8,128)(2,1)}, u32[]{:S(2)}, u32[]{:S(2)}) async-start(bf16[8,4,8,16,768]{4,3,2,1,0:T(8,128)(2,1)} %pack.1), calls=%async_computation | async-start | bytes 12582912 | tf_op jit(solution)/shard_map/all_to_all | solution.py:207
  87.1 1.2 copy-start.6
  115.4 1.7 copy-start.2
  117.0 41.6 %all-to-all-start.1 = ((bf16[8,2,8,16,768]{4,3,2,1,0:T(8,128)(2,1)}), bf16[8,2,8,16,768]{4,3,2,1,0:T(8,128)(2,1)S(1)}, u32[]{:S(2)}, u32[]{:S(2)}) async-start(bf16[8,2,8,16,768]{4,3,2,1,0:T(8,128)(2,1)} %copy-done.2), calls=%async_computation.1 | async-start | bytes 6291456 | tf_op jit(solution)/shard_map/all_to_all | solution.py:207
  125.5 67.2 %collective-permute-start.1 = (bf16[2,512,768]{2,1,0:T(8,128)(2,1)}, bf16[2,512,768]{2,1,0:T(8,128)(2,1)}, u32[]{:S(2)}, u32[]{:S(2)}) collective-permute-start(bf16[2,512,768]{2,1,0:T(8,128)(2,1)} %pad_maximum_fusion.1), channel_id=1, source_target_pairs={{4,0},{8,4},{12,8},{16,12},{20,16},{24,20},{28,24},{5,1},{9,5},{13... | collective-permute-start | bytes 4718600 | tf_op jit(solution)/shard_map/ppermute | solution.py:203
  129.1 63.7 %collective-permute-start = (bf16[2,512,768]{2,1,0:T(8,128)(2,1)}, bf16[2,512,768]{2,1,0:T(8,128)(2,1)}, u32[]{:S(2)}, u32[]{:S(2)}) collective-permute-start(bf16[2,512,768]{2,1,0:T(8,128)(2,1)} %pad_maximum_fusion), channel_id=1, source_target_pairs={{0,4},{4,8},{8,12},{12,16},{16,20},{20,24},{24,28},{1,5},{5,9},{9,... | collective-permute-start | bytes 4718600 | tf_op jit(solution)/shard_map/ppermute | solution.py:203
  158.6 134.3 %all-to-all-start.2 = ((bf16[8,2,8,16,768]{4,3,2,1,0:T(8,128)(2,1)}), bf16[8,2,8,16,768]{4,3,2,1,0:T(8,128)(2,1)}, u32[]{:S(2)}, u32[]{:S(2)}) async-start(bf16[8,2,8,16,768]{4,3,2,1,0:T(8,128)(2,1)} %get-tuple-element.77), calls=%async_computation.2 | async-start | bytes 6291456 | tf_op jit(solution)/shard_map/all_to_all | solution.py:207
  192.7 1.4 copy-start.7
  243.5 39.5 %collective-permute-start.2 = (bf16[2,512,768]{2,1,0:T(8,128)(2,1)S(1)}, bf16[2,512,768]{2,1,0:T(8,128)(2,1)S(1)}, u32[]{:S(2)}, u32[]{:S(2)}) collective-permute-start(bf16[2,512,768]{2,1,0:T(8,128)(2,1)S(1)} %get-tuple-element.71), channel_id=1, source_target_pairs={{4,0},{8,4},{12,8},{16,12},{20,16},{24,20},{28,24},{5,1},{9,5},{13... | collective-permute-start | bytes 4718600 | tf_op jit(solution)/shard_map/ppermute | solution.py:203
  245.4 37.8 %collective-permute-start.3 = (bf16[2,512,768]{2,1,0:T(8,128)(2,1)S(1)}, bf16[2,512,768]{2,1,0:T(8,128)(2,1)S(1)}, u32[]{:S(2)}, u32[]{:S(2)}) collective-permute-start(bf16[2,512,768]{2,1,0:T(8,128)(2,1)S(1)} %get-tuple-element.72), channel_id=1, source_target_pairs={{0,4},{4,8},{8,12},{12,16},{16,20},{20,24},{24,28},{1,5},{5,9},{9,... | collective-permute-start | bytes 4718600 | tf_op jit(solution)/shard_map/ppermute | solution.py:203
  282.9 1.9 copy-start.9
  283.2 2.7 copy-start.8
  289.7 9.3 %copy-start.1 = (s32[64,9]{0,1:T(8,128)S(1)}, s32[64,9]{0,1:T(8,128)}, u32[]{:S(2)}) copy-start(s32[64,9]{0,1:T(8,128)} %param.22) | copy-start | bytes 6916

commit v2 on v1

--- a/solution.py
+++ b/solution.py
@@ -14,7 +14,7 @@
 MASKED = -1e30
 SCALE = HEAD_DIM**-0.5
 EXP2_SCALE = SCALE * float(np.log2(np.e))
-VMEM = 48 << 20
+VMEM = 60 << 20
 
 
 def contract(a, b, dim_a, dim_b):
@@ -42,7 +42,7 @@
 
 
 def row_kernel(
-    band, bias, q, k, v, d, k_lo, v_lo, k_hi, v_hi,
+    band, first, mask, q, k, v, d, k_lo, v_lo, k_hi, v_hi,
     out, dq, dk, dv, lo, hi, keys, values, acc_k, acc_v,
 ):
     tokens = q.shape[0]
@@ -54,13 +54,31 @@
     acc_k[...] = jnp.zeros_like(acc_k)
     acc_v[...] = jnp.zeros_like(acc_v)
     blocks = 2 * band + 2
+    odd = lax.broadcasted_iota(jnp.int32, (1, 2 * GRIDC), 1) >= GRIDC
+    total = mask.shape[0]
+
+    def block_bias(row, block):
+        key_row = row - band + block
+        inside = (key_row >= 0) & (key_row < total)
+        sides = []
+        for side in range(2):
+            offset = block - side
+            seen = inside & (mask[row + side, offset] == 1) if 0 <= offset <= 2 * band else False
+            sides.append(jnp.where(seen, 0.0, MASKED).astype(jnp.float32))
+        return jnp.where(odd, sides[1], sides[0])
+
     for pair in range(tokens // (2 * GRIDC)):
         here = pl.ds(pair * 2 * GRIDC, 2 * GRIDC)
         window = pl.ds(pair * 2 * GRIDC, blocks * GRIDC)
 
         def add_bias(scores):
-            shaped = scores.reshape(blocks, GRIDC, 2 * GRIDC)
-            return (shaped + bias[pair][:, None, :]).reshape(scores.shape)
+            return jnp.concatenate(
+                [
+                    scores[b * GRIDC : (b + 1) * GRIDC] + block_bias(first[0] + 2 * pair, b)
+                    for b in range(blocks)
+                ],
+                axis=0,
+            )
 
         output, grad_query, grad_keys, grad_values = attend(
             q[here], d[here], keys[window], values[window], add_bias
@@ -75,19 +93,20 @@
         hi[at] = (acc[rim + tokens :] * factor).astype(hi.dtype)
 
 
-def row_attention(bias, q, k, v, d, before, after, band):
+def row_attention(first, mask, q, k, v, d, before, after, band):
     tokens, feat = q.shape
     heads = feat // HEAD_DIM
     rim = band * GRIDC
     tall = pl.BlockSpec((tokens, HEAD_DIM), lambda h: (0, h))
     rims = [pl.BlockSpec((None, rim, HEAD_DIM), lambda h, a=a: (a, 0, h)) for a in range(2)]
     both = pl.BlockSpec((2, rim, HEAD_DIM), lambda h: (0, 0, h))
+    scalars = pl.BlockSpec(memory_space=pltpu.SMEM)
     padded = tokens + 2 * rim
     pairs = tokens * (2 * band + 2) * GRIDC * heads
     return pl.pallas_call(
         functools.partial(row_kernel, band),
         grid=(heads,),
-        in_specs=[pl.BlockSpec(bias.shape, lambda h: (0, 0, 0)), tall, tall, tall, tall, *rims, *rims],
+        in_specs=[scalars, scalars, tall, tall, tall, tall, *rims, *rims],
         out_specs=[tall, tall, tall, tall, both, both],
         out_shape=[
             jax.ShapeDtypeStruct(q.shape, jnp.bfloat16),
@@ -105,13 +124,26 @@
         ],
         compiler_params=pltpu.CompilerParams(vmem_limit_bytes=VMEM),
         cost_estimate=pl.CostEstimate(
-            flops=24 * pairs * HEAD_DIM, bytes_accessed=30 * tokens * feat, transcendentals=pairs
+            flops=240 * pairs * HEAD_DIM, bytes_accessed=30 * tokens * feat, transcendentals=pairs
         ),
         name="row_heads",
-    )(bias, q, k, v, d, before, before, after, after)
-
-
-def col_kernel(bias, x, first, second):
+    )(first, mask, q, k, v, d, before, before, after, after)
+
+
+def col_kernel(mask, x, earlier, first, second, bias):
+    del earlier
+    @pl.when((pl.program_id(0) == 0) & (pl.program_id(1) == 0))
+    def _():
+        size, total = bias.shape[0], mask.shape[0]
+        row_of = lax.broadcasted_iota(jnp.int32, (size, total), 0) // GROUP
+        spread = (row_of == lax.broadcasted_iota(jnp.int32, (size, total), 1)).astype(jnp.bfloat16)
+        seen = (mask[...] == 1).astype(jnp.bfloat16)
+        by_key = contract(spread, seen, 1, 1).astype(jnp.bfloat16)
+        allowed = contract(by_key, spread, 1, 1)
+        key_col = lax.broadcasted_iota(jnp.int32, (size, size), 0) % GROUP
+        query_col = lax.broadcasted_iota(jnp.int32, (size, size), 1) % GROUP
+        bias[...] = jnp.where((key_col == query_col) & (allowed > 0.5), 0.0, MASKED)
+
     shape = (x.shape[0], *x.shape[2:])
     tokens = shape[0] * shape[1] * shape[2]
     q, k, v, d = (x[:, a].reshape(tokens, HEAD_DIM) for a in range(4))
@@ -133,7 +165,7 @@
     second[:, 1] = grad_values.astype(jnp.bfloat16).reshape(shape)
 
 
-def col_attention(bias, x):
+def col_attention(mask, x, earlier):
     n, _, rows, cols, feat = x.shape
     heads = feat // HEAD_DIM
     tokens = n * rows * GROUP
@@ -143,15 +175,18 @@
     return pl.pallas_call(
         col_kernel,
         grid=(heads, cols // GROUP),
-        in_specs=[pl.BlockSpec(bias.shape, lambda h, g: (0, 0)), spec(4)],
+        in_specs=[
+            pl.BlockSpec(mask.shape, lambda h, g: (0, 0)), spec(4), pl.BlockSpec(memory_space=pl.ANY)
+        ],
         out_specs=[spec(2), spec(2)],
         out_shape=[half, half],
+        scratch_shapes=[pltpu.VMEM((tokens, tokens), jnp.float32)],
         compiler_params=pltpu.CompilerParams(vmem_limit_bytes=VMEM),
         cost_estimate=pl.CostEstimate(
-            flops=12 * pairs * HEAD_DIM, bytes_accessed=4 * x.size, transcendentals=pairs
+            flops=240 * pairs * HEAD_DIM, bytes_accessed=4 * x.size, transcendentals=pairs
         ),
         name="col_heads",
-    )(bias, x)
+    )(mask, x, earlier)
 
 
 def pack_kernel(*refs):
@@ -205,23 +240,6 @@
 
 def exchanged(x):
     return lax.all_to_all(x, "ctx", 0, 0, tiled=True)
-
-
-def row_bias(mask, first, rows, band, total):
-    mask_rows = lax.dynamic_slice_in_dim(mask, first, rows, 0)
-    key_rows = (first + jnp.arange(rows))[:, None] + jnp.arange(2 * band + 1)[None, :] - band
-    seen = (key_rows >= 0) & (key_rows < total) & (mask_rows == 1)
-    seen = seen.reshape(rows // 2, 2, 2 * band + 1)
-    even = jnp.pad(seen[:, 0], ((0, 0), (0, 1)))
-    odd = jnp.pad(seen[:, 1], ((0, 0), (1, 0)))
-    both = jnp.stack([even, odd], axis=-1)
-    return jnp.repeat(jnp.where(both, 0.0, MASKED).astype(jnp.float32), GRIDC, axis=2)
-
-
-def col_bias(mask):
-    seen = (mask.T == 1)[:, None, :, None] & jnp.eye(GROUP, dtype=bool)[None, :, None, :]
-    size = mask.shape[0] * GROUP
-    return jnp.where(seen, 0.0, MASKED).astype(jnp.float32).reshape(size, size)
 
 
 def body(
@@ -235,25 +253,29 @@
     rim = band * GRIDC
     first_row = lax.axis_index("ctx") * rows
 
-    after = passed_along(jnp.stack([row_key[:rim], row_value[:rim]]), -1)
-    before = passed_along(jnp.stack([row_key[tokens - rim :], row_value[tokens - rim :]]), 1)
-    moved = exchanged(packed([col_query, col_key, col_value, col_cotangent], n))
-
-    bias = row_bias(row_mask, first_row, rows, band, rows * n)
+    tops = jnp.stack([row_key[:rim], row_value[:rim]])
+    ends = jnp.stack([row_key[tokens - rim :], row_value[tokens - rim :]])
+    cols = [col_query, col_key, col_value, col_cotangent]
+    tops, ends, *cols = lax.optimization_barrier((tops, ends, *cols))
+    after, before = passed_along(tops, -1), passed_along(ends, 1)
+    moved = exchanged(packed(cols, n))
+
     row_output, row_dquery, own_k, own_v, lo, hi = row_attention(
-        bias, row_query, row_key, row_value, row_cotangent, before, after, band
-    )
-    from_next = passed_along(lo, -1).astype(jnp.float32)
-    from_prev = passed_along(hi, 1).astype(jnp.float32)
-
-    first, second = col_attention(col_bias(col_mask), moved)
+        first_row.reshape(1), row_mask, row_query, row_key, row_value, row_cotangent, before, after, band
+    )
+    from_next, from_prev = passed_along(lo, -1), passed_along(hi, 1)
+
+    first, second = col_attention(col_mask, moved, row_output)
+    first, second, from_next, from_prev = lax.optimization_barrier(
+        (first, second, from_next, from_prev)
+    )
     col_output, col_dquery = unpacked(exchanged(first))
     col_dkeys, col_dvalues = unpacked(exchanged(second))
 
     row_grads = []
     for at, own in enumerate((own_k, own_v)):
-        own = own.at[tokens - rim :].add(from_next[at])
-        own = own.at[:rim].add(from_prev[at])
+        own = own.at[tokens - rim :].add(from_next[at].astype(jnp.float32))
+        own = own.at[:rim].add(from_prev[at].astype(jnp.float32))
         row_grads.append(own.astype(jnp.bfloat16))
     return (
         row_output, row_dquery, *row_grads,

time: 300 us -> 235 us (0.78)
  waiting for transfers between devices: 136 us -> 55.9 us
  blocking collectives: 0 us -> 39.3 us
  local copies, waits for them, and re-layouts: 27.1 us -> 4.34 us
  starting transfers between devices: 29.5 us -> 22.1 us
  Pallas kernels: 92.2 us -> 96.6 us
    all_to_all x3 -> x2, waiting for transfers between devices: 74.6 us -> 20.6 us  [exchanged(): return lax.all_to_all(x, 'ctx', 0, 0, tiled=True)]
    all_to_all x0 -> x1, blocking collectives: none -> 39.3 us  [exchanged(): return lax.all_to_all(x, 'ctx', 0, 0, tiled=True)]
    ppermute x4, waiting for transfers between devices: 61.3 us -> 35.2 us  [passed_along(): return lax.ppermute(block, 'ctx', route)]
    select_n x2 -> x0, local copies, waits for them, and re-layouts: 13.6 us -> none  [the longest x1 13.4 us: col_bias(): return jnp.where(seen, 0.0, MASKED).astype(jnp.float32).reshape(size, size)]
    unnamed x24 -> x15, local copies, waits for them, and re-layouts: 11 us -> 2.65 us
    scatter-add x2, other arithmetic: 1.22 us -> 8.41 us  [the longest x1 4.43 us: body(): own = own.at[tokens - rim:].add(from_next[at].astype(jnp.float32))]
    select_n x2 -> x0, other arithmetic: 6.59 us -> none  [the longest x1 6.58 us: col_bias(): return jnp.where(seen, 0.0, MASKED).astype(jnp.float32).reshape(size, size)]
    all_to_all x3 -> x2, starting transfers between devices: 16.6 us -> 10.1 us  [exchanged(): return lax.all_to_all(x, 'ctx', 0, 0, tiled=True)]
  transfers between devices with their start and end apart: 7 -> 6, of which waited for: 4 -> 5; matrix products, arithmetic and copies ran while one was open for 10% -> 6% of each run, Pallas kernels for 18% -> 39%
where the time goes in v2:
time: 235 us; the launch traced here: 232 us
  Pallas kernels  96.6 us (41%)
  waiting for transfers between devices  55.9 us (24%)
  blocking collectives  39.3 us (17%)
  starting transfers between devices  22.1 us (9%)
  other arithmetic  13.3 us (6%)
  local copies, waits for them, and re-layouts  4.34 us (2%)
    pallas_call x1, Pallas kernels, row_attention(): pl.pallas_call(functools.partial(row_kernel, band), grid=(heads,), in_spe...  49.2 us
    all_to_all x1, blocking collectives, exchanged(): return lax.all_to_all(x, 'ctx', 0, 0, tiled=True)  39.3 us
    ppermute x4, waiting for transfers between devices, passed_along(): return lax.ppermute(block, 'ctx', route)  35.2 us
    pallas_call x1, Pallas kernels, col_attention(): pl.pallas_call(col_kernel, grid=(heads, cols // GROUP), in_specs=[pl.Bloc...  27.3 us
    all_to_all x2, waiting for transfers between devices, exchanged(): return lax.all_to_all(x, 'ctx', 0, 0, tiled=True)  20.6 us
    pallas_call x2, Pallas kernels, unpacked(): pl.pallas_call(unpack_kernel, grid=(n,), in_specs=[pl.BlockSpec((None, k,...  12.2 us
    ppermute x4, starting transfers between devices, passed_along(): return lax.ppermute(block, 'ctx', route)  12.1 us
    all_to_all x2, starting transfers between devices, exchanged(): return lax.all_to_all(x, 'ctx', 0, 0, tiled=True)  10.1 us
  transfers between devices with their start and end apart: 6, of which 5 were waited for; matrix products, arithmetic and copies ran while one was open for 6% of the time, Pallas kernels for 39%

profile of v2, /device:TPU:11, one launch (start us, length us, event | category | flops | bytes accessed | tf_op | source)
XLA Modules:
  0.0 232.3 jit_solution(10517292966978085377)
XLA Ops:
  0.6 0.0 copy-start.2
  0.6 1.6 slice_bitcast_fusion.1
  2.2 0.3 copy-done.2
  2.5 0.1 slice_bitcast_fusion
  2.6 0.3 pad_maximum_fusion
  2.9 3.7 %collective-permute-start = (bf16[2,512,768]{2,1,0:T(8,128)(2,1)S(1)}, bf16[2,512,768]{2,1,0:T(8,128)(2,1)}, u32[]{:S(2)}, u32[]{:S(2)}) collective-permute-start(bf16[2,512,768]{2,1,0:T(8,128)(2,1)S(1)} %get-tuple-element.78), channel_id=1, source_target_pairs={{0,4},{4,8},{8,12},{12,16},{16,20},{20,24},{24,28},{1,5},{5,9},{9,... | collective-permute-start | bytes 4718600 | tf_op jit(solution)/shard_map/ppermute | solution.py:238
  6.6 1.9 collective-permute-start.1
  8.5 7.9 %pack.1 = bf16[8,4,8,16,768]{4,3,2,1,0:T(8,128)(2,1)} custom-call(bf16[8,128,768]{2,1,0:T(8,128)(2,1)} %bitcast.29, bf16[8,128,768]{2,1,0:T(8,128)(2,1)} %bitcast.30, bf16[8,128,768]{2,1,0:T(8,128)(2,1)} %bitcast.31, bf16[8,128,768]{2,1,0:T(8,128)(2,1)} %bitcast.32), custom_call_target="tpu_custom_call" | custom-call | bytes 12582912 | tf_op jit(solution)/shard_map/pack/pallas_call | solution.py:201
  16.4 0.0 copy-start.6
  16.4 4.8 %all-to-all-start = ((bf16[8,4,8,16,768]{4,3,2,1,0:T(8,128)(2,1)}), bf16[8,4,8,16,768]{4,3,2,1,0:T(8,128)(2,1)}, u32[]{:S(2)}, u32[]{:S(2)}) async-start(bf16[8,4,8,16,768]{4,3,2,1,0:T(8,128)(2,1)} %pack.1), calls=%async_computation | async-start | bytes 12582912 | tf_op jit(solution)/shard_map/all_to_all | solution.py:242
  21.2 0.0 copy-done.6
  21.2 0.7 copy.18.mask
  22.0 16.0 %collective-permute-done.k_lo.v_lo = bf16[2,512,768]{2,1,0:T(8,128)(2,1)} collective-permute-done((bf16[2,512,768]{2,1,0:T(8,128)(2,1)S(1)}, bf16[2,512,768]{2,1,0:T(8,128)(2,1)}, u32[]{:S(2)}, u32[]{:S(2)}) %collective-permute-start) | collective-permute-done | bytes 1572896 | tf_op jit(solution)/shard_map/ppermute | solution.py:238
  38.0 8.4 %collective-permute-done.1.k_hi.v_hi = bf16[2,512,768]{2,1,0:T(8,128)(2,1)} collective-permute-done((bf16[2,512,768]{2,1,0:T(8,128)(2,1)S(1)}, bf16[2,512,768]{2,1,0:T(8,128)(2,1)}, u32[]{:S(2)}, u32[]{:S(2)}) %collective-permute-start.1) | collective-permute-done | bytes 1572896 | tf_op jit(solution)/shard_map/ppermute | solution.py:238
  46.3 49.2 %row_heads.1 = (bf16[1024,768]{1,0:T(8,128)(2,1)}, bf16[1024,768]{1,0:T(8,128)(2,1)}, f32[1024,768]{1,0:T(8,128)}, f32[1024,768]{1,0:T(8,128)}, bf16[2,512,768]{...) custom-call(s32[1]{0:T(128)} %bitcast.first, s32[64,9]{1,0:T(8,128)} %copy.18.mask, bf16[1024,768]{1,0:T(8,128)(2,1)} %q.1, ...), custom_call_target="tpu_custom_call" | custom-call | flops 241591910400 | bytes 23592960 | tf_op jit(solution)/shard_map/row_heads/pallas_call | solution.py:106
  95.6 1.9 collective-permute-start.2
  97.5 4.5 %collective-permute-start.3 = (bf16[2,512,768]{2,1,0:T(8,128)(2,1)}, bf16[2,512,768]{2,1,0:T(8,128)(2,1)S(1)}, u32[]{:S(2)}, u32[]{:S(2)}) collective-permute-start(bf16[2,512,768]{2,1,0:T(8,128)(2,1)} %get-tuple-element.90), channel_id=1, source_target_pairs={{0,4},{4,8},{8,12},{12,16},{16,20},{20,24},{24,28},{1,5},{5,9},{9,... | collective-permute-start | bytes 4718600 | tf_op jit(solution)/shard_map/ppermute | solution.py:238
  102.0 3.5 %all-to-all-done.x = bf16[8,4,8,16,768]{4,3,2,1,0:T(8,128)(2,1)} async-done(((bf16[8,4,8,16,768]{4,3,2,1,0:T(8,128)(2,1)}), bf16[8,4,8,16,768]{4,3,2,1,0:T(8,128)(2,1)}, u32[]{:S(2)}, u32[]{:S(2)}) %all-to-all-start) | async-done | bytes 6291488 | tf_op jit(solution)/shard_map/all_to_all | solution.py:242
  105.5 27.3 %col_heads.1 = (bf16[8,2,8,16,768]{4,3,2,1,0:T(8,128)(2,1)}, bf16[8,2,8,16,768]{4,3,2,1,0:T(8,128)(2,1)}) custom-call(s32[64,64]{1,0:T(8,128)} %mask.2, bf16[8,4,8,16,768]{4,3,2,1,0:T(8,128)(2,1)} %all-to-all-done.x, bf16[1024,768]{1,0:T(8,128)(2,1)} %get-tuple-element.70.earlier), custom_call_target="tpu_custom_call" | custom-call | flops 96636764160 | bytes 12582912 | tf_op jit(solution)/shard_map/col_heads/pallas_call | solution.py:175
  132.8 10.8 %collective-permute-done.2 = bf16[2,512,768]{2,1,0:T(8,128)(2,1)S(1)} collective-permute-done((bf16[2,512,768]{2,1,0:T(8,128)(2,1)}, bf16[2,512,768]{2,1,0:T(8,128)(2,1)S(1)}, u32[]{:S(2)}, u32[]{:S(2)}) %collective-permute-start.2) | collective-permute-done | bytes 1572896 | tf_op jit(solution)/shard_map/ppermute | solution.py:238
  143.6 0.0 copy-start.5
  143.6 0.0 collective-permute-done.3
  143.6 0.0 copy-start.3
  143.6 39.3 %all_to_all.15.x = bf16[8,2,8,16,768]{4,3,2,1,0:T(8,128)(2,1)} all-to-all(bf16[8,2,8,16,768]{4,3,2,1,0:T(8,128)(2,1)} %get-tuple-element.94), channel_id=1, replica_groups=mesh['ctx'=8,'head'=4] {'ctx'}, dimensions={0} | all-to-all | bytes 6291456 | tf_op jit(solution)/shard_map/all_to_all | solution.py:242
  183.0 0.0 copy-done.5
  183.0 0.0 copy-done.3
  183.0 5.2 %all-to-all-start.2 = ((bf16[8,2,8,16,768]{4,3,2,1,0:T(8,128)(2,1)}), bf16[8,2,8,16,768]{4,3,2,1,0:T(8,128)(2,1)S(1)}, u32[]{:S(2)}, u32[]{:S(2)}) async-start(bf16[8,2,8,16,768]{4,3,2,1,0:T(8,128)(2,1)} %get-tuple-element.97), calls=%async_computation.2 | async-start | bytes 6291456 | tf_op jit(solution)/shard_map/all_to_all | solution.py:242
  188.2 0.0 copy-start.4
  188.2 4.4 %fusion.2 = (f32[1024,768]{1,0:T(8,128)}, f32[1024,768]{1,0:T(8,128)}) fusion(f32[1024,768]{1,0:T(8,128)} %get-tuple-element.93, bf16[2,512,768]{2,1,0:T(8,128)(2,1)} %copy-done.5, f32[1024,768]{1,0:T(8,128)} %get-tuple-element.82), kind=kLoop, calls=%fused_computation.7 | loop fusion | flops 1572864 | bytes 7864320 | tf_op jit(solution)/shard_map/scatter-add | solution.py:277
  192.6 0.0 copy-done.4
  192.6 4.0 %fusion = (f32[1024,768]{1,0:T(8,128)}, f32[1024,768]{1,0:T(8,128)}) fusion(f32[1024,768]{1,0:T(8,128)} %get-tuple-element.102, bf16[2,512,768]{2,1,0:T(8,128)(2,1)S(1)} %copy-done.4, f32[1024,768]{1,0:T(8,128)} %get-tuple-element.103), kind=kLoop, calls=%fused_computation.1 | loop fusion | flops 1572864 | bytes 7864320 | tf_op jit(solution)/shard_map/scatter-add | solution.py:278
  196.6 0.0 copy-start.1
  196.6 3.3 %convert_element_type.39 = bf16[1024,768]{1,0:T(8,128)(2,1)} convert(f32[1024,768]{1,0:T(8,128)} %get-tuple-element.100) | non-fusion elementwise | flops 786432 | bytes 4718592 | tf_op jit(solution)/shard_map/convert_element_type | solution.py:279
  200.0 0.0 copy-done.1
  200.0 1.3 convert_element_type.34
  201.3 6.1 %unpack.2 = (bf16[8,128,768]{2,1,0:T(8,128)(2,1)}, bf16[8,128,768]{2,1,0:T(8,128)(2,1)}) custom-call(bf16[8,2,8,16,768]{4,3,2,1,0:T(8,128)(2,1)} %all_to_all.15.x), custom_call_target="tpu_custom_call" | custom-call | bytes 6291456 | tf_op jit(solution)/shard_map/unpack/pallas_call | solution.py:222
  207.4 17.1 %all-to-all-done.2.x = bf16[8,2,8,16,768]{4,3,2,1,0:T(8,128)(2,1)S(1)} async-done(((bf16[8,2,8,16,768]{4,3,2,1,0:T(8,128)(2,1)}), bf16[8,2,8,16,768]{4,3,2,1,0:T(8,128)(2,1)S(1)}, u32[]{:S(2)}, u32[]{:S(2)}) %all-to-all-start.2) | async-done | bytes 3145760 | tf_op jit(solution)/shard_map/all_to_all | solution.py:242
  224.5 0.0 copy-start
  224.5 1.6 copy-done
  226.2 6.1 %unpack.3 = (bf16[8,128,768]{2,1,0:T(8,128)(2,1)}, bf16[8,128,768]{2,1,0:T(8,128)(2,1)}) custom-call(bf16[8,2,8,16,768]{4,3,2,1,0:T(8,128)(2,1)} %copy-done), custom_call_target="tpu_custom_call" | custom-call | bytes 6291456 | tf_op jit(solution)/shard_map/unpack/pallas_call | solution.py:222
Async XLA Ops:
  0.6 1.9 copy-start.2
  2.9 35.1 %collective-permute-start = (bf16[2,512,768]{2,1,0:T(8,128)(2,1)S(1)}, bf16[2,512,768]{2,1,0:T(8,128)(2,1)}, u32[]{:S(2)}, u32[]{:S(2)}) collective-permute-start(bf16[2,512,768]{2,1,0:T(8,128)(2,1)S(1)} %get-tuple-element.78), channel_id=1, source_target_pairs={{0,4},{4,8},{8,12},{12,16},{16,20},{20,24},{24,28},{1,5},{5,9},{9,... | collective-permute-start | bytes 4718600 | tf_op jit(solution)/shard_map/ppermute | solution.py:238
  6.6 39.8 %collective-permute-start.1 = (bf16[2,512,768]{2,1,0:T(8,128)(2,1)S(1)}, bf16[2,512,768]{2,1,0:T(8,128)(2,1)}, u32[]{:S(2)}, u32[]{:S(2)}) collective-permute-start(bf16[2,512,768]{2,1,0:T(8,128)(2,1)S(1)} %get-tuple-element.79), channel_id=1, source_target_pairs={{4,0},{8,4},{12,8},{16,12},{20,16},{24,20},{28,24},{5,1},{9,5},{13... | collective-permute-start | bytes 4718600 | tf_op jit(solution)/shard_map/ppermute | solution.py:238
  16.4 4.9 %copy-start.6 = (s32[64,9]{0,1:T(8,128)S(1)}, s32[64,9]{0,1:T(8,128)}, u32[]{:S(2)}) copy-start(s32[64,9]{0,1:T(8,128)} %param.22) | copy-start | bytes 6916
  16.4 89.1 %all-to-all-start = ((bf16[8,4,8,16,768]{4,3,2,1,0:T(8,128)(2,1)}), bf16[8,4,8,16,768]{4,3,2,1,0:T(8,128)(2,1)}, u32[]{:S(2)}, u32[]{:S(2)}) async-start(bf16[8,4,8,16,768]{4,3,2,1,0:T(8,128)(2,1)} %pack.1), calls=%async_computation | async-start | bytes 12582912 | tf_op jit(solution)/shard_map/all_to_all | solution.py:242
  95.6 48.1 %collective-permute-start.2 = (bf16[2,512,768]{2,1,0:T(8,128)(2,1)}, bf16[2,512,768]{2,1,0:T(8,128)(2,1)S(1)}, u32[]{:S(2)}, u32[]{:S(2)}) collective-permute-start(bf16[2,512,768]{2,1,0:T(8,128)(2,1)} %get-tuple-element.89), channel_id=1, source_target_pairs={{4,0},{8,4},{12,8},{16,12},{20,16},{24,20},{28,24},{5,1},{9,5},{13... | collective-permute-start | bytes 4718600 | tf_op jit(solution)/shard_map/ppermute | solution.py:238
  97.5 46.2 %collective-permute-start.3 = (bf16[2,512,768]{2,1,0:T(8,128)(2,1)}, bf16[2,512,768]{2,1,0:T(8,128)(2,1)S(1)}, u32[]{:S(2)}, u32[]{:S(2)}) collective-permute-start(bf16[2,512,768]{2,1,0:T(8,128)(2,1)} %get-tuple-element.90), channel_id=1, source_target_pairs={{0,4},{4,8},{8,12},{12,16},{16,20},{20,24},{24,28},{1,5},{5,9},{9,... | collective-permute-start | bytes 4718600 | tf_op jit(solution)/shard_map/ppermute | solution.py:238
  143.6 39.3 %copy-start.5 = (bf16[2,512,768]{2,1,0:T(8,128)(2,1)}, bf16[2,512,768]{2,1,0:T(8,128)(2,1)S(1)}, u32[]{:S(2)}) copy-start(bf16[2,512,768]{2,1,0:T(8,128)(2,1)S(1)} %collective-permute-done.2) | copy-start | bytes 4718596
  143.6 39.3 %copy-start.3 = (bf16[2,512,768]{2,1,0:T(8,128)(2,1)}, bf16[2,512,768]{2,1,0:T(8,128)(2,1)S(1)}, u32[]{:S(2)}) copy-start(bf16[2,512,768]{2,1,0:T(8,128)(2,1)S(1)} %collective-permute-done.3) | copy-start | bytes 4718596
  183.0 41.6 %all-to-all-start.2 = ((bf16[8,2,8,16,768]{4,3,2,1,0:T(8,128)(2,1)}), bf16[8,2,8,16,768]{4,3,2,1,0:T(8,128)(2,1)S(1)}, u32[]{:S(2)}, u32[]{:S(2)}) async-start(bf16[8,2,8,16,768]{4,3,2,1,0:T(8,128)(2,1)} %get-tuple-element.97), calls=%async_computation.2 | async-start | bytes 6291456 | tf_op jit(solution)/shard_map/all_to_all | solution.py:242
  188.2 4.4 %copy-start.4 = (bf16[2,512,768]{2,1,0:T(8,128)(2,1)S(1)}, bf16[2,512,768]{2,1,0:T(8,128)(2,1)}, u32[]{:S(2)}) copy-start(bf16[2,512,768]{2,1,0:T(8,128)(2,1)} %copy-done.3) | copy-start | bytes 4718596
  196.6 3.3 %copy-start.1 = (f32[1024,768]{1,0:T(8,128)S(1)}, f32[1024,768]{1,0:T(8,128)}, u32[]{:S(2)}) copy-start(f32[1024,768]{1,0:T(8,128)} %get-tuple-element.101) | copy-start | bytes 9437188
  224.5 1.6 copy-start

commit v3 on v2

--- a/solution.py
+++ b/solution.py
@@ -1,4 +1,5 @@
 import functools
+import math
 
 import jax
 import jax.numpy as jnp
@@ -15,6 +16,7 @@
 SCALE = HEAD_DIM**-0.5
 EXP2_SCALE = SCALE * float(np.log2(np.e))
 VMEM = 60 << 20
+CHIPS_APART = 4
 
 
 def contract(a, b, dim_a, dim_b):
@@ -42,8 +44,8 @@
 
 
 def row_kernel(
-    band, first, mask, q, k, v, d, k_lo, v_lo, k_hi, v_hi,
-    out, dq, dk, dv, lo, hi, keys, values, acc_k, acc_v,
+    band, place, mask, q, k, v, d, k_lo, v_lo, k_hi, v_hi, v_far,
+    out, dq, dk, dv, lo_k, lo_v, hi_k, hi_v, keys, values, acc_k, acc_v,
 ):
     tokens = q.shape[0]
     rim = k_lo.shape[0]
@@ -51,6 +53,15 @@
         whole[:rim] = before[...]
         whole[rim : rim + tokens] = own[...]
         whole[rim + tokens :] = after[...]
+
+    @pl.when(place[1] == 0)
+    def _():
+        values[:rim] = v_far[...]
+
+    @pl.when(place[1] == CHIPS_APART - 1)
+    def _():
+        values[rim + tokens :] = v_far[...]
+
     acc_k[...] = jnp.zeros_like(acc_k)
     acc_v[...] = jnp.zeros_like(acc_v)
     blocks = 2 * band + 2
@@ -74,7 +85,7 @@
         def add_bias(scores):
             return jnp.concatenate(
                 [
-                    scores[b * GRIDC : (b + 1) * GRIDC] + block_bias(first[0] + 2 * pair, b)
+                    scores[b * GRIDC : (b + 1) * GRIDC] + block_bias(place[0] + 2 * pair, b)
                     for b in range(blocks)
                 ],
                 axis=0,
@@ -87,35 +98,33 @@
         dq[here] = grad_query
         acc_k[window] += grad_keys
         acc_v[window] += grad_values
-    for at, (acc, own, factor) in enumerate(((acc_k, dk, SCALE), (acc_v, dv, 1.0))):
+    for acc, own, lo, hi, factor in ((acc_k, dk, lo_k, hi_k, SCALE), (acc_v, dv, lo_v, hi_v, 1.0)):
         own[...] = acc[rim : rim + tokens] * factor
-        lo[at] = (acc[:rim] * factor).astype(lo.dtype)
-        hi[at] = (acc[rim + tokens :] * factor).astype(hi.dtype)
-
-
-def row_attention(first, mask, q, k, v, d, before, after, band):
+        lo[...] = (acc[:rim] * factor).astype(lo.dtype)
+        hi[...] = (acc[rim + tokens :] * factor).astype(hi.dtype)
+
+
+def row_attention(place, mask, q, k, v, d, halos, band):
     tokens, feat = q.shape
     heads = feat // HEAD_DIM
     rim = band * GRIDC
     tall = pl.BlockSpec((tokens, HEAD_DIM), lambda h: (0, h))
-    rims = [pl.BlockSpec((None, rim, HEAD_DIM), lambda h, a=a: (a, 0, h)) for a in range(2)]
-    both = pl.BlockSpec((2, rim, HEAD_DIM), lambda h: (0, 0, h))
+    edge = pl.BlockSpec((rim, HEAD_DIM), lambda h: (0, h))
     scalars = pl.BlockSpec(memory_space=pltpu.SMEM)
     padded = tokens + 2 * rim
     pairs = tokens * (2 * band + 2) * GRIDC * heads
     return pl.pallas_call(
         functools.partial(row_kernel, band),
         grid=(heads,),
-        in_specs=[scalars, scalars, tall, tall, tall, tall, *rims, *rims],
-        out_specs=[tall, tall, tall, tall, both, both],
+        in_specs=[scalars, scalars, tall, tall, tall, tall] + [edge] * 5,
+        out_specs=[tall] * 4 + [edge] * 4,
         out_shape=[
             jax.ShapeDtypeStruct(q.shape, jnp.bfloat16),
             jax.ShapeDtypeStruct(q.shape, jnp.bfloat16),
             jax.ShapeDtypeStruct(q.shape, jnp.float32),
             jax.ShapeDtypeStruct(q.shape, jnp.float32),
-            jax.ShapeDtypeStruct((2, rim, feat), jnp.bfloat16),
-            jax.ShapeDtypeStruct((2, rim, feat), jnp.bfloat16),
-        ],
+        ]
+        + [jax.ShapeDtypeStruct((rim, feat), jnp.bfloat16)] * 4,
         scratch_shapes=[
             pltpu.VMEM((padded, HEAD_DIM), jnp.bfloat16),
             pltpu.VMEM((padded, HEAD_DIM), jnp.bfloat16),
@@ -127,10 +136,10 @@
             flops=240 * pairs * HEAD_DIM, bytes_accessed=30 * tokens * feat, transcendentals=pairs
         ),
         name="row_heads",
-    )(first, mask, q, k, v, d, before, before, after, after)
-
-
-def col_kernel(mask, x, earlier, first, second, bias):
+    )(place, mask, q, k, v, d, *halos)
+
+
+def col_kernel(mask, x, earlier, out, bias):
     del earlier
     @pl.when((pl.program_id(0) == 0) & (pl.program_id(1) == 0))
     def _():
@@ -159,27 +168,27 @@
         grad_values += more_values
         outputs.append(output)
         grads.append(grad_query)
-    first[:, 0] = jnp.concatenate(outputs, 0).reshape(shape)
-    first[:, 1] = jnp.concatenate(grads, 0).reshape(shape)
-    second[:, 0] = (grad_keys * SCALE).astype(jnp.bfloat16).reshape(shape)
-    second[:, 1] = grad_values.astype(jnp.bfloat16).reshape(shape)
-
-
-def col_attention(mask, x, earlier):
-    n, _, rows, cols, feat = x.shape
-    heads = feat // HEAD_DIM
+    out[:, 0] = jnp.concatenate(outputs, 0).reshape(shape)
+    out[:, 1] = jnp.concatenate(grads, 0).reshape(shape)
+    out[:, 2] = (grad_keys * SCALE).astype(jnp.bfloat16).reshape(shape)
+    out[:, 3] = grad_values.astype(jnp.bfloat16).reshape(shape)
+
+
+def col_attention(mask, x, earlier, start, heads):
+    n, k, rows, cols, _ = x.shape
     tokens = n * rows * GROUP
-    spec = lambda k: pl.BlockSpec((n, k, rows, GROUP, HEAD_DIM), lambda h, g: (0, 0, 0, g, h))
-    half = jax.ShapeDtypeStruct((n, 2, rows, cols, feat), jnp.bfloat16)
+    block = (n, k, rows, GROUP, HEAD_DIM)
     pairs = tokens * tokens * heads * (cols // GROUP)
     return pl.pallas_call(
         col_kernel,
         grid=(heads, cols // GROUP),
         in_specs=[
-            pl.BlockSpec(mask.shape, lambda h, g: (0, 0)), spec(4), pl.BlockSpec(memory_space=pl.ANY)
+            pl.BlockSpec(mask.shape, lambda h, g: (0, 0)),
+            pl.BlockSpec(block, lambda h, g: (0, 0, 0, g, h + start)),
+            pl.BlockSpec(memory_space=pl.ANY),
         ],
-        out_specs=[spec(2), spec(2)],
-        out_shape=[half, half],
+        out_specs=pl.BlockSpec(block, lambda h, g: (0, 0, 0, g, h)),
+        out_shape=jax.ShapeDtypeStruct((n, k, rows, cols, heads * HEAD_DIM), jnp.bfloat16),
         scratch_shapes=[pltpu.VMEM((tokens, tokens), jnp.float32)],
         compiler_params=pltpu.CompilerParams(vmem_limit_bytes=VMEM),
         cost_estimate=pl.CostEstimate(
@@ -212,30 +221,47 @@
     )(*(a.reshape(rows, GRIDC, feat) for a in arrays))
 
 
-def unpack_kernel(x, *parts):
-    for a, part in enumerate(parts):
+def unpack_kernel(x, *refs):
+    for a, part in enumerate(refs[-x.shape[0] :]):
         part[...] = x[a]
 
 
-def unpacked(x):
-    n, k, rows, cols, feat = x.shape
+def unpacked(x, start, whole):
+    n, k, rows, cols, width = x.shape
+    kept = [] if isinstance(whole, int) else [a.reshape(rows, n * cols, -1) for a in whole]
+    feat = kept[0].shape[-1] if kept else whole
+    step = math.gcd(start, width) if start else width
+    spec = pl.BlockSpec((rows, cols, step), lambda j, f: (0, j, start // step + f))
     outs = pl.pallas_call(
         unpack_kernel,
-        grid=(n,),
-        in_specs=[pl.BlockSpec((None, k, rows, cols, feat), lambda j: (j, 0, 0, 0, 0))],
-        out_specs=[pl.BlockSpec((rows, cols, feat), lambda j: (0, j, 0))] * k,
+        grid=(n, width // step),
+        in_specs=[pl.BlockSpec((None, k, rows, cols, step), lambda j, f: (j, 0, 0, 0, f))]
+        + [pl.BlockSpec(memory_space=pl.ANY)] * len(kept),
+        out_specs=[spec] * k,
         out_shape=[jax.ShapeDtypeStruct((rows, n * cols, feat), jnp.bfloat16)] * k,
+        input_output_aliases={1 + a: a for a in range(len(kept))},
         compiler_params=pltpu.CompilerParams(vmem_limit_bytes=VMEM),
         cost_estimate=pl.CostEstimate(flops=0, bytes_accessed=4 * x.size, transcendentals=0),
         name="unpack",
-    )(x)
+    )(x, *kept)
     return [o.reshape(rows * n * cols, feat) for o in outs]
 
 
-def passed_along(block, distance):
-    devices = range(lax.axis_size("ctx"))
-    route = [(i - distance, i) for i in devices if i - distance in devices]
-    return lax.ppermute(block, "ctx", route)
+def swapped(lo_k, lo_v, hi_k, hi_v):
+    n = lax.axis_size("ctx")
+    up = [(i, i + 1) for i in range(n - 1)]
+    down = [(j, i) for i, j in up]
+    far = [(i, j) for i, j in up if j % CHIPS_APART == 0 and j + CHIPS_APART <= n]
+    near_up = [pair for pair in up if pair not in far]
+    near_down = [(j, i) for i, j in near_up]
+    side = lax.axis_index("ctx") % CHIPS_APART
+    first = [(i, i + CHIPS_APART) for i, _ in far] + [(j, j - CHIPS_APART) for _, j in far]
+    second = [(i + CHIPS_APART, j) for i, j in far] + [(j - CHIPS_APART, i) for i, j in far]
+    hop = lax.ppermute(jnp.where(side == 0, lo_v, hi_v), "ctx", first)
+    k_before, k_after = lax.ppermute(hi_k, "ctx", up), lax.ppermute(lo_k, "ctx", down)
+    v_before, v_after = lax.ppermute(hi_v, "ctx", near_up), lax.ppermute(lo_v, "ctx", near_down)
+    far_v = lax.ppermute(hop, "ctx", second)
+    return [k_before, v_before, k_after, v_after, far_v], hop
 
 
 def exchanged(x):
@@ -251,35 +277,43 @@
     rows = tokens // GRIDC
     band = (row_mask.shape[1] - 1) // 2
     rim = band * GRIDC
-    first_row = lax.axis_index("ctx") * rows
-
-    tops = jnp.stack([row_key[:rim], row_value[:rim]])
-    ends = jnp.stack([row_key[tokens - rim :], row_value[tokens - rim :]])
+
+    rims = [a for x in (row_key, row_value) for a in (x[:rim], x[tokens - rim :])]
     cols = [col_query, col_key, col_value, col_cotangent]
-    tops, ends, *cols = lax.optimization_barrier((tops, ends, *cols))
-    after, before = passed_along(tops, -1), passed_along(ends, 1)
-    moved = exchanged(packed(cols, n))
-
-    row_output, row_dquery, own_k, own_v, lo, hi = row_attention(
-        first_row.reshape(1), row_mask, row_query, row_key, row_value, row_cotangent, before, after, band
+    *rims, cols = lax.optimization_barrier((*rims, cols))
+    halos, hop = swapped(rims[0], rims[2], rims[1], rims[3])
+    sent, hop = lax.optimization_barrier((packed(cols, n), hop))
+    moved = exchanged(sent)
+
+    me = lax.axis_index("ctx")
+    place = jnp.stack([me * rows, me % CHIPS_APART])
+    row_output, row_dquery, own_k, own_v, *sides = row_attention(
+        place, row_mask, row_query, row_key, row_value, row_cotangent, halos, band
     )
-    from_next, from_prev = passed_along(lo, -1), passed_along(hi, 1)
-
-    first, second = col_attention(col_mask, moved, row_output)
-    first, second, from_next, from_prev = lax.optimization_barrier(
-        (first, second, from_next, from_prev)
-    )
-    col_output, col_dquery = unpacked(exchanged(first))
-    col_dkeys, col_dvalues = unpacked(exchanged(second))
-
+    (k_before, v_before, k_after, v_after, far_v), hop = swapped(*sides)
+
+    feat = col_query.shape[1]
+    heads = feat // HEAD_DIM
+    half = heads // 2
+    first = col_attention(col_mask, moved, row_output, 0, half)
+    first, k_before, k_after, hop = lax.optimization_barrier((first, k_before, k_after, hop))
+    second = col_attention(col_mask, moved, first, half, heads - half)
+    second, v_before, v_after, far_v = lax.optimization_barrier((second, v_before, v_after, far_v))
+    first, second = exchanged(first), exchanged(second)
+    col_results = unpacked(second, half * HEAD_DIM, unpacked(first, 0, feat))
+
+    v_before = jnp.where(me % CHIPS_APART == 0, far_v, v_before)
+    v_after = jnp.where(me % CHIPS_APART == CHIPS_APART - 1, far_v, v_after)
     row_grads = []
-    for at, own in enumerate((own_k, own_v)):
-        own = own.at[tokens - rim :].add(from_next[at].astype(jnp.float32))
-        own = own.at[:rim].add(from_prev[at].astype(jnp.float32))
-        row_grads.append(own.astype(jnp.bfloat16))
+    for own, prev, following in ((own_k, k_before, k_after), (own_v, v_before, v_after)):
+        gap = jnp.zeros((tokens - rim, own.shape[1]), own.dtype)
+        added = jnp.concatenate([prev.astype(own.dtype), gap]) + jnp.concatenate(
+            [gap, following.astype(own.dtype)]
+        )
+        row_grads.append((own + added).astype(jnp.bfloat16))
     return (
         row_output, row_dquery, *row_grads,
-        col_output, col_dquery, col_dkeys, col_dvalues,
+        *col_results,
     )
 
 

time: 235 us -> 228 us (0.970)
  blocking collectives: 39.3 us -> 0 us
  starting transfers between devices: 22.1 us -> 54.3 us
  other arithmetic: 13.3 us -> 7.97 us
  Pallas kernels: 96.6 us -> 99.5 us
    all_to_all x1 -> x0, blocking collectives: 39.3 us -> none  [exchanged(): return lax.all_to_all(x, 'ctx', 0, 0, tiled=True)]
    ppermute x4 -> x12, waiting for transfers between devices: 35.2 us -> 10.2 us  [the longest x2 9.53 us: swapped(): hop = lax.ppermute(jnp.where(side == 0, lo_v, hi_v), 'ctx', first)]
    all_to_all x2 -> x3, waiting for transfers between devices: 20.6 us -> 44.8 us  [exchanged(): return lax.all_to_all(x, 'ctx', 0, 0, tiled=True)]
    ppermute x4 -> x12, starting transfers between devices: 12.1 us -> 31.3 us  [the longest x2 9.63 us: swapped(): hop = lax.ppermute(jnp.where(side == 0, lo_v, hi_v), 'ctx', first)]
    all_to_all x2 -> x3, starting transfers between devices: 10.1 us -> 23.1 us  [exchanged(): return lax.all_to_all(x, 'ctx', 0, 0, tiled=True)]
    scatter-add x2 -> x0, other arithmetic: 8.41 us -> none  [the longest x1 4.43 us: body(): own = own.at[tokens - rim:].add(from_next[at].astype(jnp.float32))]
    select_n x0 -> x3, other arithmetic: none -> 3.08 us  [the longest x1 1.65 us: body(): v_before = jnp.where(me % CHIPS_APART == 0, far_v, v_before)]
    pallas_call x1 -> x2, Pallas kernels: 27.3 us -> 29.8 us  [col_attention(): pl.pallas_call(col_kernel, grid=(heads, cols // GROUP), in_specs=[pl.Bloc...]
  transfers between devices with their start and end apart: 6 -> 15, of which waited for: 5 -> 4; matrix products, arithmetic and copies ran while one was open for 6% -> 4% of each run, Pallas kernels for 39% -> 42%
where the time goes in v3:
time: 228 us; the launch traced here: 224 us
  Pallas kernels  99.5 us (44%)
  waiting for transfers between devices  55.1 us (24%)
  starting transfers between devices  54.3 us (24%)
  other arithmetic  7.97 us (3%)
  local copies, waits for them, and re-layouts  6.44 us (3%)
    pallas_call x1, Pallas kernels, row_attention(): pl.pallas_call(functools.partial(row_kernel, band), grid=(heads,), in_spe...  49.6 us
    all_to_all x3, waiting for transfers between devices, exchanged(): return lax.all_to_all(x, 'ctx', 0, 0, tiled=True)  44.8 us
    pallas_call x2, Pallas kernels, col_attention(): pl.pallas_call(col_kernel, grid=(heads, cols // GROUP), in_specs=[pl.Bloc...  29.8 us
    all_to_all x3, starting transfers between devices, exchanged(): return lax.all_to_all(x, 'ctx', 0, 0, tiled=True)  23.1 us
    pallas_call x2, Pallas kernels, unpacked(): pl.pallas_call(unpack_kernel, grid=(n, width // step), in_specs=[pl.Block...  12.3 us
    ppermute x2, starting transfers between devices, swapped(): hop = lax.ppermute(jnp.where(side == 0, lo_v, hi_v), 'ctx', first)  9.63 us
    ppermute x2, waiting for transfers between devices, swapped(): hop = lax.ppermute(jnp.where(side == 0, lo_v, hi_v), 'ctx', first)  9.53 us
    ppermute x2, starting transfers between devices, swapped(): lax.ppermute(lo_v, 'ctx', near_down)  7.87 us
  transfers between devices with their start and end apart: 15, of which 4 were waited for; matrix products, arithmetic and copies ran while one was open for 4% of the time, Pallas kernels for 42%

profile of v3, /device:TPU:11, one launch (start us, length us, event | category | flops | bytes accessed | tf_op | source)
XLA Modules:
  0.0 224.2 jit_solution(10274546550560111091)
XLA Ops:
  0.6 2.1 fusion
  2.7 0.0 copy-start.6
  2.7 0.1 broadcast_select_fusion.3
  2.8 4.1 %collective-permute-start.4 = (bf16[512,768]{1,0:T(8,128)(2,1)S(1)}, bf16[512,768]{1,0:T(8,128)(2,1)}, u32[]{:S(2)}, u32[]{:S(2)}) collective-permute-start(bf16[512,768]{1,0:T(8,128)(2,1)S(1)} %broadcast_select_fusion.3), channel_id=1, source_target_pairs={{12,28},{16,0},{13,29},{17,1},{14,30},{18,2},{15,31},{19,3}} | collective-permute-start | bytes 2359304 | tf_op jit(solution)/shard_map/ppermute | solution.py:260
  6.9 1.3 collective-permute-start.1
  8.2 3.9 %collective-permute-start.3 = (bf16[512,768]{1,0:T(8,128)(2,1)S(1)}, bf16[512,768]{1,0:T(8,128)(2,1)}, u32[]{:S(2)}, u32[]{:S(2)}) collective-permute-start(bf16[512,768]{1,0:T(8,128)(2,1)S(1)} %get-tuple-element.43), channel_id=1, source_target_pairs={{4,0},{8,4},{12,8},{20,16},{24,20},{28,24},{5,1},{9,5},{13,9},{21,... | collective-permute-start | bytes 2359304 | tf_op jit(solution)/shard_map/ppermute | solution.py:262
  12.1 1.9 collective-permute-start
  14.1 2.4 %collective-permute-start.2 = (bf16[512,768]{1,0:T(8,128)(2,1)S(1)}, bf16[512,768]{1,0:T(8,128)(2,1)}, u32[]{:S(2)}, u32[]{:S(2)}) collective-permute-start(bf16[512,768]{1,0:T(8,128)(2,1)S(1)} %get-tuple-element.42), channel_id=1, source_target_pairs={{4,0},{8,4},{12,8},{16,12},{20,16},{24,20},{28,24},{5,1},{9,5},{13... | collective-permute-start | bytes 2359304 | tf_op jit(solution)/shard_map/ppermute | solution.py:261
  16.5 0.0 collective-permute-done.4
  16.5 1.3 collective-permute-start.5
  17.8 0.0 copy-done.6
  17.8 0.7 copy.22.mask
  18.5 7.9 %pack.1 = bf16[8,4,8,16,768]{4,3,2,1,0:T(8,128)(2,1)} custom-call(bf16[8,128,768]{2,1,0:T(8,128)(2,1)} %bitcast.10, bf16[8,128,768]{2,1,0:T(8,128)(2,1)} %bitcast.11, bf16[8,128,768]{2,1,0:T(8,128)(2,1)} %bitcast.12, bf16[8,128,768]{2,1,0:T(8,128)(2,1)} %bitcast.13), custom_call_target="tpu_custom_call" | custom-call | bytes 12582912 | tf_op jit(solution)/shard_map/pack/pallas_call | solution.py:210
  26.4 0.6 pad_add_fusion.place
  27.0 7.9 %all-to-all-start = ((bf16[8,4,8,16,768]{4,3,2,1,0:T(8,128)(2,1)}), bf16[8,4,8,16,768]{4,3,2,1,0:T(8,128)(2,1)}, u32[]{:S(2)}, u32[]{:S(2)}) async-start(bf16[8,4,8,16,768]{4,3,2,1,0:T(8,128)(2,1)} %pack.1), calls=%async_computation | async-start | bytes 12582912 | tf_op jit(solution)/shard_map/all_to_all | solution.py:268
  34.9 0.0 collective-permute-done.k_lo
  34.9 0.0 collective-permute-done.1.v_lo
  34.9 0.7 collective-permute-done.2.k_hi
  35.6 0.0 collective-permute-done.3.v_hi
  35.6 0.0 collective-permute-done.5.v_far
  35.6 49.6 %row_heads.1 = (bf16[1024,768]{1,0:T(8,128)(2,1)}, bf16[1024,768]{1,0:T(8,128)(2,1)}, f32[1024,768]{1,0:T(8,128)}, f32[1024,768]{1,0:T(8,128)}, bf16[512,768]{1,...) custom-call(s32[2]{0:T(128)} %pad_add_fusion.place, ...), custom_call_target="tpu_custom_call" | custom-call | flops 241591910400 | bytes 23592960 | tf_op jit(solution)/shard_map/row_heads/pallas_call | solution.py:116
  85.3 0.0 copy-start.8
  85.3 0.0 copy-start.7
  85.3 1.3 broadcast_select_fusion.2
  86.6 5.5 %collective-permute-start.8 = (bf16[512,768]{1,0:T(8,128)(2,1)S(1)}, bf16[512,768]{1,0:T(8,128)(2,1)}, u32[]{:S(2)}, u32[]{:S(2)}) collective-permute-start(bf16[512,768]{1,0:T(8,128)(2,1)S(1)} %broadcast_select_fusion.2), channel_id=1, source_target_pairs={{12,28},{16,0},{13,29},{17,1},{14,30},{18,2},{15,31},{19,3}} | collective-permute-start | bytes 2359304 | tf_op jit(solution)/shard_map/ppermute | solution.py:260
  92.2 1.3 collective-permute-start.9
  93.5 3.9 %collective-permute-start.10 = (bf16[512,768]{1,0:T(8,128)(2,1)}, bf16[512,768]{1,0:T(8,128)(2,1)}, u32[]{:S(2)}, u32[]{:S(2)}) collective-permute-start(bf16[512,768]{1,0:T(8,128)(2,1)} %get-tuple-element.54), channel_id=1, source_target_pairs={{4,0},{8,4},{12,8},{20,16},{24,20},{28,24},{5,1},{9,5},{13,9},{21,... | collective-permute-start | bytes 2359304 | tf_op jit(solution)/shard_map/ppermute | solution.py:262
  97.4 0.0 copy-done.8
  97.4 1.9 collective-permute-start.6
  99.3 0.0 copy-done.7
  99.3 2.4 %collective-permute-start.7 = (bf16[512,768]{1,0:T(8,128)(2,1)S(1)}, bf16[512,768]{1,0:T(8,128)(2,1)S(1)}, u32[]{:S(2)}, u32[]{:S(2)}) collective-permute-start(bf16[512,768]{1,0:T(8,128)(2,1)S(1)} %copy-done.7), channel_id=1, source_target_pairs={{4,0},{8,4},{12,8},{16,12},{20,16},{24,20},{28,24},{5,1},{9,5},{13... | collective-permute-start | bytes 2359304 | tf_op jit(solution)/shard_map/ppermute | solution.py:261
  101.7 9.5 %collective-permute-done.8 = bf16[512,768]{1,0:T(8,128)(2,1)} collective-permute-done((bf16[512,768]{1,0:T(8,128)(2,1)S(1)}, bf16[512,768]{1,0:T(8,128)(2,1)}, u32[]{:S(2)}, u32[]{:S(2)}) %collective-permute-start.8) | collective-permute-done | bytes 786464 | tf_op jit(solution)/shard_map/ppermute | solution.py:260
  111.3 1.3 collective-permute-start.11
  112.6 0.0 all-to-all-done.x
  112.6 14.8 %col_heads.2.earlier = bf16[8,4,8,16,384]{4,3,2,1,0:T(8,128)(2,1)} custom-call(s32[64,64]{1,0:T(8,128)} %mask.4, bf16[8,4,8,16,768]{4,3,2,1,0:T(8,128)(2,1)} %all-to-all-done.x, bf16[1024,768]{1,0:T(8,128)(2,1)} %get-tuple-element.32.earlier), custom_call_target="tpu_custom_call" | custom-call | flops 48318382080 | bytes 12582912 | tf_op jit(solution)/shard_map/col_heads/pallas_call | solution.py:182
  127.4 0.0 collective-permute-done.6
  127.4 0.0 copy-start.3
  127.4 0.0 collective-permute-done.7
  127.4 0.0 copy-start.5
  127.4 0.9 copy-done.3
  128.3 0.3 copy-done.5
  128.6 9.2 %all-to-all-start.2 = ((bf16[8,4,8,16,384]{4,3,2,1,0:T(8,128)(2,1)}), bf16[8,4,8,16,384]{4,3,2,1,0:T(8,128)(2,1)S(1)}, u32[]{:S(2)}, u32[]{:S(2)}) async-start(bf16[8,4,8,16,384]{4,3,2,1,0:T(8,128)(2,1)} %col_heads.2.earlier), calls=%async_computation.2 | async-start | bytes 6291456 | tf_op jit(solution)/shard_map/all_to_all | solution.py:268
  137.8 14.9 %col_heads.3 = bf16[8,4,8,16,384]{4,3,2,1,0:T(8,128)(2,1)} custom-call(s32[64,64]{1,0:T(8,128)} %mask.4, bf16[8,4,8,16,768]{4,3,2,1,0:T(8,128)(2,1)} %all-to-all-done.x, bf16[8,4,8,16,384]{4,3,2,1,0:T(8,128)(2,1)} %col_heads.2.earlier), custom_call_target="tpu_custom_call" | custom-call | flops 48318382080 | bytes 12582912 | tf_op jit(solution)/shard_map/col_heads/pallas_call | solution.py:182
  152.7 0.0 collective-permute-done.9
  152.7 0.0 collective-permute-done.10
  152.7 0.0 collective-permute-done.11
  152.7 21.3 %all-to-all-done.2.x = bf16[8,4,8,16,384]{4,3,2,1,0:T(8,128)(2,1)S(1)} async-done(((bf16[8,4,8,16,384]{4,3,2,1,0:T(8,128)(2,1)}), bf16[8,4,8,16,384]{4,3,2,1,0:T(8,128)(2,1)S(1)}, u32[]{:S(2)}, u32[]{:S(2)}) %all-to-all-start.2) | async-done | bytes 3145760 | tf_op jit(solution)/shard_map/all_to_all | solution.py:268
  174.1 0.0 copy-start
  174.1 1.6 copy-done
  175.7 5.9 %all-to-all-start.1 = ((bf16[8,4,8,16,384]{4,3,2,1,0:T(8,128)(2,1)}), bf16[8,4,8,16,384]{4,3,2,1,0:T(8,128)(2,1)}, u32[]{:S(2)}, u32[]{:S(2)}) async-start(bf16[8,4,8,16,384]{4,3,2,1,0:T(8,128)(2,1)} %col_heads.3), calls=%async_computation.1 | async-start | bytes 6291456 | tf_op jit(solution)/shard_map/all_to_all | solution.py:268
  181.7 0.0 copy-start.2
  181.7 0.0 copy-start.4
  181.7 1.6 broadcast_select_fusion.1
  183.3 0.7 copy-done.2
  184.0 0.2 copy-done.4
  184.2 0.0 copy-start.1
  184.2 2.8 %add_convert_fusion.1 = bf16[1024,768]{1,0:T(8,128)(2,1)} fusion(f32[1024,768]{1,0:T(8,128)S(1)} %copy-done.2, bf16[512,768]{1,0:T(8,128)(2,1)} %copy-done.5, bf16[512,768]{1,0:T(8,128)(2,1)S(1)} %copy-done.4), kind=kLoop, calls=%fused_computation.1 | loop fusion | flops 3932160 | bytes 6291456 | tf_op jit(solution)/shard_map/convert_element_type | solution.py:313
  187.0 0.0 copy-done.1
  187.0 1.5 add_convert_fusion
  188.5 6.1 %unpack.2 = (bf16[8,128,768]{2,1,0:T(8,128)(2,1)}, bf16[8,128,768]{2,1,0:T(8,128)(2,1)}, bf16[8,128,768]{2,1,0:T(8,128)(2,1)}, bf16[8,128,768]{2,1,0:T(8,128)(2,1)}) custom-call(bf16[8,4,8,16,384]{4,3,2,1,0:T(8,128)(2,1)} %copy-done), custom_call_target="tpu_custom_call" | custom-call | bytes 6291456 | tf_op jit(solution)/shard_map/unpack/pallas_call | solution.py:235
  194.6 23.5 %all-to-all-done.1.x = bf16[8,4,8,16,384]{4,3,2,1,0:T(8,128)(2,1)} async-done(((bf16[8,4,8,16,384]{4,3,2,1,0:T(8,128)(2,1)}), bf16[8,4,8,16,384]{4,3,2,1,0:T(8,128)(2,1)}, u32[]{:S(2)}, u32[]{:S(2)}) %all-to-all-start.1) | async-done | bytes 3145760 | tf_op jit(solution)/shard_map/all_to_all | solution.py:268
  218.1 6.1 %unpack.3 = (bf16[8,128,768]{2,1,0:T(8,128)(2,1)}, bf16[8,128,768]{2,1,0:T(8,128)(2,1)}, bf16[8,128,768]{2,1,0:T(8,128)(2,1)}, bf16[8,128,768]{2,1,0:T(8,128)(2,1)}) custom-call(bf16[8,4,8,16,384]{4,3,2,1,0:T(8,128)(2,1)} %all-to-all-done.1.x, ...), custom_call_target="tpu_custom_call", output_to_operand_aliasing={{0}: (1, {}), {1}: (2, {}), {2}: (3, {}), {3}: (4, {})} | custom-call | bytes 6291456 | tf_op jit(solution)/shard_map/unpack/pallas_call | solution.py:235
Async XLA Ops:
  2.7 15.1 %copy-start.6 = (s32[64,9]{0,1:T(8,128)S(1)}, s32[64,9]{0,1:T(8,128)}, u32[]{:S(2)}) copy-start(s32[64,9]{0,1:T(8,128)} %param.14) | copy-start | bytes 6916
  2.8 13.7 %collective-permute-start.4 = (bf16[512,768]{1,0:T(8,128)(2,1)S(1)}, bf16[512,768]{1,0:T(8,128)(2,1)}, u32[]{:S(2)}, u32[]{:S(2)}) collective-permute-start(bf16[512,768]{1,0:T(8,128)(2,1)S(1)} %broadcast_select_fusion.3), channel_id=1, source_target_pairs={{12,28},{16,0},{13,29},{17,1},{14,30},{18,2},{15,31},{19,3}} | collective-permute-start | bytes 2359304 | tf_op jit(solution)/shard_map/ppermute | solution.py:260
  6.9 28.0 %collective-permute-start.1 = (bf16[512,768]{1,0:T(8,128)(2,1)S(1)}, bf16[512,768]{1,0:T(8,128)(2,1)}, u32[]{:S(2)}, u32[]{:S(2)}) collective-permute-start(bf16[512,768]{1,0:T(8,128)(2,1)S(1)} %get-tuple-element.41), channel_id=1, source_target_pairs={{0,4},{4,8},{8,12},{16,20},{20,24},{24,28},{1,5},{5,9},{9,13},{17,... | collective-permute-start | bytes 2359304 | tf_op jit(solution)/shard_map/ppermute | solution.py:262
  8.2 27.4 %collective-permute-start.3 = (bf16[512,768]{1,0:T(8,128)(2,1)S(1)}, bf16[512,768]{1,0:T(8,128)(2,1)}, u32[]{:S(2)}, u32[]{:S(2)}) collective-permute-start(bf16[512,768]{1,0:T(8,128)(2,1)S(1)} %get-tuple-element.43), channel_id=1, source_target_pairs={{4,0},{8,4},{12,8},{20,16},{24,20},{28,24},{5,1},{9,5},{13,9},{21,... | collective-permute-start | bytes 2359304 | tf_op jit(solution)/shard_map/ppermute | solution.py:262
  12.1 22.8 %collective-permute-start = (bf16[512,768]{1,0:T(8,128)(2,1)S(1)}, bf16[512,768]{1,0:T(8,128)(2,1)}, u32[]{:S(2)}, u32[]{:S(2)}) collective-permute-start(bf16[512,768]{1,0:T(8,128)(2,1)S(1)} %get-tuple-element.40), channel_id=1, source_target_pairs={{0,4},{4,8},{8,12},{12,16},{16,20},{20,24},{24,28},{1,5},{5,9},{9,... | collective-permute-start | bytes 2359304 | tf_op jit(solution)/shard_map/ppermute | solution.py:261
  14.1 21.6 %collective-permute-start.2 = (bf16[512,768]{1,0:T(8,128)(2,1)S(1)}, bf16[512,768]{1,0:T(8,128)(2,1)}, u32[]{:S(2)}, u32[]{:S(2)}) collective-permute-start(bf16[512,768]{1,0:T(8,128)(2,1)S(1)} %get-tuple-element.42), channel_id=1, source_target_pairs={{4,0},{8,4},{12,8},{16,12},{20,16},{24,20},{28,24},{5,1},{9,5},{13... | collective-permute-start | bytes 2359304 | tf_op jit(solution)/shard_map/ppermute | solution.py:261
  16.5 19.1 %collective-permute-start.5 = (bf16[512,768]{1,0:T(8,128)(2,1)}, bf16[512,768]{1,0:T(8,128)(2,1)}, u32[]{:S(2)}, u32[]{:S(2)}) collective-permute-start(bf16[512,768]{1,0:T(8,128)(2,1)} %collective-permute-done.4), channel_id=1, source_target_pairs={{28,16},{0,12},{29,17},{1,13},{30,18},{2,14},{31,19},{3,15}} | collective-permute-start | bytes 2359304 | tf_op jit(solution)/shard_map/ppermute | solution.py:263
  27.0 85.5 %all-to-all-start = ((bf16[8,4,8,16,768]{4,3,2,1,0:T(8,128)(2,1)}), bf16[8,4,8,16,768]{4,3,2,1,0:T(8,128)(2,1)}, u32[]{:S(2)}, u32[]{:S(2)}) async-start(bf16[8,4,8,16,768]{4,3,2,1,0:T(8,128)(2,1)} %pack.1), calls=%async_computation | async-start | bytes 12582912 | tf_op jit(solution)/shard_map/all_to_all | solution.py:268
  85.3 12.1 %copy-start.8 = (bf16[512,768]{1,0:T(8,128)(2,1)S(1)}, bf16[512,768]{1,0:T(8,128)(2,1)}, u32[]{:S(2)}) copy-start(bf16[512,768]{1,0:T(8,128)(2,1)} %get-tuple-element.52) | copy-start | bytes 2359300
  85.3 14.0 %copy-start.7 = (bf16[512,768]{1,0:T(8,128)(2,1)S(1)}, bf16[512,768]{1,0:T(8,128)(2,1)}, u32[]{:S(2)}) copy-start(bf16[512,768]{1,0:T(8,128)(2,1)} %get-tuple-element.53) | copy-start | bytes 2359300
  86.6 24.6 %collective-permute-start.8 = (bf16[512,768]{1,0:T(8,128)(2,1)S(1)}, bf16[512,768]{1,0:T(8,128)(2,1)}, u32[]{:S(2)}, u32[]{:S(2)}) collective-permute-start(bf16[512,768]{1,0:T(8,128)(2,1)S(1)} %broadcast_select_fusion.2), channel_id=1, source_target_pairs={{12,28},{16,0},{13,29},{17,1},{14,30},{18,2},{15,31},{19,3}} | collective-permute-start | bytes 2359304 | tf_op jit(solution)/shard_map/ppermute | solution.py:260
  92.2 60.5 %collective-permute-start.9 = (bf16[512,768]{1,0:T(8,128)(2,1)}, bf16[512,768]{1,0:T(8,128)(2,1)}, u32[]{:S(2)}, u32[]{:S(2)}) collective-permute-start(bf16[512,768]{1,0:T(8,128)(2,1)} %get-tuple-element.55), channel_id=1, source_target_pairs={{0,4},{4,8},{8,12},{16,20},{20,24},{24,28},{1,5},{5,9},{9,13},{17,... | collective-permute-start | bytes 2359304 | tf_op jit(solution)/shard_map/ppermute | solution.py:262
  93.5 59.3 %collective-permute-start.10 = (bf16[512,768]{1,0:T(8,128)(2,1)}, bf16[512,768]{1,0:T(8,128)(2,1)}, u32[]{:S(2)}, u32[]{:S(2)}) collective-permute-start(bf16[512,768]{1,0:T(8,128)(2,1)} %get-tuple-element.54), channel_id=1, source_target_pairs={{4,0},{8,4},{12,8},{20,16},{24,20},{28,24},{5,1},{9,5},{13,9},{21,... | collective-permute-start | bytes 2359304 | tf_op jit(solution)/shard_map/ppermute | solution.py:262
  97.4 30.0 %collective-permute-start.6 = (bf16[512,768]{1,0:T(8,128)(2,1)S(1)}, bf16[512,768]{1,0:T(8,128)(2,1)S(1)}, u32[]{:S(2)}, u32[]{:S(2)}) collective-permute-start(bf16[512,768]{1,0:T(8,128)(2,1)S(1)} %copy-done.8), channel_id=1, source_target_pairs={{0,4},{4,8},{8,12},{12,16},{16,20},{20,24},{24,28},{1,5},{5,9},{9,... | collective-permute-start | bytes 2359304 | tf_op jit(solution)/shard_map/ppermute | solution.py:261
  99.3 28.1 %collective-permute-start.7 = (bf16[512,768]{1,0:T(8,128)(2,1)S(1)}, bf16[512,768]{1,0:T(8,128)(2,1)S(1)}, u32[]{:S(2)}, u32[]{:S(2)}) collective-permute-start(bf16[512,768]{1,0:T(8,128)(2,1)S(1)} %copy-done.7), channel_id=1, source_target_pairs={{4,0},{8,4},{12,8},{16,12},{20,16},{24,20},{28,24},{5,1},{9,5},{13... | collective-permute-start | bytes 2359304 | tf_op jit(solution)/shard_map/ppermute | solution.py:261
  111.3 41.5 %collective-permute-start.11 = (bf16[512,768]{1,0:T(8,128)(2,1)}, bf16[512,768]{1,0:T(8,128)(2,1)}, u32[]{:S(2)}, u32[]{:S(2)}) collective-permute-start(bf16[512,768]{1,0:T(8,128)(2,1)} %collective-permute-done.8), channel_id=1, source_target_pairs={{28,16},{0,12},{29,17},{1,13},{30,18},{2,14},{31,19},{3,15}} | collective-permute-start | bytes 2359304 | tf_op jit(solution)/shard_map/ppermute | solution.py:263
  127.4 0.9 copy-start.3
  127.4 1.1 copy-start.5
  128.6 45.5 %all-to-all-start.2 = ((bf16[8,4,8,16,384]{4,3,2,1,0:T(8,128)(2,1)}), bf16[8,4,8,16,384]{4,3,2,1,0:T(8,128)(2,1)S(1)}, u32[]{:S(2)}, u32[]{:S(2)}) async-start(bf16[8,4,8,16,384]{4,3,2,1,0:T(8,128)(2,1)} %col_heads.2.earlier), calls=%async_computation.2 | async-start | bytes 6291456 | tf_op jit(solution)/shard_map/all_to_all | solution.py:268
  174.1 1.6 copy-start
  175.7 42.3 %all-to-all-start.1 = ((bf16[8,4,8,16,384]{4,3,2,1,0:T(8,128)(2,1)}), bf16[8,4,8,16,384]{4,3,2,1,0:T(8,128)(2,1)}, u32[]{:S(2)}, u32[]{:S(2)}) async-start(bf16[8,4,8,16,384]{4,3,2,1,0:T(8,128)(2,1)} %col_heads.3), calls=%async_computation.1 | async-start | bytes 6291456 | tf_op jit(solution)/shard_map/all_to_all | solution.py:268
  181.7 2.4 %copy-start.2 = (f32[1024,768]{1,0:T(8,128)S(1)}, f32[1024,768]{1,0:T(8,128)}, u32[]{:S(2)}) copy-start(f32[1024,768]{1,0:T(8,128)} %get-tuple-element.46) | copy-start | bytes 9437188
  181.7 2.5 %copy-start.4 = (bf16[512,768]{1,0:T(8,128)(2,1)S(1)}, bf16[512,768]{1,0:T(8,128)(2,1)}, u32[]{:S(2)}) copy-start(bf16[512,768]{1,0:T(8,128)(2,1)} %copy-done.3) | copy-start | bytes 2359300
  184.2 2.8 %copy-start.1 = (f32[1024,768]{1,0:T(8,128)S(1)}, f32[1024,768]{1,0:T(8,128)}, u32[]{:S(2)}) copy-start(f32[1024,768]{1,0:T(8,128)} %get-tuple-element.58) | copy-start | bytes 9437188

commit v4 on v3

--- a/solution.py
+++ b/solution.py
@@ -1,5 +1,4 @@
 import functools
-import math
 
 import jax
 import jax.numpy as jnp
@@ -139,8 +138,10 @@
     )(place, mask, q, k, v, d, *halos)
 
 
-def col_kernel(mask, x, earlier, out, bias):
+def col_kernel(me, mask, x, earlier, *refs):
+    *outs, result, bias = refs
     del earlier
+
     @pl.when((pl.program_id(0) == 0) & (pl.program_id(1) == 0))
     def _():
         size, total = bias.shape[0], mask.shape[0]
@@ -168,51 +169,82 @@
         grad_values += more_values
         outputs.append(output)
         grads.append(grad_query)
-    out[:, 0] = jnp.concatenate(outputs, 0).reshape(shape)
-    out[:, 1] = jnp.concatenate(grads, 0).reshape(shape)
-    out[:, 2] = (grad_keys * SCALE).astype(jnp.bfloat16).reshape(shape)
-    out[:, 3] = grad_values.astype(jnp.bfloat16).reshape(shape)
-
-
-def col_attention(mask, x, earlier, start, heads):
-    n, k, rows, cols, _ = x.shape
+    result[:, 0] = jnp.concatenate(outputs, 0).reshape(shape)
+    result[:, 1] = jnp.concatenate(grads, 0).reshape(shape)
+    result[:, 2] = (grad_keys * SCALE).astype(jnp.bfloat16).reshape(shape)
+    result[:, 3] = grad_values.astype(jnp.bfloat16).reshape(shape)
+    for partner, out in enumerate(outs):
+        out[...] = result[me[0] ^ partner]
+
+
+def col_attention(me, mask, x, earlier):
+    n, k, rows, cols, feat = x.shape
+    heads = feat // HEAD_DIM
     tokens = n * rows * GROUP
-    block = (n, k, rows, GROUP, HEAD_DIM)
+    block = (k, rows, GROUP, HEAD_DIM)
     pairs = tokens * tokens * heads * (cols // GROUP)
     return pl.pallas_call(
         col_kernel,
         grid=(heads, cols // GROUP),
         in_specs=[
+            pl.BlockSpec(memory_space=pltpu.SMEM),
             pl.BlockSpec(mask.shape, lambda h, g: (0, 0)),
-            pl.BlockSpec(block, lambda h, g: (0, 0, 0, g, h + start)),
+            pl.BlockSpec((n, *block), lambda h, g: (0, 0, 0, g, h)),
             pl.BlockSpec(memory_space=pl.ANY),
         ],
-        out_specs=pl.BlockSpec(block, lambda h, g: (0, 0, 0, g, h)),
-        out_shape=jax.ShapeDtypeStruct((n, k, rows, cols, heads * HEAD_DIM), jnp.bfloat16),
-        scratch_shapes=[pltpu.VMEM((tokens, tokens), jnp.float32)],
+        out_specs=[pl.BlockSpec(block, lambda h, g: (0, 0, g, h))] * n,
+        out_shape=[jax.ShapeDtypeStruct((k, rows, cols, feat), jnp.bfloat16)] * n,
+        scratch_shapes=[
+            pltpu.VMEM((n, *block), jnp.bfloat16),
+            pltpu.VMEM((tokens, tokens), jnp.float32),
+        ],
         compiler_params=pltpu.CompilerParams(vmem_limit_bytes=VMEM),
         cost_estimate=pl.CostEstimate(
             flops=240 * pairs * HEAD_DIM, bytes_accessed=4 * x.size, transcendentals=pairs
         ),
         name="col_heads",
-    )(mask, x, earlier)
-
-
-def pack_kernel(*refs):
-    *parts, out = refs
-    for a, part in enumerate(parts):
-        out[a] = part[...]
+    )(me, mask, x, earlier)
+
+
+def pack_kernel(n, *refs):
+    *parts, out, held, arrived, left = refs
+    cols = GRIDC // n
+    loads = [
+        pltpu.make_async_copy(part, held.at[a], arrived.at[a]) for a, part in enumerate(parts)
+    ]
+    stores = [
+        [
+            pltpu.make_async_copy(
+                held.at[a, :, j * cols : (j + 1) * cols, :], out.at[j, a], left.at[a, j]
+            )
+            for j in range(n)
+        ]
+        for a in range(len(parts))
+    ]
+    for load in loads:
+        load.start()
+    for load, several in zip(loads, stores):
+        load.wait()
+        for store in several:
+            store.start()
+    for several in stores:
+        for store in several:
+            store.wait()
 
 
 def packed(arrays, n):
     tokens, feat = arrays[0].shape
     rows, cols, k = tokens // GRIDC, GRIDC // n, len(arrays)
     return pl.pallas_call(
-        pack_kernel,
-        grid=(n,),
-        in_specs=[pl.BlockSpec((rows, cols, feat), lambda j: (0, j, 0))] * k,
-        out_specs=pl.BlockSpec((None, k, rows, cols, feat), lambda j: (j, 0, 0, 0, 0)),
+        functools.partial(pack_kernel, n),
+        in_specs=[pl.BlockSpec(memory_space=pl.ANY)] * k,
+        out_specs=pl.BlockSpec(memory_space=pl.ANY),
         out_shape=jax.ShapeDtypeStruct((n, k, rows, cols, feat), jnp.bfloat16),
+        scratch_shapes=[
+            pltpu.VMEM((k, rows, GRIDC, feat), jnp.bfloat16),
+            pltpu.SemaphoreType.DMA((k,)),
+            pltpu.SemaphoreType.DMA((k, n)),
+        ],
         compiler_params=pltpu.CompilerParams(vmem_limit_bytes=VMEM),
         cost_estimate=pl.CostEstimate(
             flops=0, bytes_accessed=4 * k * tokens * feat, transcendentals=0
@@ -221,30 +253,49 @@
     )(*(a.reshape(rows, GRIDC, feat) for a in arrays))
 
 
-def unpack_kernel(x, *refs):
-    for a, part in enumerate(refs[-x.shape[0] :]):
-        part[...] = x[a]
-
-
-def unpacked(x, start, whole):
-    n, k, rows, cols, width = x.shape
-    kept = [] if isinstance(whole, int) else [a.reshape(rows, n * cols, -1) for a in whole]
-    feat = kept[0].shape[-1] if kept else whole
-    step = math.gcd(start, width) if start else width
-    spec = pl.BlockSpec((rows, cols, step), lambda j, f: (0, j, start // step + f))
+def unpack_kernel(n, me, *refs):
+    parts, outs, (held, arrived, left) = refs[:n], refs[n:-3], refs[-3:]
+    cols = GRIDC // n
+    loads, stores = [], []
+    for a, out in enumerate(outs):
+        for partner, part in enumerate(parts):
+            here = pl.ds(pl.multiple_of((me[0] ^ partner) * cols, cols), cols)
+            loads.append(
+                pltpu.make_async_copy(
+                    part.at[a], held.at[a, :, here, :], arrived.at[a, partner]
+                )
+            )
+        stores.append(pltpu.make_async_copy(held.at[a], out, left.at[a]))
+    for load in loads:
+        load.start()
+    for a, store in enumerate(stores):
+        for load in loads[a * n : (a + 1) * n]:
+            load.wait()
+        store.start()
+    for store in stores:
+        store.wait()
+
+
+def unpacked(me, parts):
+    n = len(parts)
+    k, rows, cols, feat = parts[0].shape
     outs = pl.pallas_call(
-        unpack_kernel,
-        grid=(n, width // step),
-        in_specs=[pl.BlockSpec((None, k, rows, cols, step), lambda j, f: (j, 0, 0, 0, f))]
-        + [pl.BlockSpec(memory_space=pl.ANY)] * len(kept),
-        out_specs=[spec] * k,
-        out_shape=[jax.ShapeDtypeStruct((rows, n * cols, feat), jnp.bfloat16)] * k,
-        input_output_aliases={1 + a: a for a in range(len(kept))},
+        functools.partial(unpack_kernel, n),
+        in_specs=[pl.BlockSpec(memory_space=pltpu.SMEM)] + [pl.BlockSpec(memory_space=pl.ANY)] * n,
+        out_specs=[pl.BlockSpec(memory_space=pl.ANY)] * k,
+        out_shape=[jax.ShapeDtypeStruct((rows, GRIDC, feat), jnp.bfloat16)] * k,
+        scratch_shapes=[
+            pltpu.VMEM((k, rows, GRIDC, feat), jnp.bfloat16),
+            pltpu.SemaphoreType.DMA((k, n)),
+            pltpu.SemaphoreType.DMA((k,)),
+        ],
         compiler_params=pltpu.CompilerParams(vmem_limit_bytes=VMEM),
-        cost_estimate=pl.CostEstimate(flops=0, bytes_accessed=4 * x.size, transcendentals=0),
+        cost_estimate=pl.CostEstimate(
+            flops=0, bytes_accessed=4 * k * rows * GRIDC * feat, transcendentals=0
+        ),
         name="unpack",
-    )(x, *kept)
-    return [o.reshape(rows * n * cols, feat) for o in outs]
+    )(me, *parts)
+    return [o.reshape(rows * GRIDC, feat) for o in outs]
 
 
 def swapped(lo_k, lo_v, hi_k, hi_v):
@@ -290,18 +341,16 @@
     row_output, row_dquery, own_k, own_v, *sides = row_attention(
         place, row_mask, row_query, row_key, row_value, row_cotangent, halos, band
     )
-    (k_before, v_before, k_after, v_after, far_v), hop = swapped(*sides)
-
-    feat = col_query.shape[1]
-    heads = feat // HEAD_DIM
-    half = heads // 2
-    first = col_attention(col_mask, moved, row_output, 0, half)
-    first, k_before, k_after, hop = lax.optimization_barrier((first, k_before, k_after, hop))
-    second = col_attention(col_mask, moved, first, half, heads - half)
-    second, v_before, v_after, far_v = lax.optimization_barrier((second, v_before, v_after, far_v))
-    first, second = exchanged(first), exchanged(second)
-    col_results = unpacked(second, half * HEAD_DIM, unpacked(first, 0, feat))
-
+    halos, _ = swapped(*sides)
+
+    results = col_attention(me.reshape(1), col_mask, moved, row_output)
+    results, halos = lax.optimization_barrier((results, halos))
+    returned = [results[0]] + [
+        lax.ppermute(results[k], "ctx", [(i, i ^ k) for i in range(n)]) for k in range(1, n)
+    ]
+    col_results = unpacked(me.reshape(1), returned)
+
+    k_before, v_before, k_after, v_after, far_v = halos
     v_before = jnp.where(me % CHIPS_APART == 0, far_v, v_before)
     v_after = jnp.where(me % CHIPS_APART == CHIPS_APART - 1, far_v, v_after)
     row_grads = []

time: 228 us -> 226 us (level); the launches traced: 224 us -> 225 us
  waiting for transfers between devices: 55.1 us -> 66.3 us
  Pallas kernels: 99.5 us -> 88.7 us
  starting transfers between devices: 54.3 us -> 58.2 us
  local copies, waits for them, and re-layouts: 6.44 us -> 3.76 us
    ppermute x0 -> x7, waiting for transfers between devices: none -> 59.8 us  [body(): lax.ppermute(results[k], 'ctx', [(i, i ^ k) for i in range(n)])]
    all_to_all x3 -> x1, waiting for transfers between devices: 44.8 us -> 0.01 us  [exchanged(): return lax.all_to_all(x, 'ctx', 0, 0, tiled=True)]
    all_to_all x3 -> x1, starting transfers between devices: 23.1 us -> 7.92 us  [exchanged(): return lax.all_to_all(x, 'ctx', 0, 0, tiled=True)]
    ppermute x0 -> x7, starting transfers between devices: none -> 13.8 us  [body(): lax.ppermute(results[k], 'ctx', [(i, i ^ k) for i in range(n)])]
    pallas_call x3 -> x2, Pallas kernels: 20.1 us -> 11.1 us  [the longest x1 5.61 us: unpacked(): pl.pallas_call(functools.partial(unpack_kernel, n), in_specs=[pl.BlockSpe...]
    ppermute x2, waiting for transfers between devices: 9.53 us -> 5.31 us  [swapped(): hop = lax.ppermute(jnp.where(side == 0, lo_v, hi_v), 'ctx', first)]
    ppermute x2, starting transfers between devices: 3.82 us -> 7.86 us  [swapped(): lax.ppermute(hi_k, 'ctx', up)]
    unnamed x19 -> x15, local copies, waits for them, and re-layouts: 4.39 us -> 1.71 us
  transfers between devices with their start and end apart: 15 -> 20, of which waited for: 4 -> 5; matrix products, arithmetic and copies ran while one was open for 4% -> 3% of each run, Pallas kernels for 42% -> 37%
where the time goes in v4:
time: 226 us; the launch traced here: 225 us
  Pallas kernels  88.7 us (39%)
  waiting for transfers between devices  66.3 us (29%)
  starting transfers between devices  58.2 us (26%)
  other arithmetic  6.5 us (3%)
  local copies, waits for them, and re-layouts  3.76 us (2%)
    ppermute x7, waiting for transfers between devices, body(): lax.ppermute(results[k], 'ctx', [(i, i ^ k) for i in range(n)])  59.8 us
    pallas_call x1, Pallas kernels, row_attention(): pl.pallas_call(functools.partial(row_kernel, band), grid=(heads,), in_spe...  49.7 us
    pallas_call x1, Pallas kernels, col_attention(): pl.pallas_call(col_kernel, grid=(heads, cols // GROUP), in_specs=[pl.Bloc...  28 us
    ppermute x7, starting transfers between devices, body(): lax.ppermute(results[k], 'ctx', [(i, i ^ k) for i in range(n)])  13.8 us
    ppermute x2, starting transfers between devices, swapped(): hop = lax.ppermute(jnp.where(side == 0, lo_v, hi_v), 'ctx', first)  9.85 us
    ppermute x2, starting transfers between devices, swapped(): lax.ppermute(lo_v, 'ctx', near_down)  9.58 us
    all_to_all x1, starting transfers between devices, exchanged(): return lax.all_to_all(x, 'ctx', 0, 0, tiled=True)  7.92 us
    ppermute x2, starting transfers between devices, swapped(): lax.ppermute(hi_k, 'ctx', up)  7.86 us
  transfers between devices with their start and end apart: 20, of which 5 were waited for; matrix products, arithmetic and copies ran while one was open for 3% of the time, Pallas kernels for 37%

profile of v4, /device:TPU:11, one launch (start us, length us, event | category | flops | bytes accessed | tf_op | source)
XLA Modules:
  0.0 224.5 jit_solution(16482197665491418928)
XLA Ops:
  0.6 2.1 fusion
  2.7 0.0 copy-start.6
  2.7 0.1 broadcast_select_fusion.3
  2.8 4.1 %collective-permute-start.4 = (bf16[512,768]{1,0:T(8,128)(2,1)S(1)}, bf16[512,768]{1,0:T(8,128)(2,1)}, u32[]{:S(2)}, u32[]{:S(2)}) collective-permute-start(bf16[512,768]{1,0:T(8,128)(2,1)S(1)} %broadcast_select_fusion.3), channel_id=1, source_target_pairs={{12,28},{16,0},{13,29},{17,1},{14,30},{18,2},{15,31},{19,3}} | collective-permute-start | bytes 2359304 | tf_op jit(solution)/shard_map/ppermute | solution.py:311
  6.9 1.3 collective-permute-start.1
  8.2 3.8 %collective-permute-start = (bf16[512,768]{1,0:T(8,128)(2,1)S(1)}, bf16[512,768]{1,0:T(8,128)(2,1)}, u32[]{:S(2)}, u32[]{:S(2)}) collective-permute-start(bf16[512,768]{1,0:T(8,128)(2,1)S(1)} %get-tuple-element.50), channel_id=1, source_target_pairs={{0,4},{4,8},{8,12},{12,16},{16,20},{20,24},{24,28},{1,5},{5,9},{9,... | collective-permute-start | bytes 2359304 | tf_op jit(solution)/shard_map/ppermute | solution.py:312
  12.0 1.9 collective-permute-start.2
  13.9 3.8 %collective-permute-start.3 = (bf16[512,768]{1,0:T(8,128)(2,1)S(1)}, bf16[512,768]{1,0:T(8,128)(2,1)}, u32[]{:S(2)}, u32[]{:S(2)}) collective-permute-start(bf16[512,768]{1,0:T(8,128)(2,1)S(1)} %get-tuple-element.53), channel_id=1, source_target_pairs={{4,0},{8,4},{12,8},{20,16},{24,20},{28,24},{5,1},{9,5},{13,9},{21,... | collective-permute-start | bytes 2359304 | tf_op jit(solution)/shard_map/ppermute | solution.py:313
  17.7 0.0 collective-permute-done.4
  17.7 1.3 collective-permute-start.5
  19.0 0.0 copy-done.6
  19.0 0.7 copy.18.mask
  19.7 5.5 %pack.1 = bf16[8,4,8,16,768]{4,3,2,1,0:T(8,128)(2,1)} custom-call(bf16[8,128,768]{2,1,0:T(8,128)(2,1)} %bitcast.11, bf16[8,128,768]{2,1,0:T(8,128)(2,1)} %bitcast.12, bf16[8,128,768]{2,1,0:T(8,128)(2,1)} %bitcast.13, bf16[8,128,768]{2,1,0:T(8,128)(2,1)} %bitcast.14), custom_call_target="tpu_custom_call" | custom-call | bytes 12582912 | tf_op jit(solution)/shard_map/pack/pallas_call | solution.py:238
  25.2 0.6 pad_add_fusion.place
  25.8 7.9 %all-to-all-start = ((bf16[8,4,8,16,768]{4,3,2,1,0:T(8,128)(2,1)}), bf16[8,4,8,16,768]{4,3,2,1,0:T(8,128)(2,1)}, u32[]{:S(2)}, u32[]{:S(2)}) async-start(bf16[8,4,8,16,768]{4,3,2,1,0:T(8,128)(2,1)} %pack.1), calls=%async_computation | async-start | bytes 12582912 | tf_op jit(solution)/shard_map/all_to_all | solution.py:319
  33.7 0.0 collective-permute-done.k_lo
  33.7 1.1 collective-permute-done.2.k_hi
  34.8 0.0 collective-permute-done.1.v_lo
  34.8 0.0 collective-permute-done.3.v_hi
  34.8 0.0 collective-permute-done.5.v_far
  34.8 49.7 %row_heads.1 = (bf16[1024,768]{1,0:T(8,128)(2,1)}, bf16[1024,768]{1,0:T(8,128)(2,1)}, f32[1024,768]{1,0:T(8,128)}, f32[1024,768]{1,0:T(8,128)}, bf16[512,768]{1,...) custom-call(s32[2]{0:T(128)} %pad_add_fusion.place, ...), custom_call_target="tpu_custom_call" | custom-call | flops 241591910400 | bytes 23592960 | tf_op jit(solution)/shard_map/row_heads/pallas_call | solution.py:115
  84.5 0.0 copy-start.5
  84.5 0.0 copy-start.4
  84.5 1.3 broadcast_select_fusion.2
  85.9 5.8 %collective-permute-start.10 = (bf16[512,768]{1,0:T(8,128)(2,1)S(1)}, bf16[512,768]{1,0:T(8,128)(2,1)}, u32[]{:S(2)}, u32[]{:S(2)}) collective-permute-start(bf16[512,768]{1,0:T(8,128)(2,1)S(1)} %broadcast_select_fusion.2), channel_id=1, source_target_pairs={{12,28},{16,0},{13,29},{17,1},{14,30},{18,2},{15,31},{19,3}} | collective-permute-start | bytes 2359304 | tf_op jit(solution)/shard_map/ppermute | solution.py:311
  91.6 0.0 copy-done.5
  91.6 1.3 collective-permute-start.7
  92.9 0.0 copy-done.4
  92.9 5.8 %collective-permute-start.9 = (bf16[512,768]{1,0:T(8,128)(2,1)S(1)}, bf16[512,768]{1,0:T(8,128)(2,1)}, u32[]{:S(2)}, u32[]{:S(2)}) collective-permute-start(bf16[512,768]{1,0:T(8,128)(2,1)S(1)} %copy-done.4), channel_id=1, source_target_pairs={{4,0},{8,4},{12,8},{20,16},{24,20},{28,24},{5,1},{9,5},{13,9},{21,... | collective-permute-start | bytes 2359304 | tf_op jit(solution)/shard_map/ppermute | solution.py:313
  98.8 4.0 %collective-permute-start.6 = (bf16[512,768]{1,0:T(8,128)(2,1)}, bf16[512,768]{1,0:T(8,128)(2,1)S(1)}, u32[]{:S(2)}, u32[]{:S(2)}) collective-permute-start(bf16[512,768]{1,0:T(8,128)(2,1)} %get-tuple-element.70), channel_id=1, source_target_pairs={{0,4},{4,8},{8,12},{12,16},{16,20},{20,24},{24,28},{1,5},{5,9},{9,... | collective-permute-start | bytes 2359304 | tf_op jit(solution)/shard_map/ppermute | solution.py:312
  102.8 1.9 collective-permute-start.8
  104.7 5.3 %collective-permute-done.10 = bf16[512,768]{1,0:T(8,128)(2,1)} collective-permute-done((bf16[512,768]{1,0:T(8,128)(2,1)S(1)}, bf16[512,768]{1,0:T(8,128)(2,1)}, u32[]{:S(2)}, u32[]{:S(2)}) %collective-permute-start.10) | collective-permute-done | bytes 786464 | tf_op jit(solution)/shard_map/ppermute | solution.py:311
  110.0 1.5 collective-permute-start.11
  111.5 0.0 all-to-all-done.x
  111.5 28.0 %col_heads.1 = (bf16[4,8,16,768]{3,2,1,0:T(8,128)(2,1)}, bf16[4,8,16,768]{3,2,1,0:T(8,128)(2,1)}, bf16[4,8,16,768]{3,2,1,0:T(8,128)(2,1)}, bf16[4,8,16,768]{3,2,...) custom-call(s32[1]{0:T(128)} %bitcast.2.me, ...), custom_call_target="tpu_custom_call" | custom-call | flops 96636764160 | bytes 12582912 | tf_op jit(solution)/shard_map/col_heads/pallas_call | solution.py:186
  139.5 0.0 collective-permute-done.6
  139.5 0.0 collective-permute-done.8
  139.5 0.0 collective-permute-done.7
  139.6 0.0 collective-permute-done.9
  139.6 0.0 collective-permute-done.11
  139.6 0.1 collective-permute-start.12
  139.7 8.6 %collective-permute-start.13 = (bf16[4,8,16,768]{3,2,1,0:T(8,128)(2,1)}, bf16[4,8,16,768]{3,2,1,0:T(8,128)(2,1)S(1)}, u32[]{:S(2)}, u32[]{:S(2)}) collective-permute-start(bf16[4,8,16,768]{3,2,1,0:T(8,128)(2,1)} %get-tuple-element.82), channel_id=1, source_target_pairs={{0,8},{4,12},{8,0},{12,4},{16,24},{20,28},{24,16},{28,20},{1,9},{5... | collective-permute-start | bytes 2359304 | tf_op jit(solution)/shard_map/ppermute | solution.py:349
  148.3 0.0 copy-start.1
  148.3 0.1 collective-permute-start.14
  148.3 1.7 collective-permute-start.15
  150.0 0.3 collective-permute-start.16
  150.3 0.0 collective-permute-done.12.refs_1_
  150.3 1.2 collective-permute-start.17
  151.5 14.9 %collective-permute-done.13.refs_2_ = bf16[4,8,16,768]{3,2,1,0:T(8,128)(2,1)S(1)} collective-permute-done((bf16[4,8,16,768]{3,2,1,0:T(8,128)(2,1)}, bf16[4,8,16,768]{3,2,1,0:T(8,128)(2,1)S(1)}, u32[]{:S(2)}, u32[]{:S(2)}) %collective-permute-start.13) | collective-permute-done | bytes 786464 | tf_op jit(solution)/shard_map/ppermute | solution.py:349
  166.4 1.9 collective-permute-start.18
  168.3 1.5 broadcast_select_fusion.1
  169.8 0.0 copy-done.2
  169.8 0.0 copy-done.3
  169.8 0.0 copy-done.1
  169.8 0.0 copy-start
  169.9 1.5 add_convert_fusion.1
  171.3 1.0 copy-done
  172.3 1.5 add_convert_fusion
  173.8 10.0 %collective-permute-done.14.refs_3_ = bf16[4,8,16,768]{3,2,1,0:T(8,128)(2,1)} collective-permute-done((bf16[4,8,16,768]{3,2,1,0:T(8,128)(2,1)}, bf16[4,8,16,768]{3,2,1,0:T(8,128)(2,1)}, u32[]{:S(2)}, u32[]{:S(2)}) %collective-permute-start.14) | collective-permute-done | bytes 786464 | tf_op jit(solution)/shard_map/ppermute | solution.py:349
  183.8 0.0 collective-permute-done.15.refs_4_
  183.8 34.9 %collective-permute-done.16.refs_5_ = bf16[4,8,16,768]{3,2,1,0:T(8,128)(2,1)} collective-permute-done((bf16[4,8,16,768]{3,2,1,0:T(8,128)(2,1)}, bf16[4,8,16,768]{3,2,1,0:T(8,128)(2,1)}, u32[]{:S(2)}, u32[]{:S(2)}) %collective-permute-start.16) | collective-permute-done | bytes 786464 | tf_op jit(solution)/shard_map/ppermute | solution.py:349
  218.7 0.0 collective-permute-done.17.refs_6_
  218.7 0.0 collective-permute-done.18.refs_7_
  218.7 5.6 %unpack.1 = (bf16[8,128,768]{2,1,0:T(8,128)(2,1)}, bf16[8,128,768]{2,1,0:T(8,128)(2,1)}, bf16[8,128,768]{2,1,0:T(8,128)(2,1)}, bf16[8,128,768]{2,1,0:T(8,128)(2,1)}) custom-call(s32[1]{0:T(128)} %bitcast.2.me, bf16[4,8,16,768]{3,2,1,0:T(8,128)(2,1)} %get-tuple-element.80.refs_0_, bf16[4,8,16,768]{3,2,1,0:T(8,128)(2,1)} %copy-done.2, ...), custom_call_target="tpu_custom_call" | custom-call | bytes 12582912 | tf_op jit(solution)/shard_map/unpack/pallas_call | solution.py:282
  (2 shorter events, 0.0 us)
Async XLA Ops:
  2.7 16.3 %copy-start.6 = (s32[64,9]{0,1:T(8,128)S(1)}, s32[64,9]{0,1:T(8,128)}, u32[]{:S(2)}) copy-start(s32[64,9]{0,1:T(8,128)} %param.14) | copy-start | bytes 6916
  2.8 14.9 %collective-permute-start.4 = (bf16[512,768]{1,0:T(8,128)(2,1)S(1)}, bf16[512,768]{1,0:T(8,128)(2,1)}, u32[]{:S(2)}, u32[]{:S(2)}) collective-permute-start(bf16[512,768]{1,0:T(8,128)(2,1)S(1)} %broadcast_select_fusion.3), channel_id=1, source_target_pairs={{12,28},{16,0},{13,29},{17,1},{14,30},{18,2},{15,31},{19,3}} | collective-permute-start | bytes 2359304 | tf_op jit(solution)/shard_map/ppermute | solution.py:311
  6.9 27.9 %collective-permute-start.1 = (bf16[512,768]{1,0:T(8,128)(2,1)S(1)}, bf16[512,768]{1,0:T(8,128)(2,1)}, u32[]{:S(2)}, u32[]{:S(2)}) collective-permute-start(bf16[512,768]{1,0:T(8,128)(2,1)S(1)} %get-tuple-element.51), channel_id=1, source_target_pairs={{0,4},{4,8},{8,12},{16,20},{20,24},{24,28},{1,5},{5,9},{9,13},{17,... | collective-permute-start | bytes 2359304 | tf_op jit(solution)/shard_map/ppermute | solution.py:313
  8.2 25.5 %collective-permute-start = (bf16[512,768]{1,0:T(8,128)(2,1)S(1)}, bf16[512,768]{1,0:T(8,128)(2,1)}, u32[]{:S(2)}, u32[]{:S(2)}) collective-permute-start(bf16[512,768]{1,0:T(8,128)(2,1)S(1)} %get-tuple-element.50), channel_id=1, source_target_pairs={{0,4},{4,8},{8,12},{12,16},{16,20},{20,24},{24,28},{1,5},{5,9},{9,... | collective-permute-start | bytes 2359304 | tf_op jit(solution)/shard_map/ppermute | solution.py:312
  12.0 22.8 %collective-permute-start.2 = (bf16[512,768]{1,0:T(8,128)(2,1)S(1)}, bf16[512,768]{1,0:T(8,128)(2,1)}, u32[]{:S(2)}, u32[]{:S(2)}) collective-permute-start(bf16[512,768]{1,0:T(8,128)(2,1)S(1)} %get-tuple-element.52), channel_id=1, source_target_pairs={{4,0},{8,4},{12,8},{16,12},{20,16},{24,20},{28,24},{5,1},{9,5},{13... | collective-permute-start | bytes 2359304 | tf_op jit(solution)/shard_map/ppermute | solution.py:312
  13.9 20.9 %collective-permute-start.3 = (bf16[512,768]{1,0:T(8,128)(2,1)S(1)}, bf16[512,768]{1,0:T(8,128)(2,1)}, u32[]{:S(2)}, u32[]{:S(2)}) collective-permute-start(bf16[512,768]{1,0:T(8,128)(2,1)S(1)} %get-tuple-element.53), channel_id=1, source_target_pairs={{4,0},{8,4},{12,8},{20,16},{24,20},{28,24},{5,1},{9,5},{13,9},{21,... | collective-permute-start | bytes 2359304 | tf_op jit(solution)/shard_map/ppermute | solution.py:313
  17.7 17.1 %collective-permute-start.5 = (bf16[512,768]{1,0:T(8,128)(2,1)}, bf16[512,768]{1,0:T(8,128)(2,1)}, u32[]{:S(2)}, u32[]{:S(2)}) collective-permute-start(bf16[512,768]{1,0:T(8,128)(2,1)} %collective-permute-done.4), channel_id=1, source_target_pairs={{28,16},{0,12},{29,17},{1,13},{30,18},{2,14},{31,19},{3,15}} | collective-permute-start | bytes 2359304 | tf_op jit(solution)/shard_map/ppermute | solution.py:314
  25.8 85.7 %all-to-all-start = ((bf16[8,4,8,16,768]{4,3,2,1,0:T(8,128)(2,1)}), bf16[8,4,8,16,768]{4,3,2,1,0:T(8,128)(2,1)}, u32[]{:S(2)}, u32[]{:S(2)}) async-start(bf16[8,4,8,16,768]{4,3,2,1,0:T(8,128)(2,1)} %pack.1), calls=%async_computation | async-start | bytes 12582912 | tf_op jit(solution)/shard_map/all_to_all | solution.py:319
  84.5 7.1 %copy-start.5 = (bf16[512,768]{1,0:T(8,128)(2,1)S(1)}, bf16[512,768]{1,0:T(8,128)(2,1)}, u32[]{:S(2)}) copy-start(bf16[512,768]{1,0:T(8,128)(2,1)} %get-tuple-element.71) | copy-start | bytes 2359300
  84.5 8.4 %copy-start.4 = (bf16[512,768]{1,0:T(8,128)(2,1)S(1)}, bf16[512,768]{1,0:T(8,128)(2,1)}, u32[]{:S(2)}) copy-start(bf16[512,768]{1,0:T(8,128)(2,1)} %get-tuple-element.73) | copy-start | bytes 2359300
  85.9 24.2 %collective-permute-start.10 = (bf16[512,768]{1,0:T(8,128)(2,1)S(1)}, bf16[512,768]{1,0:T(8,128)(2,1)}, u32[]{:S(2)}, u32[]{:S(2)}) collective-permute-start(bf16[512,768]{1,0:T(8,128)(2,1)S(1)} %broadcast_select_fusion.2), channel_id=1, source_target_pairs={{12,28},{16,0},{13,29},{17,1},{14,30},{18,2},{15,31},{19,3}} | collective-permute-start | bytes 2359304 | tf_op jit(solution)/shard_map/ppermute | solution.py:311
  91.6 47.9 %collective-permute-start.7 = (bf16[512,768]{1,0:T(8,128)(2,1)S(1)}, bf16[512,768]{1,0:T(8,128)(2,1)}, u32[]{:S(2)}, u32[]{:S(2)}) collective-permute-start(bf16[512,768]{1,0:T(8,128)(2,1)S(1)} %copy-done.5), channel_id=1, source_target_pairs={{0,4},{4,8},{8,12},{16,20},{20,24},{24,28},{1,5},{5,9},{9,13},{17,... | collective-permute-start | bytes 2359304 | tf_op jit(solution)/shard_map/ppermute | solution.py:313
  92.9 46.6 %collective-permute-start.9 = (bf16[512,768]{1,0:T(8,128)(2,1)S(1)}, bf16[512,768]{1,0:T(8,128)(2,1)}, u32[]{:S(2)}, u32[]{:S(2)}) collective-permute-start(bf16[512,768]{1,0:T(8,128)(2,1)S(1)} %copy-done.4), channel_id=1, source_target_pairs={{4,0},{8,4},{12,8},{20,16},{24,20},{28,24},{5,1},{9,5},{13,9},{21,... | collective-permute-start | bytes 2359304 | tf_op jit(solution)/shard_map/ppermute | solution.py:313
  98.8 40.7 %collective-permute-start.6 = (bf16[512,768]{1,0:T(8,128)(2,1)}, bf16[512,768]{1,0:T(8,128)(2,1)S(1)}, u32[]{:S(2)}, u32[]{:S(2)}) collective-permute-start(bf16[512,768]{1,0:T(8,128)(2,1)} %get-tuple-element.70), channel_id=1, source_target_pairs={{0,4},{4,8},{8,12},{12,16},{16,20},{20,24},{24,28},{1,5},{5,9},{9,... | collective-permute-start | bytes 2359304 | tf_op jit(solution)/shard_map/ppermute | solution.py:312
  102.8 36.7 %collective-permute-start.8 = (bf16[512,768]{1,0:T(8,128)(2,1)}, bf16[512,768]{1,0:T(8,128)(2,1)S(1)}, u32[]{:S(2)}, u32[]{:S(2)}) collective-permute-start(bf16[512,768]{1,0:T(8,128)(2,1)} %get-tuple-element.72), channel_id=1, source_target_pairs={{4,0},{8,4},{12,8},{16,12},{20,16},{24,20},{28,24},{5,1},{9,5},{13... | collective-permute-start | bytes 2359304 | tf_op jit(solution)/shard_map/ppermute | solution.py:312
  110.0 29.5 %collective-permute-start.11 = (bf16[512,768]{1,0:T(8,128)(2,1)}, bf16[512,768]{1,0:T(8,128)(2,1)}, u32[]{:S(2)}, u32[]{:S(2)}) collective-permute-start(bf16[512,768]{1,0:T(8,128)(2,1)} %collective-permute-done.10), channel_id=1, source_target_pairs={{28,16},{0,12},{29,17},{1,13},{30,18},{2,14},{31,19},{3,15}} | collective-permute-start | bytes 2359304 | tf_op jit(solution)/shard_map/ppermute | solution.py:314
  139.6 10.7 %collective-permute-start.12 = (bf16[4,8,16,768]{3,2,1,0:T(8,128)(2,1)}, bf16[4,8,16,768]{3,2,1,0:T(8,128)(2,1)S(1)}, u32[]{:S(2)}, u32[]{:S(2)}) collective-permute-start(bf16[4,8,16,768]{3,2,1,0:T(8,128)(2,1)} %get-tuple-element.81), channel_id=1, source_target_pairs={{0,4},{4,0},{8,12},{12,8},{16,20},{20,16},{24,28},{28,24},{1,5},{5... | collective-permute-start | bytes 2359304 | tf_op jit(solution)/shard_map/ppermute | solution.py:349
  139.7 26.7 %collective-permute-start.13 = (bf16[4,8,16,768]{3,2,1,0:T(8,128)(2,1)}, bf16[4,8,16,768]{3,2,1,0:T(8,128)(2,1)S(1)}, u32[]{:S(2)}, u32[]{:S(2)}) collective-permute-start(bf16[4,8,16,768]{3,2,1,0:T(8,128)(2,1)} %get-tuple-element.82), channel_id=1, source_target_pairs={{0,8},{4,12},{8,0},{12,4},{16,24},{20,28},{24,16},{28,20},{1,9},{5... | collective-permute-start | bytes 2359304 | tf_op jit(solution)/shard_map/ppermute | solution.py:349
  148.3 21.6 %copy-start.1 = (f32[1024,768]{1,0:T(8,128)S(1)}, f32[1024,768]{1,0:T(8,128)}, u32[]{:S(2)}) copy-start(f32[1024,768]{1,0:T(8,128)} %get-tuple-element.56) | copy-start | bytes 9437188
  148.3 35.5 %collective-permute-start.14 = (bf16[4,8,16,768]{3,2,1,0:T(8,128)(2,1)}, bf16[4,8,16,768]{3,2,1,0:T(8,128)(2,1)}, u32[]{:S(2)}, u32[]{:S(2)}) collective-permute-start(bf16[4,8,16,768]{3,2,1,0:T(8,128)(2,1)} %get-tuple-element.83), channel_id=1, source_target_pairs={{0,12},{4,8},{8,4},{12,0},{16,28},{20,24},{24,20},{28,16},{1,13},{... | collective-permute-start | bytes 2359304 | tf_op jit(solution)/shard_map/ppermute | solution.py:349
  148.3 35.5 %collective-permute-start.15 = (bf16[4,8,16,768]{3,2,1,0:T(8,128)(2,1)}, bf16[4,8,16,768]{3,2,1,0:T(8,128)(2,1)}, u32[]{:S(2)}, u32[]{:S(2)}) collective-permute-start(bf16[4,8,16,768]{3,2,1,0:T(8,128)(2,1)} %get-tuple-element.84), channel_id=1, source_target_pairs={{0,16},{4,20},{8,24},{12,28},{16,0},{20,4},{24,8},{28,12},{1,17},{... | collective-permute-start | bytes 2359304 | tf_op jit(solution)/shard_map/ppermute | solution.py:349
  150.0 68.7 %collective-permute-start.16 = (bf16[4,8,16,768]{3,2,1,0:T(8,128)(2,1)}, bf16[4,8,16,768]{3,2,1,0:T(8,128)(2,1)}, u32[]{:S(2)}, u32[]{:S(2)}) collective-permute-start(bf16[4,8,16,768]{3,2,1,0:T(8,128)(2,1)} %get-tuple-element.85), channel_id=1, source_target_pairs={{0,20},{4,16},{8,28},{12,24},{16,4},{20,0},{24,12},{28,8},{1,21},{... | collective-permute-start | bytes 2359304 | tf_op jit(solution)/shard_map/ppermute | solution.py:349
  150.3 19.5 %copy-start.2 = (bf16[4,8,16,768]{3,2,1,0:T(8,128)(2,1)}, bf16[4,8,16,768]{3,2,1,0:T(8,128)(2,1)S(1)}, u32[]{:S(2)}) copy-start(bf16[4,8,16,768]{3,2,1,0:T(8,128)(2,1)S(1)} %collective-permute-done.12.refs_1_) | copy-start | bytes 2359300
  150.3 68.4 %collective-permute-start.17 = (bf16[4,8,16,768]{3,2,1,0:T(8,128)(2,1)}, bf16[4,8,16,768]{3,2,1,0:T(8,128)(2,1)}, u32[]{:S(2)}, u32[]{:S(2)}) collective-permute-start(bf16[4,8,16,768]{3,2,1,0:T(8,128)(2,1)} %get-tuple-element.86), channel_id=1, source_target_pairs={{0,24},{4,28},{8,16},{12,20},{16,8},{20,12},{24,0},{28,4},{1,25},{... | collective-permute-start | bytes 2359304 | tf_op jit(solution)/shard_map/ppermute | solution.py:349
  166.4 3.4 %copy-start.3 = (bf16[4,8,16,768]{3,2,1,0:T(8,128)(2,1)}, bf16[4,8,16,768]{3,2,1,0:T(8,128)(2,1)S(1)}, u32[]{:S(2)}) copy-start(bf16[4,8,16,768]{3,2,1,0:T(8,128)(2,1)S(1)} %collective-permute-done.13.refs_2_) | copy-start | bytes 2359300
  166.4 52.3 %collective-permute-start.18 = (bf16[4,8,16,768]{3,2,1,0:T(8,128)(2,1)}, bf16[4,8,16,768]{3,2,1,0:T(8,128)(2,1)}, u32[]{:S(2)}, u32[]{:S(2)}) collective-permute-start(bf16[4,8,16,768]{3,2,1,0:T(8,128)(2,1)} %get-tuple-element.87), channel_id=1, source_target_pairs={{0,28},{4,24},{8,20},{12,16},{16,12},{20,8},{24,4},{28,0},{1,29},{... | collective-permute-start | bytes 2359304 | tf_op jit(solution)/shard_map/ppermute | solution.py:349
  169.8 2.5 %copy-start = (f32[1024,768]{1,0:T(8,128)S(1)}, f32[1024,768]{1,0:T(8,128)}, u32[]{:S(2)}) copy-start(f32[1024,768]{1,0:T(8,128)} %get-tuple-element.76) | copy-start | bytes 9437188

commit v5 on v4

--- a/solution.py
+++ b/solution.py
@@ -43,23 +43,27 @@
 
 
 def row_kernel(
-    band, place, mask, q, k, v, d, k_lo, v_lo, k_hi, v_hi, v_far,
-    out, dq, dk, dv, lo_k, lo_v, hi_k, hi_v, keys, values, acc_k, acc_v,
+    band, place, mask, q, k, v, d, inner_kv, outer_k, outer_v, far_v,
+    out, dq, dk, dv, inner_grads, outer_dk, outer_dv, keys, values, acc_k, acc_v,
 ):
     tokens = q.shape[0]
-    rim = k_lo.shape[0]
-    for whole, before, own, after in ((keys, k_lo, k, k_hi), (values, v_lo, v, v_hi)):
-        whole[:rim] = before[...]
-        whole[rim : rim + tokens] = own[...]
-        whole[rim + tokens :] = after[...]
-
-    @pl.when(place[1] == 0)
+    rim = outer_k.shape[0]
+    odd_device = place[1]
+    inner = pl.ds(pl.multiple_of((1 - odd_device) * (rim + tokens), GRIDC), rim)
+    outer = pl.ds(pl.multiple_of(odd_device * (rim + tokens), GRIDC), rim)
+    keys[rim : rim + tokens] = k[...]
+    values[rim : rim + tokens] = v[...]
+    keys[inner] = inner_kv[0]
+    values[inner] = inner_kv[1]
+    keys[outer] = outer_k[...]
+
+    @pl.when(place[2] == 0)
     def _():
-        values[:rim] = v_far[...]
-
-    @pl.when(place[1] == CHIPS_APART - 1)
+        values[outer] = outer_v[...]
+
+    @pl.when(place[2] == 1)
     def _():
-        values[rim + tokens :] = v_far[...]
+        values[outer] = far_v[...]
 
     acc_k[...] = jnp.zeros_like(acc_k)
     acc_v[...] = jnp.zeros_like(acc_v)
@@ -97,10 +101,11 @@
         dq[here] = grad_query
         acc_k[window] += grad_keys
         acc_v[window] += grad_values
-    for acc, own, lo, hi, factor in ((acc_k, dk, lo_k, hi_k, SCALE), (acc_v, dv, lo_v, hi_v, 1.0)):
+    sides = ((acc_k, dk, outer_dk, SCALE), (acc_v, dv, outer_dv, 1.0))
+    for at, (acc, own, across, factor) in enumerate(sides):
         own[...] = acc[rim : rim + tokens] * factor
-        lo[...] = (acc[:rim] * factor).astype(lo.dtype)
-        hi[...] = (acc[rim + tokens :] * factor).astype(hi.dtype)
+        inner_grads[at] = (acc[inner] * factor).astype(across.dtype)
+        across[...] = (acc[outer] * factor).astype(across.dtype)
 
 
 def row_attention(place, mask, q, k, v, d, halos, band):
@@ -109,21 +114,24 @@
     rim = band * GRIDC
     tall = pl.BlockSpec((tokens, HEAD_DIM), lambda h: (0, h))
     edge = pl.BlockSpec((rim, HEAD_DIM), lambda h: (0, h))
+    both = pl.BlockSpec((2, rim, HEAD_DIM), lambda h: (0, 0, h))
     scalars = pl.BlockSpec(memory_space=pltpu.SMEM)
     padded = tokens + 2 * rim
     pairs = tokens * (2 * band + 2) * GRIDC * heads
     return pl.pallas_call(
         functools.partial(row_kernel, band),
         grid=(heads,),
-        in_specs=[scalars, scalars, tall, tall, tall, tall] + [edge] * 5,
-        out_specs=[tall] * 4 + [edge] * 4,
+        in_specs=[scalars, scalars, tall, tall, tall, tall, both, edge, edge, edge],
+        out_specs=[tall] * 4 + [both, edge, edge],
         out_shape=[
             jax.ShapeDtypeStruct(q.shape, jnp.bfloat16),
             jax.ShapeDtypeStruct(q.shape, jnp.bfloat16),
             jax.ShapeDtypeStruct(q.shape, jnp.float32),
             jax.ShapeDtypeStruct(q.shape, jnp.float32),
-        ]
-        + [jax.ShapeDtypeStruct((rim, feat), jnp.bfloat16)] * 4,
+            jax.ShapeDtypeStruct((2, rim, feat), jnp.bfloat16),
+            jax.ShapeDtypeStruct((rim, feat), jnp.bfloat16),
+            jax.ShapeDtypeStruct((rim, feat), jnp.bfloat16),
+        ],
         scratch_shapes=[
             pltpu.VMEM((padded, HEAD_DIM), jnp.bfloat16),
             pltpu.VMEM((padded, HEAD_DIM), jnp.bfloat16),
@@ -138,8 +146,8 @@
     )(place, mask, q, k, v, d, *halos)
 
 
-def col_kernel(me, mask, x, earlier, *refs):
-    *outs, result, bias = refs
+def col_kernel(n_parts, me, mask, x, earlier, *refs):
+    outs, result, bias = refs[:n_parts], refs[n_parts], refs[-1]
     del earlier
 
     @pl.when((pl.program_id(0) == 0) & (pl.program_id(1) == 0))
@@ -177,27 +185,33 @@
         out[...] = result[me[0] ^ partner]
 
 
-def col_attention(me, mask, x, earlier):
-    n, k, rows, cols, feat = x.shape
-    heads = feat // HEAD_DIM
+def col_attention(me, mask, x, earlier, start, heads, in_parts):
+    n, k, rows, cols, _ = x.shape
+    n_parts = n if in_parts else 0
     tokens = n * rows * GROUP
     block = (k, rows, GROUP, HEAD_DIM)
     pairs = tokens * tokens * heads * (cols // GROUP)
+    part = (k, rows, cols, heads * HEAD_DIM)
+    if in_parts:
+        out_specs = [pl.BlockSpec(block, lambda h, g: (0, 0, g, h))] * n
+        out_shape = [jax.ShapeDtypeStruct(part, jnp.bfloat16)] * n
+        held = [pltpu.VMEM((n, *block), jnp.bfloat16)]
+    else:
+        out_specs = pl.BlockSpec((n, *block), lambda h, g: (0, 0, 0, g, h))
+        out_shape = jax.ShapeDtypeStruct((n, *part), jnp.bfloat16)
+        held = []
     return pl.pallas_call(
-        col_kernel,
+        functools.partial(col_kernel, n_parts),
         grid=(heads, cols // GROUP),
         in_specs=[
             pl.BlockSpec(memory_space=pltpu.SMEM),
             pl.BlockSpec(mask.shape, lambda h, g: (0, 0)),
-            pl.BlockSpec((n, *block), lambda h, g: (0, 0, 0, g, h)),
+            pl.BlockSpec((n, *block), lambda h, g: (0, 0, 0, g, h + start)),
             pl.BlockSpec(memory_space=pl.ANY),
         ],
-        out_specs=[pl.BlockSpec(block, lambda h, g: (0, 0, g, h))] * n,
-        out_shape=[jax.ShapeDtypeStruct((k, rows, cols, feat), jnp.bfloat16)] * n,
-        scratch_shapes=[
-            pltpu.VMEM((n, *block), jnp.bfloat16),
-            pltpu.VMEM((tokens, tokens), jnp.float32),
-        ],
+        out_specs=out_specs,
+        out_shape=out_shape,
+        scratch_shapes=held + [pltpu.VMEM((tokens, tokens), jnp.float32)],
         compiler_params=pltpu.CompilerParams(vmem_limit_bytes=VMEM),
         cost_estimate=pl.CostEstimate(
             flops=240 * pairs * HEAD_DIM, bytes_accessed=4 * x.size, transcendentals=pairs
@@ -253,19 +267,25 @@
     )(*(a.reshape(rows, GRIDC, feat) for a in arrays))
 
 
-def unpack_kernel(n, me, *refs):
-    parts, outs, (held, arrived, left) = refs[:n], refs[n:-3], refs[-3:]
+def unpack_kernel(in_parts, n, start, me, *refs):
+    held, arrived, left = refs[-3:]
+    k, _, _, width = held.shape
+    outs = refs[-3 - k : -3]
     cols = GRIDC // n
     loads, stores = [], []
     for a, out in enumerate(outs):
-        for partner, part in enumerate(parts):
-            here = pl.ds(pl.multiple_of((me[0] ^ partner) * cols, cols), cols)
+        for i in range(n):
+            if in_parts:
+                part, source = refs[i], me[0] ^ i
+            else:
+                part, source = refs[0].at[i], i
+            here = pl.ds(pl.multiple_of(source * cols, cols), cols)
             loads.append(
-                pltpu.make_async_copy(
-                    part.at[a], held.at[a, :, here, :], arrived.at[a, partner]
-                )
+                pltpu.make_async_copy(part.at[a], held.at[a, :, here, :], arrived.at[a, i])
             )
-        stores.append(pltpu.make_async_copy(held.at[a], out, left.at[a]))
+        stores.append(
+            pltpu.make_async_copy(held.at[a], out.at[:, :, start : start + width], left.at[a])
+        )
     for load in loads:
         load.start()
     for a, store in enumerate(stores):
@@ -276,43 +296,47 @@
         store.wait()
 
 
-def unpacked(me, parts):
-    n = len(parts)
-    k, rows, cols, feat = parts[0].shape
+def unpacked(me, parts, start, feat, kept):
+    in_parts = isinstance(parts, list)
+    parts = parts if in_parts else [parts]
+    k, rows, cols, width = parts[0].shape[-4:]
+    n = GRIDC // cols
+    kept = [a.reshape(rows, GRIDC, feat) for a in kept]
     outs = pl.pallas_call(
-        functools.partial(unpack_kernel, n),
-        in_specs=[pl.BlockSpec(memory_space=pltpu.SMEM)] + [pl.BlockSpec(memory_space=pl.ANY)] * n,
+        functools.partial(unpack_kernel, in_parts, n, start),
+        in_specs=[pl.BlockSpec(memory_space=pltpu.SMEM)]
+        + [pl.BlockSpec(memory_space=pl.ANY)] * (len(parts) + len(kept)),
         out_specs=[pl.BlockSpec(memory_space=pl.ANY)] * k,
         out_shape=[jax.ShapeDtypeStruct((rows, GRIDC, feat), jnp.bfloat16)] * k,
         scratch_shapes=[
-            pltpu.VMEM((k, rows, GRIDC, feat), jnp.bfloat16),
+            pltpu.VMEM((k, rows, GRIDC, width), jnp.bfloat16),
             pltpu.SemaphoreType.DMA((k, n)),
             pltpu.SemaphoreType.DMA((k,)),
         ],
+        input_output_aliases={1 + len(parts) + a: a for a in range(len(kept))},
         compiler_params=pltpu.CompilerParams(vmem_limit_bytes=VMEM),
         cost_estimate=pl.CostEstimate(
-            flops=0, bytes_accessed=4 * k * rows * GRIDC * feat, transcendentals=0
+            flops=0, bytes_accessed=4 * k * rows * GRIDC * width, transcendentals=0
         ),
         name="unpack",
-    )(me, *parts)
+    )(me, *parts, *kept)
     return [o.reshape(rows * GRIDC, feat) for o in outs]
 
 
-def swapped(lo_k, lo_v, hi_k, hi_v):
+def swapped(inner, outer_k, outer_v):
     n = lax.axis_size("ctx")
-    up = [(i, i + 1) for i in range(n - 1)]
-    down = [(j, i) for i, j in up]
-    far = [(i, j) for i, j in up if j % CHIPS_APART == 0 and j + CHIPS_APART <= n]
-    near_up = [pair for pair in up if pair not in far]
-    near_down = [(j, i) for i, j in near_up]
-    side = lax.axis_index("ctx") % CHIPS_APART
-    first = [(i, i + CHIPS_APART) for i, _ in far] + [(j, j - CHIPS_APART) for _, j in far]
-    second = [(i + CHIPS_APART, j) for i, j in far] + [(j - CHIPS_APART, i) for i, j in far]
-    hop = lax.ppermute(jnp.where(side == 0, lo_v, hi_v), "ctx", first)
-    k_before, k_after = lax.ppermute(hi_k, "ctx", up), lax.ppermute(lo_k, "ctx", down)
-    v_before, v_after = lax.ppermute(hi_v, "ctx", near_up), lax.ppermute(lo_v, "ctx", near_down)
-    far_v = lax.ppermute(hop, "ctx", second)
-    return [k_before, v_before, k_after, v_after, far_v], hop
+    across = [(i, i + 1) for i in range(1, n - 1, 2)]
+    far = [(i, j) for i, j in across if j % CHIPS_APART == 0 and j + CHIPS_APART <= n]
+    near = [pair for pair in across if pair not in far]
+    back = lambda pairs: [(j, i) for i, j in pairs]
+    step = CHIPS_APART
+    first = [(i, i + step) for i, _ in far] + [(j, j - step) for _, j in far]
+    second = [(i + step, j) for i, j in far] + [(j - step, i) for i, j in far]
+    outer_v = lax.ppermute(outer_v, "ctx", near + back(near) + first)
+    outer_k = lax.ppermute(outer_k, "ctx", across + back(across))
+    inner = lax.ppermute(inner, "ctx", [(i, i ^ 1) for i in range(n)])
+    far_v = lax.ppermute(outer_v, "ctx", second)
+    return inner, outer_k, outer_v, far_v
 
 
 def exchanged(x):
@@ -329,36 +353,50 @@
     band = (row_mask.shape[1] - 1) // 2
     rim = band * GRIDC
 
-    rims = [a for x in (row_key, row_value) for a in (x[:rim], x[tokens - rim :])]
+    feat = row_key.shape[1]
+    me = lax.axis_index("ctx")
+    odd = me % 2
+    side = me % CHIPS_APART
+    inner_at, outer_at = (1 - odd) * (tokens - rim), odd * (tokens - rim)
+    rim_of = lambda x, at: lax.dynamic_slice_in_dim(x, at, rim, 0)
+    inner = jnp.stack([rim_of(row_key, inner_at), rim_of(row_value, inner_at)])
+    outer_k, outer_v = rim_of(row_key, outer_at), rim_of(row_value, outer_at)
     cols = [col_query, col_key, col_value, col_cotangent]
-    *rims, cols = lax.optimization_barrier((*rims, cols))
-    halos, hop = swapped(rims[0], rims[2], rims[1], rims[3])
-    sent, hop = lax.optimization_barrier((packed(cols, n), hop))
+    inner, outer_k, outer_v, cols = lax.optimization_barrier((inner, outer_k, outer_v, cols))
+    halos = swapped(inner, outer_k, outer_v)
+    sent, outer_v = lax.optimization_barrier((packed(cols, n), halos[2]))
     moved = exchanged(sent)
 
-    me = lax.axis_index("ctx")
-    place = jnp.stack([me * rows, me % CHIPS_APART])
+    is_far = (side == 0) | (side == CHIPS_APART - 1)
+    place = jnp.stack([me * rows, odd, is_far.astype(odd.dtype)])
     row_output, row_dquery, own_k, own_v, *sides = row_attention(
         place, row_mask, row_query, row_key, row_value, row_cotangent, halos, band
     )
-    halos, _ = swapped(*sides)
-
-    results = col_attention(me.reshape(1), col_mask, moved, row_output)
-    results, halos = lax.optimization_barrier((results, halos))
-    returned = [results[0]] + [
-        lax.ppermute(results[k], "ctx", [(i, i ^ k) for i in range(n)]) for k in range(1, n)
+    inner, outer_k, outer_v, far_v = swapped(*sides)
+
+    heads = col_query.shape[1] // HEAD_DIM
+    half = heads // 2
+    where = me.reshape(1)
+    partners = [[(i, i ^ k) for i in range(n)] for k in range(n)]
+    send = lambda parts: [parts[0]] + [
+        lax.ppermute(part, "ctx", pairs) for part, pairs in zip(parts[1:], partners[1:])
     ]
-    col_results = unpacked(me.reshape(1), returned)
-
-    k_before, v_before, k_after, v_after, far_v = halos
-    v_before = jnp.where(me % CHIPS_APART == 0, far_v, v_before)
-    v_after = jnp.where(me % CHIPS_APART == CHIPS_APART - 1, far_v, v_after)
+    first = col_attention(where, col_mask, moved, row_output, 0, half, False)
+    first, inner, outer_k, outer_v = lax.optimization_barrier((first, inner, outer_k, outer_v))
+    second = col_attention(where, col_mask, moved, first, half, heads - half, True)
+    second, far_v = lax.optimization_barrier((second, far_v))
+    first, second = exchanged(first), send(second)
+    col_feat = col_query.shape[1]
+    col_results = unpacked(where, first, 0, col_feat, [])
+    col_results = unpacked(where, second, half * HEAD_DIM, col_feat, col_results)
+
+    outer_v = jnp.where(is_far, far_v, outer_v)
     row_grads = []
-    for own, prev, following in ((own_k, k_before, k_after), (own_v, v_before, v_after)):
-        gap = jnp.zeros((tokens - rim, own.shape[1]), own.dtype)
-        added = jnp.concatenate([prev.astype(own.dtype), gap]) + jnp.concatenate(
-            [gap, following.astype(own.dtype)]
-        )
+    for own, near, across in ((own_k, inner[0], outer_k), (own_v, inner[1], outer_v)):
+        lo = jnp.where(odd == 1, near, across).astype(own.dtype)
+        hi = jnp.where(odd == 1, across, near).astype(own.dtype)
+        gap = jnp.zeros((tokens - rim, feat), own.dtype)
+        added = jnp.concatenate([lo, gap]) + jnp.concatenate([gap, hi])
         row_grads.append((own + added).astype(jnp.bfloat16))
     return (
         row_output, row_dquery, *row_grads,

time: 226 us -> 217 us (0.960)
  starting transfers between devices: 58.2 us -> 47.2 us
  waiting for transfers between devices: 66.3 us -> 61.4 us
  Pallas kernels: 88.7 us -> 92.4 us
  local copies, waits for them, and re-layouts: 3.76 us -> 6.78 us
    ppermute x19 -> x15, starting transfers between devices: 50.3 us -> 23.7 us  [the longest x7 7.51 us: body(): lax.ppermute(part, 'ctx', pairs)]
    all_to_all x1 -> x2, starting transfers between devices: 7.92 us -> 23.5 us  [exchanged(): return lax.all_to_all(x, 'ctx', 0, 0, tiled=True)]
    ppermute x19 -> x15, waiting for transfers between devices: 66.3 us -> 61.4 us  [the longest x7 36.3 us: body(): lax.ppermute(part, 'ctx', pairs)]
    unnamed x15 -> x17, local copies, waits for them, and re-layouts: 1.71 us -> 4.72 us
    pallas_call x2 -> x4, Pallas kernels: 33.6 us -> 36.3 us  [the longest x2 29.9 us: col_attention(): pl.pallas_call(functools.partial(col_kernel, n_parts), grid=(heads, cols...]
  transfers between devices with their start and end apart: 20 -> 17, of which waited for: 5 -> 5; matrix products, arithmetic and copies ran while one was open for 3% -> 3% of each run, Pallas kernels for 37% -> 42%
where the time goes in v5:
time: 217 us; the launch traced here: 215 us
  Pallas kernels  92.4 us (43%)
  waiting for transfers between devices  61.4 us (28%)
  starting transfers between devices  47.2 us (22%)
  local copies, waits for them, and re-layouts  6.78 us (3%)
  other arithmetic  5.92 us (3%)
    pallas_call x1, Pallas kernels, row_attention(): pl.pallas_call(functools.partial(row_kernel, band), grid=(heads,), in_spe...  50.6 us
    ppermute x7, waiting for transfers between devices, body(): lax.ppermute(part, 'ctx', pairs)  36.3 us
    pallas_call x2, Pallas kernels, col_attention(): pl.pallas_call(functools.partial(col_kernel, n_parts), grid=(heads, cols...  29.9 us
    ppermute x2, waiting for transfers between devices, swapped(): outer_v = lax.ppermute(outer_v, 'ctx', near + back(near) + first)  25.1 us
    all_to_all x2, starting transfers between devices, exchanged(): return lax.all_to_all(x, 'ctx', 0, 0, tiled=True)  23.5 us
    ppermute x7, starting transfers between devices, body(): lax.ppermute(part, 'ctx', pairs)  7.51 us
    ppermute x2, starting transfers between devices, swapped(): outer_v = lax.ppermute(outer_v, 'ctx', near + back(near) + first)  7.17 us
    pallas_call x2, Pallas kernels, unpacked(): pl.pallas_call(functools.partial(unpack_kernel, in_parts, n, start), in_s...  6.36 us
  transfers between devices with their start and end apart: 17, of which 5 were waited for; matrix products, arithmetic and copies ran while one was open for 3% of the time, Pallas kernels for 42%

profile of v5, /device:TPU:11, one launch (start us, length us, event | category | flops | bytes accessed | tf_op | source)
XLA Modules:
  0.0 214.8 jit_solution(12395536924281406812)
XLA Ops:
  0.7 2.1 constant_dynamic-slice_fusion
  2.7 0.0 copy-start.6
  2.7 0.1 pad_maximum_fusion
  2.9 0.7 collective-permute-start
  3.6 3.2 %collective-permute-start.2 = (bf16[512,768]{1,0:T(8,128)(2,1)S(1)}, bf16[512,768]{1,0:T(8,128)(2,1)S(1)}, u32[]{:S(2)}, u32[]{:S(2)}) collective-permute-start(bf16[512,768]{1,0:T(8,128)(2,1)S(1)} %get-tuple-element.54), channel_id=1, source_target_pairs={{4,8},{20,24},{8,4},{24,20},{12,28},{16,0},{5,9},{21,25},{9,5},{25... | collective-permute-start | bytes 2359304 | tf_op jit(solution)/shard_map/ppermute | solution.py:335
  6.8 2.3 %collective-permute-start.1 = (bf16[512,768]{1,0:T(8,128)(2,1)S(1)}, bf16[512,768]{1,0:T(8,128)(2,1)}, u32[]{:S(2)}, u32[]{:S(2)}) collective-permute-start(bf16[512,768]{1,0:T(8,128)(2,1)S(1)} %get-tuple-element.53), channel_id=1, source_target_pairs={{4,8},{12,16},{20,24},{8,4},{16,12},{24,20},{5,9},{13,17},{21,25},... | collective-permute-start | bytes 2359304 | tf_op jit(solution)/shard_map/ppermute | solution.py:336
  9.1 6.6 %collective-permute-done.2.outer_v = bf16[512,768]{1,0:T(8,128)(2,1)S(1)} collective-permute-done((bf16[512,768]{1,0:T(8,128)(2,1)S(1)}, bf16[512,768]{1,0:T(8,128)(2,1)S(1)}, u32[]{:S(2)}, u32[]{:S(2)}) %collective-permute-start.2) | collective-permute-done | bytes 786464 | tf_op jit(solution)/shard_map/ppermute | solution.py:335
  15.7 0.0 copy-start.7
  15.7 1.3 collective-permute-start.3
  17.0 0.0 copy-done.6
  17.0 0.7 copy.22.mask
  17.7 5.5 %pack.1 = bf16[8,4,8,16,768]{4,3,2,1,0:T(8,128)(2,1)} custom-call(bf16[8,128,768]{2,1,0:T(8,128)(2,1)} %bitcast.22, bf16[8,128,768]{2,1,0:T(8,128)(2,1)} %bitcast.23, bf16[8,128,768]{2,1,0:T(8,128)(2,1)} %bitcast.24, bf16[8,128,768]{2,1,0:T(8,128)(2,1)} %bitcast.25), custom_call_target="tpu_custom_call" | custom-call | bytes 12582912 | tf_op jit(solution)/shard_map/pack/pallas_call | solution.py:252
  23.2 0.0 copy-done.7
  23.2 0.6 pad_add_fusion.place
  23.8 10.0 %all-to-all-start = ((bf16[8,4,8,16,768]{4,3,2,1,0:T(8,128)(2,1)}), bf16[8,4,8,16,768]{4,3,2,1,0:T(8,128)(2,1)}, u32[]{:S(2)}, u32[]{:S(2)}) async-start(bf16[8,4,8,16,768]{4,3,2,1,0:T(8,128)(2,1)} %pack.1), calls=%async_computation | async-start | bytes 12582912 | tf_op jit(solution)/shard_map/all_to_all | solution.py:343
  33.7 0.0 collective-permute-done.1.outer_k
  33.7 0.0 collective-permute-done.inner_kv
  33.7 0.0 collective-permute-done.3.far_v
  33.7 50.6 %row_heads.1 = (bf16[1024,768]{1,0:T(8,128)(2,1)}, bf16[1024,768]{1,0:T(8,128)(2,1)}, f32[1024,768]{1,0:T(8,128)}, f32[1024,768]{1,0:T(8,128)}, bf16[2,512,768]{...) custom-call(s32[3]{0:T(128)} %pad_add_fusion.place, s32[64,9]{1,0:T(8,128)} %copy.22.mask, ...), custom_call_target="tpu_custom_call" | custom-call | flops 241591910400 | bytes 23592960 | tf_op jit(solution)/shard_map/row_heads/pallas_call | solution.py:121
  84.4 4.0 %collective-permute-start.6 = (bf16[512,768]{1,0:T(8,128)(2,1)}, bf16[512,768]{1,0:T(8,128)(2,1)}, u32[]{:S(2)}, u32[]{:S(2)}) collective-permute-start(bf16[512,768]{1,0:T(8,128)(2,1)} %get-tuple-element.65), channel_id=1, source_target_pairs={{4,8},{20,24},{8,4},{24,20},{12,28},{16,0},{5,9},{21,25},{9,5},{25... | collective-permute-start | bytes 2359304 | tf_op jit(solution)/shard_map/ppermute | solution.py:335
  88.3 0.6 collective-permute-start.4
  88.9 2.9 %collective-permute-start.5 = (bf16[512,768]{1,0:T(8,128)(2,1)}, bf16[512,768]{1,0:T(8,128)(2,1)S(1)}, u32[]{:S(2)}, u32[]{:S(2)}) collective-permute-start(bf16[512,768]{1,0:T(8,128)(2,1)} %get-tuple-element.64), channel_id=1, source_target_pairs={{4,8},{12,16},{20,24},{8,4},{16,12},{24,20},{5,9},{13,17},{21,25},... | collective-permute-start | bytes 2359304 | tf_op jit(solution)/shard_map/ppermute | solution.py:336
  91.8 18.5 %collective-permute-done.6 = bf16[512,768]{1,0:T(8,128)(2,1)} collective-permute-done((bf16[512,768]{1,0:T(8,128)(2,1)}, bf16[512,768]{1,0:T(8,128)(2,1)}, u32[]{:S(2)}, u32[]{:S(2)}) %collective-permute-start.6) | collective-permute-done | bytes 786464 | tf_op jit(solution)/shard_map/ppermute | solution.py:335
  110.4 1.3 collective-permute-start.7
  111.6 0.0 all-to-all-done.x
  111.7 14.9 %col_heads.2.earlier = bf16[8,4,8,16,384]{4,3,2,1,0:T(8,128)(2,1)} custom-call(s32[1]{0:T(128)} %bitcast.5.me, s32[64,64]{1,0:T(8,128)} %mask.4, bf16[8,4,8,16,768]{4,3,2,1,0:T(8,128)(2,1)} %all-to-all-done.x, bf16[1024,768]{1,0:T(8,128)(2,1)} %get-tuple-element.44.earlier), custom_call_target="tpu_custom_call" | custom-call | flops 48318382080 | bytes 12582912 | tf_op jit(solution)/shard_map/col_heads/pallas_call | solution.py:203
  126.5 0.0 collective-permute-done.5
  126.5 0.0 copy-start.4
  126.5 0.0 collective-permute-done.4
  126.5 0.0 copy-start.3
  126.5 0.9 copy-done.4
  127.4 0.5 copy-done.3
  127.9 13.6 %all-to-all-start.1 = ((bf16[8,4,8,16,384]{4,3,2,1,0:T(8,128)(2,1)}), bf16[8,4,8,16,384]{4,3,2,1,0:T(8,128)(2,1)S(1)}, u32[]{:S(2)}, u32[]{:S(2)}) async-start(bf16[8,4,8,16,384]{4,3,2,1,0:T(8,128)(2,1)} %col_heads.2.earlier), calls=%async_computation.1 | async-start | bytes 6291456 | tf_op jit(solution)/shard_map/all_to_all | solution.py:343
  141.5 15.1 %col_heads.3 = (bf16[4,8,16,384]{3,2,1,0:T(8,128)(2,1)}, bf16[4,8,16,384]{3,2,1,0:T(8,128)(2,1)}, bf16[4,8,16,384]{3,2,1,0:T(8,128)(2,1)}, bf16[4,8,16,384]{3,2,...) custom-call(s32[1]{0:T(128)} %bitcast.5.me, ...), custom_call_target="tpu_custom_call" | custom-call | flops 48318382080 | bytes 12582912 | tf_op jit(solution)/shard_map/col_heads/pallas_call | solution.py:203
  156.6 0.0 collective-permute-done.7
  156.6 0.4 collective-permute-start.8
  157.0 0.6 collective-permute-start.9
  157.6 1.2 collective-permute-start.10
  158.8 1.2 collective-permute-start.11
  160.0 0.5 collective-permute-start.12
  160.5 0.0 copy-start.2
  160.5 2.2 %bitcast_select_fusion.1 = (bf16[512,768]{1,0:T(8,128)(2,1)S(1)}, bf16[512,768]{1,0:T(8,128)(2,1)S(1)}, bf16[512,768]{1,0:T(8,128)(2,1)S(1)}, bf16[512,768]{1,0:T(8,128)(2,1)S(1)}) fusion(pred[]{:T(512)S(6)} %eq.17, bf16[2,512,768]{2,1,0:T(8,128)(2,1)} %copy-done.3, bf16[512,768]{1,0:T(8,128)(2,1)} %collective-permute-done.7, ...), kind=kLoop, calls=%fused_computation.4 | loop fusion | flops 1966080 | bytes 7077890 | tf_op jit(solution)/shard_map/jit(_where)/select_n | solution.py:396
  162.7 0.0 collective-permute-done.8.refs_1_
  162.7 0.0 copy-start.5
  162.7 1.3 collective-permute-start.13
  164.0 22.0 %collective-permute-done.9.refs_2_ = bf16[4,8,16,384]{3,2,1,0:T(8,128)(2,1)} collective-permute-done((bf16[4,8,16,384]{3,2,1,0:T(8,128)(2,1)}, bf16[4,8,16,384]{3,2,1,0:T(8,128)(2,1)}, u32[]{:S(2)}, u32[]{:S(2)}) %collective-permute-start.9) | collective-permute-done | bytes 393248 | tf_op jit(solution)/shard_map/ppermute | solution.py:382
  186.0 2.3 %collective-permute-start.14 = (bf16[4,8,16,384]{3,2,1,0:T(8,128)(2,1)}, bf16[4,8,16,384]{3,2,1,0:T(8,128)(2,1)}, u32[]{:S(2)}, u32[]{:S(2)}) collective-permute-start(bf16[4,8,16,384]{3,2,1,0:T(8,128)(2,1)} %get-tuple-element.87), channel_id=1, source_target_pairs={{0,28},{4,24},{8,20},{12,16},{16,12},{20,8},{24,4},{28,0},{1,29},{... | collective-permute-start | bytes 1179656 | tf_op jit(solution)/shard_map/ppermute | solution.py:382
  188.4 0.0 copy-done.2
  188.4 0.0 copy-start.1
  188.4 1.5 add_convert_fusion.1
  189.8 0.0 copy-done.5
  189.9 1.0 copy-done.1
  190.8 1.5 add_convert_fusion
  192.3 0.0 all-to-all-done.1.refs_0_
  192.3 0.0 copy-start
  192.3 1.6 copy-done
  193.9 3.2 %unpack.2 = (bf16[8,128,768]{2,1,0:T(8,128)(2,1)}, bf16[8,128,768]{2,1,0:T(8,128)(2,1)}, bf16[8,128,768]{2,1,0:T(8,128)(2,1)}, bf16[8,128,768]{2,1,0:T(8,128)(2,1)}) custom-call(s32[1]{0:T(128)} %bitcast.5.me, bf16[8,4,8,16,384]{4,3,2,1,0:T(8,128)(2,1)} %copy-done), custom_call_target="tpu_custom_call" | custom-call | bytes 6291456 | tf_op jit(solution)/shard_map/unpack/pallas_call | solution.py:305
  197.1 0.0 collective-permute-done.10.refs_3_
  197.1 0.0 collective-permute-done.11.refs_4_
  197.2 0.0 collective-permute-done.12.refs_5_
  197.2 5.6 %collective-permute-done.13.refs_6_ = bf16[4,8,16,384]{3,2,1,0:T(8,128)(2,1)} collective-permute-done((bf16[4,8,16,384]{3,2,1,0:T(8,128)(2,1)}, bf16[4,8,16,384]{3,2,1,0:T(8,128)(2,1)}, u32[]{:S(2)}, u32[]{:S(2)}) %collective-permute-start.13) | collective-permute-done | bytes 393248 | tf_op jit(solution)/shard_map/ppermute | solution.py:382
  202.8 8.6 %collective-permute-done.14.refs_7_ = bf16[4,8,16,384]{3,2,1,0:T(8,128)(2,1)} collective-permute-done((bf16[4,8,16,384]{3,2,1,0:T(8,128)(2,1)}, bf16[4,8,16,384]{3,2,1,0:T(8,128)(2,1)}, u32[]{:S(2)}, u32[]{:S(2)}) %collective-permute-start.14) | collective-permute-done | bytes 393248 | tf_op jit(solution)/shard_map/ppermute | solution.py:382
  211.4 3.2 %unpack.3 = (bf16[8,128,768]{2,1,0:T(8,128)(2,1)}, bf16[8,128,768]{2,1,0:T(8,128)(2,1)}, bf16[8,128,768]{2,1,0:T(8,128)(2,1)}, bf16[8,128,768]{2,1,0:T(8,128)(2,1)}) custom-call(s32[1]{0:T(128)} %bitcast.5.me, bf16[4,8,16,384]{3,2,1,0:T(8,128)(2,1)} %get-tuple-element.80.refs_0_, ...), custom_call_target="tpu_custom_call", output_to_operand_aliasing={{0}: (9, {}), {1}: (10, {}), {2}: (11, {}), {3}: (12, {})} | custom-call | bytes 6291456 | tf_op jit(solution)/shard_map/unpack/pallas_call | solution.py:305
Async XLA Ops:
  2.7 14.3 %copy-start.6 = (s32[64,9]{0,1:T(8,128)S(1)}, s32[64,9]{0,1:T(8,128)}, u32[]{:S(2)}) copy-start(s32[64,9]{0,1:T(8,128)} %param.14) | copy-start | bytes 6916
  2.9 30.8 %collective-permute-start = (bf16[2,512,768]{2,1,0:T(8,128)(2,1)S(1)}, bf16[2,512,768]{2,1,0:T(8,128)(2,1)}, u32[]{:S(2)}, u32[]{:S(2)}) collective-permute-start(bf16[2,512,768]{2,1,0:T(8,128)(2,1)S(1)} %pad_maximum_fusion), channel_id=1, source_target_pairs={{0,4},{4,0},{8,12},{12,8},{16,20},{20,16},{24,28},{28,24},{1,5},{5... | collective-permute-start | bytes 4718600 | tf_op jit(solution)/shard_map/ppermute | solution.py:337
  3.6 12.1 %collective-permute-start.2 = (bf16[512,768]{1,0:T(8,128)(2,1)S(1)}, bf16[512,768]{1,0:T(8,128)(2,1)S(1)}, u32[]{:S(2)}, u32[]{:S(2)}) collective-permute-start(bf16[512,768]{1,0:T(8,128)(2,1)S(1)} %get-tuple-element.54), channel_id=1, source_target_pairs={{4,8},{20,24},{8,4},{24,20},{12,28},{16,0},{5,9},{21,25},{9,5},{25... | collective-permute-start | bytes 2359304 | tf_op jit(solution)/shard_map/ppermute | solution.py:335
  6.8 26.9 %collective-permute-start.1 = (bf16[512,768]{1,0:T(8,128)(2,1)S(1)}, bf16[512,768]{1,0:T(8,128)(2,1)}, u32[]{:S(2)}, u32[]{:S(2)}) collective-permute-start(bf16[512,768]{1,0:T(8,128)(2,1)S(1)} %get-tuple-element.53), channel_id=1, source_target_pairs={{4,8},{12,16},{20,24},{8,4},{16,12},{24,20},{5,9},{13,17},{21,25},... | collective-permute-start | bytes 2359304 | tf_op jit(solution)/shard_map/ppermute | solution.py:336
  15.7 7.5 %copy-start.7 = (bf16[512,768]{1,0:T(8,128)(2,1)}, bf16[512,768]{1,0:T(8,128)(2,1)S(1)}, u32[]{:S(2)}) copy-start(bf16[512,768]{1,0:T(8,128)(2,1)S(1)} %collective-permute-done.2.outer_v) | copy-start | bytes 2359300
  15.7 18.0 %collective-permute-start.3 = (bf16[512,768]{1,0:T(8,128)(2,1)S(1)}, bf16[512,768]{1,0:T(8,128)(2,1)}, u32[]{:S(2)}, u32[]{:S(2)}) collective-permute-start(bf16[512,768]{1,0:T(8,128)(2,1)S(1)} %collective-permute-done.2.outer_v), channel_id=1, source_target_pairs={{28,16},{0,12},{29,17},{1,13},{30,18},{2,14},{31,19},{3,15}} | collective-permute-start | bytes 2359304 | tf_op jit(solution)/shard_map/ppermute | solution.py:338
  23.8 87.9 %all-to-all-start = ((bf16[8,4,8,16,768]{4,3,2,1,0:T(8,128)(2,1)}), bf16[8,4,8,16,768]{4,3,2,1,0:T(8,128)(2,1)}, u32[]{:S(2)}, u32[]{:S(2)}) async-start(bf16[8,4,8,16,768]{4,3,2,1,0:T(8,128)(2,1)} %pack.1), calls=%async_computation | async-start | bytes 12582912 | tf_op jit(solution)/shard_map/all_to_all | solution.py:343
  84.4 26.0 %collective-permute-start.6 = (bf16[512,768]{1,0:T(8,128)(2,1)}, bf16[512,768]{1,0:T(8,128)(2,1)}, u32[]{:S(2)}, u32[]{:S(2)}) collective-permute-start(bf16[512,768]{1,0:T(8,128)(2,1)} %get-tuple-element.65), channel_id=1, source_target_pairs={{4,8},{20,24},{8,4},{24,20},{12,28},{16,0},{5,9},{21,25},{9,5},{25... | collective-permute-start | bytes 2359304 | tf_op jit(solution)/shard_map/ppermute | solution.py:335
  88.3 38.2 %collective-permute-start.4 = (bf16[2,512,768]{2,1,0:T(8,128)(2,1)}, bf16[2,512,768]{2,1,0:T(8,128)(2,1)S(1)}, u32[]{:S(2)}, u32[]{:S(2)}) collective-permute-start(bf16[2,512,768]{2,1,0:T(8,128)(2,1)} %get-tuple-element.63), channel_id=1, source_target_pairs={{0,4},{4,0},{8,12},{12,8},{16,20},{20,16},{24,28},{28,24},{1,5},{5... | collective-permute-start | bytes 4718600 | tf_op jit(solution)/shard_map/ppermute | solution.py:337
  88.9 37.6 %collective-permute-start.5 = (bf16[512,768]{1,0:T(8,128)(2,1)}, bf16[512,768]{1,0:T(8,128)(2,1)S(1)}, u32[]{:S(2)}, u32[]{:S(2)}) collective-permute-start(bf16[512,768]{1,0:T(8,128)(2,1)} %get-tuple-element.64), channel_id=1, source_target_pairs={{4,8},{12,16},{20,24},{8,4},{16,12},{24,20},{5,9},{13,17},{21,25},... | collective-permute-start | bytes 2359304 | tf_op jit(solution)/shard_map/ppermute | solution.py:336
  110.4 46.2 %collective-permute-start.7 = (bf16[512,768]{1,0:T(8,128)(2,1)}, bf16[512,768]{1,0:T(8,128)(2,1)}, u32[]{:S(2)}, u32[]{:S(2)}) collective-permute-start(bf16[512,768]{1,0:T(8,128)(2,1)} %collective-permute-done.6), channel_id=1, source_target_pairs={{28,16},{0,12},{29,17},{1,13},{30,18},{2,14},{31,19},{3,15}} | collective-permute-start | bytes 2359304 | tf_op jit(solution)/shard_map/ppermute | solution.py:338
  126.5 0.9 copy-start.4
  126.5 1.4 copy-start.3
  127.9 64.4 %all-to-all-start.1 = ((bf16[8,4,8,16,384]{4,3,2,1,0:T(8,128)(2,1)}), bf16[8,4,8,16,384]{4,3,2,1,0:T(8,128)(2,1)S(1)}, u32[]{:S(2)}, u32[]{:S(2)}) async-start(bf16[8,4,8,16,384]{4,3,2,1,0:T(8,128)(2,1)} %col_heads.2.earlier), calls=%async_computation.1 | async-start | bytes 6291456 | tf_op jit(solution)/shard_map/all_to_all | solution.py:343
  156.6 6.2 %collective-permute-start.8 = (bf16[4,8,16,384]{3,2,1,0:T(8,128)(2,1)}, bf16[4,8,16,384]{3,2,1,0:T(8,128)(2,1)S(1)}, u32[]{:S(2)}, u32[]{:S(2)}) collective-permute-start(bf16[4,8,16,384]{3,2,1,0:T(8,128)(2,1)} %get-tuple-element.81), channel_id=1, source_target_pairs={{0,4},{4,0},{8,12},{12,8},{16,20},{20,16},{24,28},{28,24},{1,5},{5... | collective-permute-start | bytes 1179656 | tf_op jit(solution)/shard_map/ppermute | solution.py:382
  157.0 29.0 %collective-permute-start.9 = (bf16[4,8,16,384]{3,2,1,0:T(8,128)(2,1)}, bf16[4,8,16,384]{3,2,1,0:T(8,128)(2,1)}, u32[]{:S(2)}, u32[]{:S(2)}) collective-permute-start(bf16[4,8,16,384]{3,2,1,0:T(8,128)(2,1)} %get-tuple-element.82), channel_id=1, source_target_pairs={{0,8},{4,12},{8,0},{12,4},{16,24},{20,28},{24,16},{28,20},{1,9},{5... | collective-permute-start | bytes 1179656 | tf_op jit(solution)/shard_map/ppermute | solution.py:382
  157.6 39.5 %collective-permute-start.10 = (bf16[4,8,16,384]{3,2,1,0:T(8,128)(2,1)}, bf16[4,8,16,384]{3,2,1,0:T(8,128)(2,1)}, u32[]{:S(2)}, u32[]{:S(2)}) collective-permute-start(bf16[4,8,16,384]{3,2,1,0:T(8,128)(2,1)} %get-tuple-element.83), channel_id=1, source_target_pairs={{0,12},{4,8},{8,4},{12,0},{16,28},{20,24},{24,20},{28,16},{1,13},{... | collective-permute-start | bytes 1179656 | tf_op jit(solution)/shard_map/ppermute | solution.py:382
  158.8 38.4 %collective-permute-start.11 = (bf16[4,8,16,384]{3,2,1,0:T(8,128)(2,1)}, bf16[4,8,16,384]{3,2,1,0:T(8,128)(2,1)}, u32[]{:S(2)}, u32[]{:S(2)}) collective-permute-start(bf16[4,8,16,384]{3,2,1,0:T(8,128)(2,1)} %get-tuple-element.84), channel_id=1, source_target_pairs={{0,16},{4,20},{8,24},{12,28},{16,0},{20,4},{24,8},{28,12},{1,17},{... | collective-permute-start | bytes 1179656 | tf_op jit(solution)/shard_map/ppermute | solution.py:382
  160.0 37.2 %collective-permute-start.12 = (bf16[4,8,16,384]{3,2,1,0:T(8,128)(2,1)}, bf16[4,8,16,384]{3,2,1,0:T(8,128)(2,1)}, u32[]{:S(2)}, u32[]{:S(2)}) collective-permute-start(bf16[4,8,16,384]{3,2,1,0:T(8,128)(2,1)} %get-tuple-element.85), channel_id=1, source_target_pairs={{0,20},{4,16},{8,28},{12,24},{16,4},{20,0},{24,12},{28,8},{1,21},{... | collective-permute-start | bytes 1179656 | tf_op jit(solution)/shard_map/ppermute | solution.py:382
  160.5 27.9 %copy-start.2 = (f32[1024,768]{1,0:T(8,128)S(1)}, f32[1024,768]{1,0:T(8,128)}, u32[]{:S(2)}) copy-start(f32[1024,768]{1,0:T(8,128)} %get-tuple-element.57) | copy-start | bytes 9437188
  162.7 27.1 %copy-start.5 = (bf16[4,8,16,384]{3,2,1,0:T(8,128)(2,1)}, bf16[4,8,16,384]{3,2,1,0:T(8,128)(2,1)S(1)}, u32[]{:S(2)}) copy-start(bf16[4,8,16,384]{3,2,1,0:T(8,128)(2,1)S(1)} %collective-permute-done.8.refs_1_) | copy-start | bytes 1179652
  162.7 40.1 %collective-permute-start.13 = (bf16[4,8,16,384]{3,2,1,0:T(8,128)(2,1)}, bf16[4,8,16,384]{3,2,1,0:T(8,128)(2,1)}, u32[]{:S(2)}, u32[]{:S(2)}) collective-permute-start(bf16[4,8,16,384]{3,2,1,0:T(8,128)(2,1)} %get-tuple-element.86), channel_id=1, source_target_pairs={{0,24},{4,28},{8,16},{12,20},{16,8},{20,12},{24,0},{28,4},{1,25},{... | collective-permute-start | bytes 1179656 | tf_op jit(solution)/shard_map/ppermute | solution.py:382
  186.0 25.4 %collective-permute-start.14 = (bf16[4,8,16,384]{3,2,1,0:T(8,128)(2,1)}, bf16[4,8,16,384]{3,2,1,0:T(8,128)(2,1)}, u32[]{:S(2)}, u32[]{:S(2)}) collective-permute-start(bf16[4,8,16,384]{3,2,1,0:T(8,128)(2,1)} %get-tuple-element.87), channel_id=1, source_target_pairs={{0,28},{4,24},{8,20},{12,16},{16,12},{20,8},{24,4},{28,0},{1,29},{... | collective-permute-start | bytes 1179656 | tf_op jit(solution)/shard_map/ppermute | solution.py:382
  188.4 2.5 %copy-start.1 = (f32[1024,768]{1,0:T(8,128)S(1)}, f32[1024,768]{1,0:T(8,128)}, u32[]{:S(2)}) copy-start(f32[1024,768]{1,0:T(8,128)} %get-tuple-element.68) | copy-start | bytes 9437188
  192.3 1.6 copy-start

commit v6 on v5

--- a/solution.py
+++ b/solution.py
@@ -335,8 +335,7 @@
     outer_v = lax.ppermute(outer_v, "ctx", near + back(near) + first)
     outer_k = lax.ppermute(outer_k, "ctx", across + back(across))
     inner = lax.ppermute(inner, "ctx", [(i, i ^ 1) for i in range(n)])
-    far_v = lax.ppermute(outer_v, "ctx", second)
-    return inner, outer_k, outer_v, far_v
+    return inner, outer_k, outer_v, lambda passed: lax.ppermute(passed, "ctx", second)
 
 
 def exchanged(x):
@@ -363,8 +362,9 @@
     outer_k, outer_v = rim_of(row_key, outer_at), rim_of(row_value, outer_at)
     cols = [col_query, col_key, col_value, col_cotangent]
     inner, outer_k, outer_v, cols = lax.optimization_barrier((inner, outer_k, outer_v, cols))
-    halos = swapped(inner, outer_k, outer_v)
-    sent, outer_v = lax.optimization_barrier((packed(cols, n), halos[2]))
+    inner, outer_k, outer_v, second_hop = swapped(inner, outer_k, outer_v)
+    sent, outer_v = lax.optimization_barrier((packed(cols, n), outer_v))
+    halos = [inner, outer_k, outer_v, second_hop(outer_v)]
     moved = exchanged(sent)
 
     is_far = (side == 0) | (side == CHIPS_APART - 1)
@@ -372,7 +372,7 @@
     row_output, row_dquery, own_k, own_v, *sides = row_attention(
         place, row_mask, row_query, row_key, row_value, row_cotangent, halos, band
     )
-    inner, outer_k, outer_v, far_v = swapped(*sides)
+    inner, outer_k, outer_v, second_hop = swapped(*sides)
 
     heads = col_query.shape[1] // HEAD_DIM
     half = heads // 2
@@ -382,15 +382,15 @@
         lax.ppermute(part, "ctx", pairs) for part, pairs in zip(parts[1:], partners[1:])
     ]
     first = col_attention(where, col_mask, moved, row_output, 0, half, False)
-    first, inner, outer_k, outer_v = lax.optimization_barrier((first, inner, outer_k, outer_v))
+    first, inner, outer_k = lax.optimization_barrier((first, inner, outer_k))
     second = col_attention(where, col_mask, moved, first, half, heads - half, True)
-    second, far_v = lax.optimization_barrier((second, far_v))
+    second, outer_v = lax.optimization_barrier((second, outer_v))
     first, second = exchanged(first), send(second)
     col_feat = col_query.shape[1]
     col_results = unpacked(where, first, 0, col_feat, [])
     col_results = unpacked(where, second, half * HEAD_DIM, col_feat, col_results)
 
-    outer_v = jnp.where(is_far, far_v, outer_v)
+    outer_v = jnp.where(is_far, second_hop(outer_v), outer_v)
     row_grads = []
     for own, near, across in ((own_k, inner[0], outer_k), (own_v, inner[1], outer_v)):
         lo = jnp.where(odd == 1, near, across).astype(own.dtype)

time: 217 us -> 210 us (0.968)
  starting transfers between devices: 47.2 us -> 40.7 us
    ppermute x2, waiting for transfers between devices: 0.01 us -> 38.5 us  [swapped(): lax.ppermute(passed, 'ctx', second)]
    ppermute x2, waiting for transfers between devices: 25.1 us -> 0.01 us  [swapped(): outer_v = lax.ppermute(outer_v, 'ctx', near + back(near) + first)]
    ppermute x7, waiting for transfers between devices: 36.3 us -> 12.5 us  [body(): lax.ppermute(part, 'ctx', pairs)]
    ppermute x2, waiting for transfers between devices: 0.01 us -> 5.59 us  [swapped(): outer_k = lax.ppermute(outer_k, 'ctx', across + back(across))]
    all_to_all x2, starting transfers between devices: 23.5 us -> 18.3 us  [exchanged(): return lax.all_to_all(x, 'ctx', 0, 0, tiled=True)]
    all_to_all x2, waiting for transfers between devices: 0.01 us -> 3.09 us  [exchanged(): return lax.all_to_all(x, 'ctx', 0, 0, tiled=True)]
  transfers between devices with their start and end apart: 17 -> 17, of which waited for: 5 -> 6; matrix products, arithmetic and copies ran while one was open for 3% -> 3% of each run, Pallas kernels for 42% -> 43%
where the time goes in v6:
time: 210 us; the launch traced here: 207 us
  Pallas kernels  92.4 us (44%)
  waiting for transfers between devices  59.7 us (28%)
  starting transfers between devices  40.7 us (19%)
  local copies, waits for them, and re-layouts  7.66 us (4%)
  other arithmetic  5.91 us (3%)
    pallas_call x1, Pallas kernels, row_attention(): pl.pallas_call(functools.partial(row_kernel, band), grid=(heads,), in_spe...  50.6 us
    ppermute x2, waiting for transfers between devices, swapped(): lax.ppermute(passed, 'ctx', second)  38.5 us
    pallas_call x2, Pallas kernels, col_attention(): pl.pallas_call(functools.partial(col_kernel, n_parts), grid=(heads, cols...  29.9 us
    all_to_all x2, starting transfers between devices, exchanged(): return lax.all_to_all(x, 'ctx', 0, 0, tiled=True)  18.3 us
    ppermute x7, waiting for transfers between devices, body(): lax.ppermute(part, 'ctx', pairs)  12.5 us
    ppermute x7, starting transfers between devices, body(): lax.ppermute(part, 'ctx', pairs)  8.45 us
    pallas_call x2, Pallas kernels, unpacked(): pl.pallas_call(functools.partial(unpack_kernel, in_parts, n, start), in_s...  6.37 us
    ppermute x2, starting transfers between devices, swapped(): outer_v = lax.ppermute(outer_v, 'ctx', near + back(near) + first)  6.25 us
  transfers between devices with their start and end apart: 17, of which 6 were waited for; matrix products, arithmetic and copies ran while one was open for 3% of the time, Pallas kernels for 43%

profile of v6, /device:TPU:11, one launch (start us, length us, event | category | flops | bytes accessed | tf_op | source)
XLA Modules:
  0.0 207.3 jit_solution(17751414181290569451)
XLA Ops:
  0.7 2.1 constant_dynamic-slice_fusion
  2.7 0.1 pad_maximum_fusion
  2.9 4.1 %collective-permute-start.2 = (bf16[512,768]{1,0:T(8,128)(2,1)S(1)}, bf16[512,768]{1,0:T(8,128)(2,1)}, u32[]{:S(2)}, u32[]{:S(2)}) collective-permute-start(bf16[512,768]{1,0:T(8,128)(2,1)S(1)} %get-tuple-element.58), channel_id=1, source_target_pairs={{4,8},{20,24},{8,4},{24,20},{12,28},{16,0},{5,9},{21,25},{9,5},{25... | collective-permute-start | bytes 2359304 | tf_op jit(solution)/shard_map/ppermute | solution.py:335
  6.9 0.0 collective-permute-start
  6.9 3.2 %collective-permute-start.1 = (bf16[512,768]{1,0:T(8,128)(2,1)S(1)}, bf16[512,768]{1,0:T(8,128)(2,1)}, u32[]{:S(2)}, u32[]{:S(2)}) collective-permute-start(bf16[512,768]{1,0:T(8,128)(2,1)S(1)} %get-tuple-element.53), channel_id=1, source_target_pairs={{4,8},{12,16},{20,24},{8,4},{16,12},{24,20},{5,9},{13,17},{21,25},... | collective-permute-start | bytes 2359304 | tf_op jit(solution)/shard_map/ppermute | solution.py:336
  10.1 0.0 copy-start.6
  10.1 5.5 %pack.1 = bf16[8,4,8,16,768]{4,3,2,1,0:T(8,128)(2,1)} custom-call(bf16[8,128,768]{2,1,0:T(8,128)(2,1)} %bitcast.22, bf16[8,128,768]{2,1,0:T(8,128)(2,1)} %bitcast.23, bf16[8,128,768]{2,1,0:T(8,128)(2,1)} %bitcast.24, bf16[8,128,768]{2,1,0:T(8,128)(2,1)} %bitcast.25), custom_call_target="tpu_custom_call" | custom-call | bytes 12582912 | tf_op jit(solution)/shard_map/pack/pallas_call | solution.py:252
  15.6 0.0 collective-permute-done.2.outer_v
  15.6 1.3 collective-permute-start.3
  16.9 0.0 copy-done.6
  16.9 0.7 copy.22.mask
  17.7 0.6 pad_add_fusion.place
  18.2 9.0 %all-to-all-start = ((bf16[8,4,8,16,768]{4,3,2,1,0:T(8,128)(2,1)}), bf16[8,4,8,16,768]{4,3,2,1,0:T(8,128)(2,1)}, u32[]{:S(2)}, u32[]{:S(2)}) async-start(bf16[8,4,8,16,768]{4,3,2,1,0:T(8,128)(2,1)} %pack.1), calls=%async_computation | async-start | bytes 12582912 | tf_op jit(solution)/shard_map/all_to_all | solution.py:342
  27.2 2.5 %collective-permute-done.1.outer_k = bf16[512,768]{1,0:T(8,128)(2,1)} collective-permute-done((bf16[512,768]{1,0:T(8,128)(2,1)S(1)}, bf16[512,768]{1,0:T(8,128)(2,1)}, u32[]{:S(2)}, u32[]{:S(2)}) %collective-permute-start.1) | collective-permute-done | bytes 786464 | tf_op jit(solution)/shard_map/ppermute | solution.py:336
  29.7 0.0 collective-permute-done.inner_kv
  29.7 8.2 %collective-permute-done.3.far_v = bf16[512,768]{1,0:T(8,128)(2,1)S(1)} collective-permute-done((bf16[512,768]{1,0:T(8,128)(2,1)}, bf16[512,768]{1,0:T(8,128)(2,1)S(1)}, u32[]{:S(2)}, u32[]{:S(2)}) %collective-permute-start.3) | collective-permute-done | bytes 786464 | tf_op jit(solution)/shard_map/ppermute | solution.py:338
  37.9 0.0 copy-start.7
  37.9 0.9 copy-done.7
  38.8 50.6 %row_heads.1 = (bf16[1024,768]{1,0:T(8,128)(2,1)}, bf16[1024,768]{1,0:T(8,128)(2,1)}, f32[1024,768]{1,0:T(8,128)}, f32[1024,768]{1,0:T(8,128)}, bf16[2,512,768]{...) custom-call(s32[3]{0:T(128)} %pad_add_fusion.place, s32[64,9]{1,0:T(8,128)} %copy.22.mask, ...), custom_call_target="tpu_custom_call" | custom-call | flops 241591910400 | bytes 23592960 | tf_op jit(solution)/shard_map/row_heads/pallas_call | solution.py:121
  89.4 1.9 collective-permute-start.5
  91.3 2.2 %collective-permute-start.6 = (bf16[512,768]{1,0:T(8,128)(2,1)}, bf16[512,768]{1,0:T(8,128)(2,1)}, u32[]{:S(2)}, u32[]{:S(2)}) collective-permute-start(bf16[512,768]{1,0:T(8,128)(2,1)} %get-tuple-element.78), channel_id=1, source_target_pairs={{4,8},{20,24},{8,4},{24,20},{12,28},{16,0},{5,9},{21,25},{9,5},{25... | collective-permute-start | bytes 2359304 | tf_op jit(solution)/shard_map/ppermute | solution.py:335
  93.5 0.0 collective-permute-start.4
  93.5 3.1 %all-to-all-done.x = bf16[8,4,8,16,768]{4,3,2,1,0:T(8,128)(2,1)} async-done(((bf16[8,4,8,16,768]{4,3,2,1,0:T(8,128)(2,1)}), bf16[8,4,8,16,768]{4,3,2,1,0:T(8,128)(2,1)}, u32[]{:S(2)}, u32[]{:S(2)}) %all-to-all-start) | async-done | bytes 6291488 | tf_op jit(solution)/shard_map/all_to_all | solution.py:342
  96.6 14.8 %col_heads.2.earlier = bf16[8,4,8,16,384]{4,3,2,1,0:T(8,128)(2,1)} custom-call(s32[1]{0:T(128)} %bitcast.9.me, s32[64,64]{1,0:T(8,128)} %mask.4, bf16[8,4,8,16,768]{4,3,2,1,0:T(8,128)(2,1)} %all-to-all-done.x, bf16[1024,768]{1,0:T(8,128)(2,1)} %get-tuple-element.44.earlier), custom_call_target="tpu_custom_call" | custom-call | flops 48318382080 | bytes 12582912 | tf_op jit(solution)/shard_map/col_heads/pallas_call | solution.py:203
  111.4 3.1 %collective-permute-done.5 = bf16[512,768]{1,0:T(8,128)(2,1)S(1)} collective-permute-done((bf16[512,768]{1,0:T(8,128)(2,1)}, bf16[512,768]{1,0:T(8,128)(2,1)S(1)}, u32[]{:S(2)}, u32[]{:S(2)}) %collective-permute-start.5) | collective-permute-done | bytes 786464 | tf_op jit(solution)/shard_map/ppermute | solution.py:336
  114.5 0.0 copy-start.4
  114.5 0.0 collective-permute-done.4
  114.5 0.0 copy-start.3
  114.5 0.9 copy-done.4
  115.4 0.5 copy-done.3
  115.9 9.3 %all-to-all-start.1 = ((bf16[8,4,8,16,384]{4,3,2,1,0:T(8,128)(2,1)}), bf16[8,4,8,16,384]{4,3,2,1,0:T(8,128)(2,1)S(1)}, u32[]{:S(2)}, u32[]{:S(2)}) async-start(bf16[8,4,8,16,384]{4,3,2,1,0:T(8,128)(2,1)} %col_heads.2.earlier), calls=%async_computation.1 | async-start | bytes 6291456 | tf_op jit(solution)/shard_map/all_to_all | solution.py:342
  125.2 15.1 %col_heads.3 = (bf16[4,8,16,384]{3,2,1,0:T(8,128)(2,1)}, bf16[4,8,16,384]{3,2,1,0:T(8,128)(2,1)}, bf16[4,8,16,384]{3,2,1,0:T(8,128)(2,1)}, bf16[4,8,16,384]{3,2,...) custom-call(s32[1]{0:T(128)} %bitcast.9.me, ...), custom_call_target="tpu_custom_call" | custom-call | flops 48318382080 | bytes 12582912 | tf_op jit(solution)/shard_map/col_heads/pallas_call | solution.py:203
  140.3 0.0 collective-permute-done.6
  140.3 1.3 collective-permute-start.7
  141.6 0.9 collective-permute-start.8
  142.5 2.5 %collective-permute-start.9 = (bf16[4,8,16,384]{3,2,1,0:T(8,128)(2,1)}, bf16[4,8,16,384]{3,2,1,0:T(8,128)(2,1)}, u32[]{:S(2)}, u32[]{:S(2)}) collective-permute-start(bf16[4,8,16,384]{3,2,1,0:T(8,128)(2,1)} %get-tuple-element.82), channel_id=1, source_target_pairs={{0,8},{4,12},{8,0},{12,4},{16,24},{20,28},{24,16},{28,20},{1,9},{5... | collective-permute-start | bytes 1179656 | tf_op jit(solution)/shard_map/ppermute | solution.py:382
  145.0 0.0 collective-permute-start.10
  145.0 2.0 collective-permute-start.11
  147.0 30.3 %collective-permute-done.7 = bf16[512,768]{1,0:T(8,128)(2,1)} collective-permute-done((bf16[512,768]{1,0:T(8,128)(2,1)}, bf16[512,768]{1,0:T(8,128)(2,1)}, u32[]{:S(2)}, u32[]{:S(2)}) %collective-permute-start.7) | collective-permute-done | bytes 786464 | tf_op jit(solution)/shard_map/ppermute | solution.py:338
  177.3 0.0 collective-permute-start.12
  177.3 0.0 copy-start.2
  177.3 2.2 %bitcast_select_fusion.1 = (bf16[512,768]{1,0:T(8,128)(2,1)S(1)}, bf16[512,768]{1,0:T(8,128)(2,1)S(1)}, bf16[512,768]{1,0:T(8,128)(2,1)S(1)}, bf16[512,768]{1,0:T(8,128)(2,1)S(1)}) fusion(pred[]{:T(512)S(6)} %eq.17, bf16[2,512,768]{2,1,0:T(8,128)(2,1)} %copy-done.3, bf16[512,768]{1,0:T(8,128)(2,1)} %collective-permute-done.7, ...), kind=kLoop, calls=%fused_computation.4 | loop fusion | flops 1966080 | bytes 7077890 | tf_op jit(solution)/shard_map/jit(_where)/select_n | solution.py:396
  179.6 0.0 collective-permute-done.8.refs_1_
  179.6 0.0 copy-start.5
  179.6 1.0 collective-permute-start.13
  180.6 0.0 collective-permute-done.9.refs_2_
  180.6 2.1 %collective-permute-start.14 = (bf16[4,8,16,384]{3,2,1,0:T(8,128)(2,1)}, bf16[4,8,16,384]{3,2,1,0:T(8,128)(2,1)}, u32[]{:S(2)}, u32[]{:S(2)}) collective-permute-start(bf16[4,8,16,384]{3,2,1,0:T(8,128)(2,1)} %get-tuple-element.87), channel_id=1, source_target_pairs={{0,28},{4,24},{8,20},{12,16},{16,12},{20,8},{24,4},{28,0},{1,29},{... | collective-permute-start | bytes 1179656 | tf_op jit(solution)/shard_map/ppermute | solution.py:382
  182.7 0.0 copy-done.2
  182.7 0.0 copy-start.1
  182.7 1.5 add_convert_fusion.1
  184.2 0.0 copy-done.5
  184.2 1.0 copy-done.1
  185.1 1.5 add_convert_fusion
  186.6 0.0 all-to-all-done.1.refs_0_
  186.6 0.0 copy-start
  186.6 1.6 copy-done
  188.3 3.2 %unpack.2 = (bf16[8,128,768]{2,1,0:T(8,128)(2,1)}, bf16[8,128,768]{2,1,0:T(8,128)(2,1)}, bf16[8,128,768]{2,1,0:T(8,128)(2,1)}, bf16[8,128,768]{2,1,0:T(8,128)(2,1)}) custom-call(s32[1]{0:T(128)} %bitcast.9.me, bf16[8,4,8,16,384]{4,3,2,1,0:T(8,128)(2,1)} %copy-done), custom_call_target="tpu_custom_call" | custom-call | bytes 6291456 | tf_op jit(solution)/shard_map/unpack/pallas_call | solution.py:305
  191.4 0.0 collective-permute-done.10.refs_3_
  191.5 0.0 collective-permute-done.11.refs_4_
  191.5 12.5 %collective-permute-done.12.refs_5_ = bf16[4,8,16,384]{3,2,1,0:T(8,128)(2,1)} collective-permute-done((bf16[4,8,16,384]{3,2,1,0:T(8,128)(2,1)}, bf16[4,8,16,384]{3,2,1,0:T(8,128)(2,1)}, u32[]{:S(2)}, u32[]{:S(2)}) %collective-permute-start.12) | collective-permute-done | bytes 393248 | tf_op jit(solution)/shard_map/ppermute | solution.py:382
  204.0 0.0 collective-permute-done.13.refs_6_
  204.0 0.0 collective-permute-done.14.refs_7_
  204.0 3.2 %unpack.3 = (bf16[8,128,768]{2,1,0:T(8,128)(2,1)}, bf16[8,128,768]{2,1,0:T(8,128)(2,1)}, bf16[8,128,768]{2,1,0:T(8,128)(2,1)}, bf16[8,128,768]{2,1,0:T(8,128)(2,1)}) custom-call(s32[1]{0:T(128)} %bitcast.9.me, bf16[4,8,16,384]{3,2,1,0:T(8,128)(2,1)} %get-tuple-element.80.refs_0_, ...), custom_call_target="tpu_custom_call", output_to_operand_aliasing={{0}: (9, {}), {1}: (10, {}), {2}: (11, {}), {3}: (12, {})} | custom-call | bytes 6291456 | tf_op jit(solution)/shard_map/unpack/pallas_call | solution.py:305
Async XLA Ops:
  2.9 12.7 %collective-permute-start.2 = (bf16[512,768]{1,0:T(8,128)(2,1)S(1)}, bf16[512,768]{1,0:T(8,128)(2,1)}, u32[]{:S(2)}, u32[]{:S(2)}) collective-permute-start(bf16[512,768]{1,0:T(8,128)(2,1)S(1)} %get-tuple-element.58), channel_id=1, source_target_pairs={{4,8},{20,24},{8,4},{24,20},{12,28},{16,0},{5,9},{21,25},{9,5},{25... | collective-permute-start | bytes 2359304 | tf_op jit(solution)/shard_map/ppermute | solution.py:335
  6.9 22.8 %collective-permute-start = (bf16[2,512,768]{2,1,0:T(8,128)(2,1)S(1)}, bf16[2,512,768]{2,1,0:T(8,128)(2,1)}, u32[]{:S(2)}, u32[]{:S(2)}) collective-permute-start(bf16[2,512,768]{2,1,0:T(8,128)(2,1)S(1)} %pad_maximum_fusion), channel_id=1, source_target_pairs={{0,4},{4,0},{8,12},{12,8},{16,20},{20,16},{24,28},{28,24},{1,5},{5... | collective-permute-start | bytes 4718600 | tf_op jit(solution)/shard_map/ppermute | solution.py:337
  6.9 22.8 %collective-permute-start.1 = (bf16[512,768]{1,0:T(8,128)(2,1)S(1)}, bf16[512,768]{1,0:T(8,128)(2,1)}, u32[]{:S(2)}, u32[]{:S(2)}) collective-permute-start(bf16[512,768]{1,0:T(8,128)(2,1)S(1)} %get-tuple-element.53), channel_id=1, source_target_pairs={{4,8},{12,16},{20,24},{8,4},{16,12},{24,20},{5,9},{13,17},{21,25},... | collective-permute-start | bytes 2359304 | tf_op jit(solution)/shard_map/ppermute | solution.py:336
  10.1 6.8 %copy-start.6 = (s32[64,9]{0,1:T(8,128)S(1)}, s32[64,9]{0,1:T(8,128)}, u32[]{:S(2)}) copy-start(s32[64,9]{0,1:T(8,128)} %param.14) | copy-start | bytes 6916
  15.6 22.3 %collective-permute-start.3 = (bf16[512,768]{1,0:T(8,128)(2,1)}, bf16[512,768]{1,0:T(8,128)(2,1)S(1)}, u32[]{:S(2)}, u32[]{:S(2)}) collective-permute-start(bf16[512,768]{1,0:T(8,128)(2,1)} %collective-permute-done.2.outer_v), channel_id=1, source_target_pairs={{28,16},{0,12},{29,17},{1,13},{30,18},{2,14},{31,19},{3,15}} | collective-permute-start | bytes 2359304 | tf_op jit(solution)/shard_map/ppermute | solution.py:338
  18.2 78.4 %all-to-all-start = ((bf16[8,4,8,16,768]{4,3,2,1,0:T(8,128)(2,1)}), bf16[8,4,8,16,768]{4,3,2,1,0:T(8,128)(2,1)}, u32[]{:S(2)}, u32[]{:S(2)}) async-start(bf16[8,4,8,16,768]{4,3,2,1,0:T(8,128)(2,1)} %pack.1), calls=%async_computation | async-start | bytes 12582912 | tf_op jit(solution)/shard_map/all_to_all | solution.py:342
  37.9 0.9 copy-start.7
  89.4 25.1 %collective-permute-start.5 = (bf16[512,768]{1,0:T(8,128)(2,1)}, bf16[512,768]{1,0:T(8,128)(2,1)S(1)}, u32[]{:S(2)}, u32[]{:S(2)}) collective-permute-start(bf16[512,768]{1,0:T(8,128)(2,1)} %get-tuple-element.65), channel_id=1, source_target_pairs={{4,8},{12,16},{20,24},{8,4},{16,12},{24,20},{5,9},{13,17},{21,25},... | collective-permute-start | bytes 2359304 | tf_op jit(solution)/shard_map/ppermute | solution.py:336
  91.3 49.0 %collective-permute-start.6 = (bf16[512,768]{1,0:T(8,128)(2,1)}, bf16[512,768]{1,0:T(8,128)(2,1)}, u32[]{:S(2)}, u32[]{:S(2)}) collective-permute-start(bf16[512,768]{1,0:T(8,128)(2,1)} %get-tuple-element.78), channel_id=1, source_target_pairs={{4,8},{20,24},{8,4},{24,20},{12,28},{16,0},{5,9},{21,25},{9,5},{25... | collective-permute-start | bytes 2359304 | tf_op jit(solution)/shard_map/ppermute | solution.py:335
  93.5 21.0 %collective-permute-start.4 = (bf16[2,512,768]{2,1,0:T(8,128)(2,1)}, bf16[2,512,768]{2,1,0:T(8,128)(2,1)S(1)}, u32[]{:S(2)}, u32[]{:S(2)}) collective-permute-start(bf16[2,512,768]{2,1,0:T(8,128)(2,1)} %get-tuple-element.64), channel_id=1, source_target_pairs={{0,4},{4,0},{8,12},{12,8},{16,20},{20,16},{24,28},{28,24},{1,5},{5... | collective-permute-start | bytes 4718600 | tf_op jit(solution)/shard_map/ppermute | solution.py:337
  114.5 0.9 copy-start.4
  114.5 1.4 copy-start.3
  115.9 70.7 %all-to-all-start.1 = ((bf16[8,4,8,16,384]{4,3,2,1,0:T(8,128)(2,1)}), bf16[8,4,8,16,384]{4,3,2,1,0:T(8,128)(2,1)S(1)}, u32[]{:S(2)}, u32[]{:S(2)}) async-start(bf16[8,4,8,16,384]{4,3,2,1,0:T(8,128)(2,1)} %col_heads.2.earlier), calls=%async_computation.1 | async-start | bytes 6291456 | tf_op jit(solution)/shard_map/all_to_all | solution.py:342
  140.3 37.0 %collective-permute-start.7 = (bf16[512,768]{1,0:T(8,128)(2,1)}, bf16[512,768]{1,0:T(8,128)(2,1)}, u32[]{:S(2)}, u32[]{:S(2)}) collective-permute-start(bf16[512,768]{1,0:T(8,128)(2,1)} %collective-permute-done.6), channel_id=1, source_target_pairs={{28,16},{0,12},{29,17},{1,13},{30,18},{2,14},{31,19},{3,15}} | collective-permute-start | bytes 2359304 | tf_op jit(solution)/shard_map/ppermute | solution.py:338
  141.6 37.9 %collective-permute-start.8 = (bf16[4,8,16,384]{3,2,1,0:T(8,128)(2,1)}, bf16[4,8,16,384]{3,2,1,0:T(8,128)(2,1)S(1)}, u32[]{:S(2)}, u32[]{:S(2)}) collective-permute-start(bf16[4,8,16,384]{3,2,1,0:T(8,128)(2,1)} %get-tuple-element.81), channel_id=1, source_target_pairs={{0,4},{4,0},{8,12},{12,8},{16,20},{20,16},{24,28},{28,24},{1,5},{5... | collective-permute-start | bytes 1179656 | tf_op jit(solution)/shard_map/ppermute | solution.py:382
  142.5 38.1 %collective-permute-start.9 = (bf16[4,8,16,384]{3,2,1,0:T(8,128)(2,1)}, bf16[4,8,16,384]{3,2,1,0:T(8,128)(2,1)}, u32[]{:S(2)}, u32[]{:S(2)}) collective-permute-start(bf16[4,8,16,384]{3,2,1,0:T(8,128)(2,1)} %get-tuple-element.82), channel_id=1, source_target_pairs={{0,8},{4,12},{8,0},{12,4},{16,24},{20,28},{24,16},{28,20},{1,9},{5... | collective-permute-start | bytes 1179656 | tf_op jit(solution)/shard_map/ppermute | solution.py:382
  145.0 46.4 %collective-permute-start.10 = (bf16[4,8,16,384]{3,2,1,0:T(8,128)(2,1)}, bf16[4,8,16,384]{3,2,1,0:T(8,128)(2,1)}, u32[]{:S(2)}, u32[]{:S(2)}) collective-permute-start(bf16[4,8,16,384]{3,2,1,0:T(8,128)(2,1)} %get-tuple-element.83), channel_id=1, source_target_pairs={{0,12},{4,8},{8,4},{12,0},{16,28},{20,24},{24,20},{28,16},{1,13},{... | collective-permute-start | bytes 1179656 | tf_op jit(solution)/shard_map/ppermute | solution.py:382
  145.0 46.4 %collective-permute-start.11 = (bf16[4,8,16,384]{3,2,1,0:T(8,128)(2,1)}, bf16[4,8,16,384]{3,2,1,0:T(8,128)(2,1)}, u32[]{:S(2)}, u32[]{:S(2)}) collective-permute-start(bf16[4,8,16,384]{3,2,1,0:T(8,128)(2,1)} %get-tuple-element.84), channel_id=1, source_target_pairs={{0,16},{4,20},{8,24},{12,28},{16,0},{20,4},{24,8},{28,12},{1,17},{... | collective-permute-start | bytes 1179656 | tf_op jit(solution)/shard_map/ppermute | solution.py:382
  177.3 26.6 %collective-permute-start.12 = (bf16[4,8,16,384]{3,2,1,0:T(8,128)(2,1)}, bf16[4,8,16,384]{3,2,1,0:T(8,128)(2,1)}, u32[]{:S(2)}, u32[]{:S(2)}) collective-permute-start(bf16[4,8,16,384]{3,2,1,0:T(8,128)(2,1)} %get-tuple-element.85), channel_id=1, source_target_pairs={{0,20},{4,16},{8,28},{12,24},{16,4},{20,0},{24,12},{28,8},{1,21},{... | collective-permute-start | bytes 1179656 | tf_op jit(solution)/shard_map/ppermute | solution.py:382
  177.3 5.3 %copy-start.2 = (f32[1024,768]{1,0:T(8,128)S(1)}, f32[1024,768]{1,0:T(8,128)}, u32[]{:S(2)}) copy-start(f32[1024,768]{1,0:T(8,128)} %get-tuple-element.62) | copy-start | bytes 9437188
  179.6 4.6 %copy-start.5 = (bf16[4,8,16,384]{3,2,1,0:T(8,128)(2,1)}, bf16[4,8,16,384]{3,2,1,0:T(8,128)(2,1)S(1)}, u32[]{:S(2)}) copy-start(bf16[4,8,16,384]{3,2,1,0:T(8,128)(2,1)S(1)} %collective-permute-done.8.refs_1_) | copy-start | bytes 1179652
  179.6 24.4 %collective-permute-start.13 = (bf16[4,8,16,384]{3,2,1,0:T(8,128)(2,1)}, bf16[4,8,16,384]{3,2,1,0:T(8,128)(2,1)}, u32[]{:S(2)}, u32[]{:S(2)}) collective-permute-start(bf16[4,8,16,384]{3,2,1,0:T(8,128)(2,1)} %get-tuple-element.86), channel_id=1, source_target_pairs={{0,24},{4,28},{8,16},{12,20},{16,8},{20,12},{24,0},{28,4},{1,25},{... | collective-permute-start | bytes 1179656 | tf_op jit(solution)/shard_map/ppermute | solution.py:382
  180.6 23.4 %collective-permute-start.14 = (bf16[4,8,16,384]{3,2,1,0:T(8,128)(2,1)}, bf16[4,8,16,384]{3,2,1,0:T(8,128)(2,1)}, u32[]{:S(2)}, u32[]{:S(2)}) collective-permute-start(bf16[4,8,16,384]{3,2,1,0:T(8,128)(2,1)} %get-tuple-element.87), channel_id=1, source_target_pairs={{0,28},{4,24},{8,20},{12,16},{16,12},{20,8},{24,4},{28,0},{1,29},{... | collective-permute-start | bytes 1179656 | tf_op jit(solution)/shard_map/ppermute | solution.py:382
  182.7 2.5 %copy-start.1 = (f32[1024,768]{1,0:T(8,128)S(1)}, f32[1024,768]{1,0:T(8,128)}, u32[]{:S(2)}) copy-start(f32[1024,768]{1,0:T(8,128)} %get-tuple-element.68) | copy-start | bytes 9437188
  186.6 1.6 copy-start

commit v7 on v6

--- a/solution.py
+++ b/solution.py
@@ -267,56 +267,51 @@
     )(*(a.reshape(rows, GRIDC, feat) for a in arrays))
 
 
-def unpack_kernel(in_parts, n, start, me, *refs):
+def unpack_kernel(partners, start, me, *refs):
     held, arrived, left = refs[-3:]
-    k, _, _, width = held.shape
+    count, k, _, cols, width = held.shape
     outs = refs[-3 - k : -3]
-    cols = GRIDC // n
     loads, stores = [], []
-    for a, out in enumerate(outs):
-        for i in range(n):
-            if in_parts:
-                part, source = refs[i], me[0] ^ i
-            else:
-                part, source = refs[0].at[i], i
-            here = pl.ds(pl.multiple_of(source * cols, cols), cols)
-            loads.append(
-                pltpu.make_async_copy(part.at[a], held.at[a, :, here, :], arrived.at[a, i])
+    for i in range(count):
+        part, source = (refs[0].at[i], i) if partners is None else (refs[i], me[0] ^ partners[i])
+        here = pl.ds(pl.multiple_of(source * cols, cols), cols)
+        loads.append(pltpu.make_async_copy(part, held.at[i], arrived.at[i]))
+        stores += [
+            pltpu.make_async_copy(
+                held.at[i, a], out.at[:, here, start : start + width], left.at[i, a]
             )
-        stores.append(
-            pltpu.make_async_copy(held.at[a], out.at[:, :, start : start + width], left.at[a])
-        )
+            for a, out in enumerate(outs)
+        ]
     for load in loads:
         load.start()
-    for a, store in enumerate(stores):
-        for load in loads[a * n : (a + 1) * n]:
-            load.wait()
-        store.start()
+    for i, load in enumerate(loads):
+        load.wait()
+        for store in stores[i * k : (i + 1) * k]:
+            store.start()
     for store in stores:
         store.wait()
 
 
-def unpacked(me, parts, start, feat, kept):
-    in_parts = isinstance(parts, list)
-    parts = parts if in_parts else [parts]
+def unpacked(me, parts, partners, start, feat, kept):
+    parts = [parts] if partners is None else parts
     k, rows, cols, width = parts[0].shape[-4:]
-    n = GRIDC // cols
+    count = GRIDC // cols if partners is None else len(parts)
     kept = [a.reshape(rows, GRIDC, feat) for a in kept]
     outs = pl.pallas_call(
-        functools.partial(unpack_kernel, in_parts, n, start),
+        functools.partial(unpack_kernel, partners, start),
         in_specs=[pl.BlockSpec(memory_space=pltpu.SMEM)]
         + [pl.BlockSpec(memory_space=pl.ANY)] * (len(parts) + len(kept)),
         out_specs=[pl.BlockSpec(memory_space=pl.ANY)] * k,
         out_shape=[jax.ShapeDtypeStruct((rows, GRIDC, feat), jnp.bfloat16)] * k,
         scratch_shapes=[
-            pltpu.VMEM((k, rows, GRIDC, width), jnp.bfloat16),
-            pltpu.SemaphoreType.DMA((k, n)),
-            pltpu.SemaphoreType.DMA((k,)),
+            pltpu.VMEM((count, k, rows, cols, width), jnp.bfloat16),
+            pltpu.SemaphoreType.DMA((count,)),
+            pltpu.SemaphoreType.DMA((count, k)),
         ],
         input_output_aliases={1 + len(parts) + a: a for a in range(len(kept))},
         compiler_params=pltpu.CompilerParams(vmem_limit_bytes=VMEM),
         cost_estimate=pl.CostEstimate(
-            flops=0, bytes_accessed=4 * k * rows * GRIDC * width, transcendentals=0
+            flops=0, bytes_accessed=4 * k * rows * count * cols * width, transcendentals=0
         ),
         name="unpack",
     )(me, *parts, *kept)
@@ -358,10 +353,11 @@
     side = me % CHIPS_APART
     inner_at, outer_at = (1 - odd) * (tokens - rim), odd * (tokens - rim)
     rim_of = lambda x, at: lax.dynamic_slice_in_dim(x, at, rim, 0)
-    inner = jnp.stack([rim_of(row_key, inner_at), rim_of(row_value, inner_at)])
-    outer_k, outer_v = rim_of(row_key, outer_at), rim_of(row_value, outer_at)
     cols = [col_query, col_key, col_value, col_cotangent]
-    inner, outer_k, outer_v, cols = lax.optimization_barrier((inner, outer_k, outer_v, cols))
+    outer_v = rim_of(row_value, outer_at)
+    outer_v, key, value, cols = lax.optimization_barrier((outer_v, row_key, row_value, cols))
+    outer_k = rim_of(key, outer_at)
+    inner = jnp.stack([rim_of(key, inner_at), rim_of(value, inner_at)])
     inner, outer_k, outer_v, second_hop = swapped(inner, outer_k, outer_v)
     sent, outer_v = lax.optimization_barrier((packed(cols, n), outer_v))
     halos = [inner, outer_k, outer_v, second_hop(outer_v)]
@@ -375,20 +371,25 @@
     inner, outer_k, outer_v, second_hop = swapped(*sides)
 
     heads = col_query.shape[1] // HEAD_DIM
-    half = heads // 2
+    half = heads // 3
     where = me.reshape(1)
     partners = [[(i, i ^ k) for i in range(n)] for k in range(n)]
-    send = lambda parts: [parts[0]] + [
-        lax.ppermute(part, "ctx", pairs) for part, pairs in zip(parts[1:], partners[1:])
-    ]
     first = col_attention(where, col_mask, moved, row_output, 0, half, False)
     first, inner, outer_k = lax.optimization_barrier((first, inner, outer_k))
     second = col_attention(where, col_mask, moved, first, half, heads - half, True)
     second, outer_v = lax.optimization_barrier((second, outer_v))
-    first, second = exchanged(first), send(second)
+    first = exchanged(first)
+    arrived = [second[0]] + [
+        lax.ppermute(second[k], "ctx", partners[k]) for k in range(1, n - 2)
+    ]
+    *last, arrived[2] = lax.optimization_barrier((second[n - 2], second[n - 1], arrived[2]))
+    arrived += [lax.ppermute(part, "ctx", pairs) for part, pairs in zip(last, partners[n - 2 :])]
     col_feat = col_query.shape[1]
-    col_results = unpacked(where, first, 0, col_feat, [])
-    col_results = unpacked(where, second, half * HEAD_DIM, col_feat, col_results)
+    col_results = unpacked(where, first, None, 0, col_feat, [])
+    for some in (list(range(n - 2)), [n - 2, n - 1]):
+        col_results = unpacked(
+            where, [arrived[k] for k in some], some, half * HEAD_DIM, col_feat, col_results
+        )
 
     outer_v = jnp.where(is_far, second_hop(outer_v), outer_v)
     row_grads = []

time: 210 us -> 211 us (level)
  the two profiles are of different devices: /device:TPU:11 before, /device:TPU:0 now
where the time goes in v7:
time: 211 us
  Pallas kernels  93.7 us (44%)
  waiting for transfers between devices  64.3 us (30%)
  starting transfers between devices  38.4 us (18%)
  local copies, waits for them, and re-layouts  8.03 us (4%)
  other arithmetic  5.16 us (2%)
    pallas_call x1, Pallas kernels, row_attention(): pl.pallas_call(functools.partial(row_kernel, band), grid=(heads,), in_spe...  50.6 us
    ppermute x5, waiting for transfers between devices, body(): lax.ppermute(second[k], 'ctx', partners[k])  41.9 us
    pallas_call x2, Pallas kernels, col_attention(): pl.pallas_call(functools.partial(col_kernel, n_parts), grid=(heads, cols...  30 us
    all_to_all x2, waiting for transfers between devices, exchanged(): return lax.all_to_all(x, 'ctx', 0, 0, tiled=True)  11.1 us
    all_to_all x2, starting transfers between devices, exchanged(): return lax.all_to_all(x, 'ctx', 0, 0, tiled=True)  10.7 us
    ppermute x2, waiting for transfers between devices, swapped(): lax.ppermute(passed, 'ctx', second)  10.1 us
    ppermute x2, starting transfers between devices, swapped(): lax.ppermute(passed, 'ctx', second)  9.28 us
    ppermute x2, starting transfers between devices, swapped(): inner = lax.ppermute(inner, 'ctx', [(i, i ^ 1) for i in range(n)])  7.86 us
  transfers between devices with their start and end apart: 17, of which 5 were waited for; matrix products, arithmetic and copies ran while one was open for 3% of the time, Pallas kernels for 44%

profile of v7, /device:TPU:0, one launch (start us, length us, event | category | flops | bytes accessed | tf_op | source)
XLA Modules:
  0.0 210.7 jit_solution(3113969946232637625)
XLA Ops:
  0.6 0.0 copy-start.4
  0.7 0.0 copy-start.3
  0.7 2.2 %constant_dynamic-slice_fusion.1 = bf16[512,768]{1,0:T(8,128)(2,1)} fusion(bf16[1024,768]{1,0:T(8,128)(2,1)} %v.1, s32[]{:T(128)S(6)} %select_n.47), kind=kLoop, calls=%fused_computation.11 | loop fusion | bytes 1572868 | tf_op jit(solution)/shard_map/dynamic_slice | solution.py:355
  2.9 1.3 collective-permute-start.2
  4.2 0.0 copy-done.4
  4.2 0.1 dynamic-slice_bitcast_fusion
  4.3 0.0 copy-done.3
  4.3 1.0 constant_dynamic-slice_fusion
  5.3 0.1 pad_maximum_fusion
  5.4 3.7 %collective-permute-start = (bf16[2,512,768]{2,1,0:T(8,128)(2,1)S(1)}, bf16[2,512,768]{2,1,0:T(8,128)(2,1)S(1)}, u32[]{:S(2)}, u32[]{:S(2)}) collective-permute-start(bf16[2,512,768]{2,1,0:T(8,128)(2,1)S(1)} %pad_maximum_fusion), channel_id=1, source_target_pairs={{0,4},{4,0},{8,12},{12,8},{16,20},{20,16},{24,28},{28,24},{1,5},{5... | collective-permute-start | bytes 4718600 | tf_op jit(solution)/shard_map/ppermute | solution.py:332
  9.2 1.6 collective-permute-start.1
  10.7 0.0 copy-start.7
  10.7 5.5 %pack.1 = bf16[8,4,8,16,768]{4,3,2,1,0:T(8,128)(2,1)} custom-call(bf16[8,128,768]{2,1,0:T(8,128)(2,1)} %bitcast.26, bf16[8,128,768]{2,1,0:T(8,128)(2,1)} %bitcast.27, bf16[8,128,768]{2,1,0:T(8,128)(2,1)} %bitcast.28, bf16[8,128,768]{2,1,0:T(8,128)(2,1)} %bitcast.29), custom_call_target="tpu_custom_call" | custom-call | bytes 12582912 | tf_op jit(solution)/shard_map/pack/pallas_call | solution.py:252
  16.2 1.2 collective-permute-done.2.outer_v
  17.4 4.7 %collective-permute-start.3 = (bf16[512,768]{1,0:T(8,128)(2,1)}, bf16[512,768]{1,0:T(8,128)(2,1)}, u32[]{:S(2)}, u32[]{:S(2)}) collective-permute-start(bf16[512,768]{1,0:T(8,128)(2,1)} %collective-permute-done.2.outer_v), channel_id=1, source_target_pairs={{28,16},{0,12},{29,17},{1,13},{30,18},{2,14},{31,19},{3,15}} | collective-permute-start | bytes 2359304 | tf_op jit(solution)/shard_map/ppermute | solution.py:333
  22.1 0.0 copy-done.7
  22.1 0.7 copy.26.mask
  22.8 0.7 pad_add_fusion.place
  23.4 4.8 %all-to-all-start = ((bf16[8,4,8,16,768]{4,3,2,1,0:T(8,128)(2,1)}), bf16[8,4,8,16,768]{4,3,2,1,0:T(8,128)(2,1)}, u32[]{:S(2)}, u32[]{:S(2)}) async-start(bf16[8,4,8,16,768]{4,3,2,1,0:T(8,128)(2,1)} %pack.1), calls=%async_computation | async-start | bytes 12582912 | tf_op jit(solution)/shard_map/all_to_all | solution.py:337
  28.2 0.0 collective-permute-done.1.outer_k
  28.2 0.0 collective-permute-done.inner_kv
  28.2 0.0 copy-start.8
  28.2 10.1 %collective-permute-done.3.far_v = bf16[512,768]{1,0:T(8,128)(2,1)} collective-permute-done((bf16[512,768]{1,0:T(8,128)(2,1)}, bf16[512,768]{1,0:T(8,128)(2,1)}, u32[]{:S(2)}, u32[]{:S(2)}) %collective-permute-start.3) | collective-permute-done | bytes 786464 | tf_op jit(solution)/shard_map/ppermute | solution.py:333
  38.3 0.0 copy-done.8
  38.3 50.6 %row_heads.1 = (bf16[1024,768]{1,0:T(8,128)(2,1)}, bf16[1024,768]{1,0:T(8,128)(2,1)}, f32[1024,768]{1,0:T(8,128)}, f32[1024,768]{1,0:T(8,128)}, bf16[2,512,768]{...) custom-call(s32[3]{0:T(128)} %pad_add_fusion.place, s32[64,9]{1,0:T(8,128)} %copy.26.mask, ...), custom_call_target="tpu_custom_call" | custom-call | flops 241591910400 | bytes 23592960 | tf_op jit(solution)/shard_map/row_heads/pallas_call | solution.py:121
  88.9 0.7 collective-permute-start.5
  89.6 1.3 collective-permute-start.6
  90.9 4.1 %collective-permute-start.4 = (bf16[2,512,768]{2,1,0:T(8,128)(2,1)}, bf16[2,512,768]{2,1,0:T(8,128)(2,1)S(1)}, u32[]{:S(2)}, u32[]{:S(2)}) collective-permute-start(bf16[2,512,768]{2,1,0:T(8,128)(2,1)} %get-tuple-element.71), channel_id=1, source_target_pairs={{0,4},{4,0},{8,12},{12,8},{16,20},{20,16},{24,28},{28,24},{1,5},{5... | collective-permute-start | bytes 4718600 | tf_op jit(solution)/shard_map/ppermute | solution.py:332
  95.0 11.1 %all-to-all-done.x = bf16[8,4,8,16,768]{4,3,2,1,0:T(8,128)(2,1)} async-done(((bf16[8,4,8,16,768]{4,3,2,1,0:T(8,128)(2,1)}), bf16[8,4,8,16,768]{4,3,2,1,0:T(8,128)(2,1)}, u32[]{:S(2)}, u32[]{:S(2)}) %all-to-all-start) | async-done | bytes 6291488 | tf_op jit(solution)/shard_map/all_to_all | solution.py:337
  106.2 10.7 %col_heads.2.earlier = bf16[8,4,8,16,256]{4,3,2,1,0:T(8,128)(2,1)} custom-call(s32[1]{0:T(128)} %bitcast.9.me, s32[64,64]{1,0:T(8,128)} %mask.4, bf16[8,4,8,16,768]{4,3,2,1,0:T(8,128)(2,1)} %all-to-all-done.x, bf16[1024,768]{1,0:T(8,128)(2,1)} %get-tuple-element.51.earlier), custom_call_target="tpu_custom_call" | custom-call | flops 32212254720 | bytes 12582912 | tf_op jit(solution)/shard_map/col_heads/pallas_call | solution.py:203
  116.8 0.0 collective-permute-done.5
  116.8 0.0 collective-permute-done.4
  116.8 0.0 copy-start.5
  116.9 1.1 copy-done.5
  118.0 5.9 %all-to-all-start.1 = ((bf16[8,4,8,16,256]{4,3,2,1,0:T(8,128)(2,1)}), bf16[8,4,8,16,256]{4,3,2,1,0:T(8,128)(2,1)S(1)}, u32[]{:S(2)}, u32[]{:S(2)}) async-start(bf16[8,4,8,16,256]{4,3,2,1,0:T(8,128)(2,1)} %col_heads.2.earlier), calls=%async_computation.1 | async-start | bytes 4194304 | tf_op jit(solution)/shard_map/all_to_all | solution.py:337
  123.9 19.4 %col_heads.3 = (bf16[4,8,16,512]{3,2,1,0:T(8,128)(2,1)}, bf16[4,8,16,512]{3,2,1,0:T(8,128)(2,1)}, bf16[4,8,16,512]{3,2,1,0:T(8,128)(2,1)}, bf16[4,8,16,512]{3,2,...) custom-call(s32[1]{0:T(128)} %bitcast.9.me, ...), custom_call_target="tpu_custom_call" | custom-call | flops 64424509440 | bytes 12582912 | tf_op jit(solution)/shard_map/col_heads/pallas_call | solution.py:203
  143.3 0.0 collective-permute-done.6
  143.3 4.6 %collective-permute-start.7 = (bf16[512,768]{1,0:T(8,128)(2,1)}, bf16[512,768]{1,0:T(8,128)(2,1)}, u32[]{:S(2)}, u32[]{:S(2)}) collective-permute-start(bf16[512,768]{1,0:T(8,128)(2,1)} %collective-permute-done.6), channel_id=1, source_target_pairs={{28,16},{0,12},{29,17},{1,13},{30,18},{2,14},{31,19},{3,15}} | collective-permute-start | bytes 2359304 | tf_op jit(solution)/shard_map/ppermute | solution.py:333
  147.9 0.0 collective-permute-start.8
  148.0 0.0 collective-permute-start.11
  148.0 2.1 %collective-permute-start.12 = (bf16[4,8,16,512]{3,2,1,0:T(8,128)(2,1)}, bf16[4,8,16,512]{3,2,1,0:T(8,128)(2,1)}, u32[]{:S(2)}, u32[]{:S(2)}) collective-permute-start(bf16[4,8,16,512]{3,2,1,0:T(8,128)(2,1)} %get-tuple-element.95), channel_id=1, source_target_pairs={{0,12},{4,8},{8,4},{12,0},{16,28},{20,24},{24,20},{28,16},{1,13},{... | collective-permute-start | bytes 1572872 | tf_op jit(solution)/shard_map/ppermute | solution.py:383
  150.1 0.0 collective-permute-start.13
  150.1 22.9 %collective-permute-done.8.refs_2_ = bf16[4,8,16,512]{3,2,1,0:T(8,128)(2,1)S(1)} collective-permute-done((bf16[4,8,16,512]{3,2,1,0:T(8,128)(2,1)}, bf16[4,8,16,512]{3,2,1,0:T(8,128)(2,1)S(1)}, u32[]{:S(2)}, u32[]{:S(2)}) %collective-permute-start.8) | collective-permute-done | bytes 524320 | tf_op jit(solution)/shard_map/ppermute | solution.py:383
  173.0 0.0 copy-start.6
  173.0 2.9 %collective-permute-start.14 = (bf16[4,8,16,512]{3,2,1,0:T(8,128)(2,1)}, bf16[4,8,16,512]{3,2,1,0:T(8,128)(2,1)}, u32[]{:S(2)}, u32[]{:S(2)}) collective-permute-start(bf16[4,8,16,512]{3,2,1,0:T(8,128)(2,1)} %get-tuple-element.97), channel_id=1, source_target_pairs={{0,20},{4,16},{8,28},{12,24},{16,4},{20,0},{24,12},{28,8},{1,21},{... | collective-permute-start | bytes 1572872 | tf_op jit(solution)/shard_map/ppermute | solution.py:383
  175.8 0.0 collective-permute-done.11.refs_1_
  175.8 0.0 collective-permute-start.9
  175.9 0.0 collective-permute-done.7
  175.9 0.8 collective-permute-start.10
  176.6 2.0 bitcast_select_fusion.1
  178.6 0.0 copy-done.6
  178.6 0.6 copy-done.1
  179.2 1.0 copy-done.2
  180.2 2.4 %add_convert_fusion = (bf16[1024,768]{1,0:T(8,128)(2,1)}, bf16[1024,768]{1,0:T(8,128)(2,1)}) fusion(f32[1024,768]{1,0:T(8,128)S(1)} %copy-done.2, bf16[512,768]{1,0:T(8,128)(2,1)S(1)} %get-tuple-element.111, bf16[512,768]{1,0:T(8,128)(2,1)S(1)} %get-tuple-element.110, f32[1024,768]{1,0:T(8,128)S(1)} %copy-done.1, bf16[512,768]{1,0:T(8,128)(2,1)S(1)} %get-tuple-element.114, ...), kind=kLoop, calls=%fused_computation | loop fusion | flops 7864320 | bytes 12582912 | tf_op jit(solution)/shard_map/convert_element_type | solution.py:401
  182.5 0.0 all-to-all-done.1.refs_0_
  182.5 1.3 copy-done
  183.9 2.6 %unpack.3 = (bf16[8,128,768]{2,1,0:T(8,128)(2,1)}, bf16[8,128,768]{2,1,0:T(8,128)(2,1)}, bf16[8,128,768]{2,1,0:T(8,128)(2,1)}, bf16[8,128,768]{2,1,0:T(8,128)(2,1)}) custom-call(s32[1]{0:T(128)} %bitcast.9.me, bf16[8,4,8,16,256]{4,3,2,1,0:T(8,128)(2,1)} %copy-done), custom_call_target="tpu_custom_call" | custom-call | bytes 4194304 | tf_op jit(solution)/shard_map/unpack/pallas_call | solution.py:300
  186.5 0.0 collective-permute-done.12.refs_3_
  186.5 0.0 collective-permute-done.13.refs_4_
  186.5 19.0 %collective-permute-done.14.refs_5_ = bf16[4,8,16,512]{3,2,1,0:T(8,128)(2,1)} collective-permute-done((bf16[4,8,16,512]{3,2,1,0:T(8,128)(2,1)}, bf16[4,8,16,512]{3,2,1,0:T(8,128)(2,1)}, u32[]{:S(2)}, u32[]{:S(2)}) %collective-permute-start.14) | collective-permute-done | bytes 524320 | tf_op jit(solution)/shard_map/ppermute | solution.py:383
  205.5 2.9 %unpack.4 = (bf16[8,128,768]{2,1,0:T(8,128)(2,1)}, bf16[8,128,768]{2,1,0:T(8,128)(2,1)}, bf16[8,128,768]{2,1,0:T(8,128)(2,1)}, bf16[8,128,768]{2,1,0:T(8,128)(2,1)}) custom-call(s32[1]{0:T(128)} %bitcast.9.me, bf16[4,8,16,512]{3,2,1,0:T(8,128)(2,1)} %get-tuple-element.92.refs_0_, ...), custom_call_target="tpu_custom_call", output_to_operand_aliasing={{0}: (7, {}), {1}: (8, {}), {2}: (9, {}), {3}: (10, {})} | custom-call | bytes 6291456 | tf_op jit(solution)/shard_map/unpack/pallas_call | solution.py:300
  208.4 0.0 collective-permute-done.9.refs_0_
  208.5 0.0 collective-permute-done.10.refs_1_
  208.5 2.1 unpack.5
  (3 shorter events, 0.0 us)
Async XLA Ops:
  0.6 3.6 %copy-start.4 = (bf16[1024,768]{1,0:T(8,128)(2,1)S(1)}, bf16[1024,768]{1,0:T(8,128)(2,1)}, u32[]{:S(2)}) copy-start(bf16[1024,768]{1,0:T(8,128)(2,1)} %v.1) | copy-start | bytes 4718596
  0.7 3.6 %copy-start.3 = (bf16[1024,768]{1,0:T(8,128)(2,1)S(1)}, bf16[1024,768]{1,0:T(8,128)(2,1)}, u32[]{:S(2)}) copy-start(bf16[1024,768]{1,0:T(8,128)(2,1)} %k.1) | copy-start | bytes 4718596
  2.9 14.5 %collective-permute-start.2 = (bf16[512,768]{1,0:T(8,128)(2,1)}, bf16[512,768]{1,0:T(8,128)(2,1)}, u32[]{:S(2)}, u32[]{:S(2)}) collective-permute-start(bf16[512,768]{1,0:T(8,128)(2,1)} %constant_dynamic-slice_fusion.1), channel_id=1, source_target_pairs={{4,8},{20,24},{8,4},{24,20},{12,28},{16,0},{5,9},{21,25},{9,5},{25... | collective-permute-start | bytes 2359304 | tf_op jit(solution)/shard_map/ppermute | solution.py:330
  5.4 22.8 %collective-permute-start = (bf16[2,512,768]{2,1,0:T(8,128)(2,1)S(1)}, bf16[2,512,768]{2,1,0:T(8,128)(2,1)S(1)}, u32[]{:S(2)}, u32[]{:S(2)}) collective-permute-start(bf16[2,512,768]{2,1,0:T(8,128)(2,1)S(1)} %pad_maximum_fusion), channel_id=1, source_target_pairs={{0,4},{4,0},{8,12},{12,8},{16,20},{20,16},{24,28},{28,24},{1,5},{5... | collective-permute-start | bytes 4718600 | tf_op jit(solution)/shard_map/ppermute | solution.py:332
  9.2 19.0 %collective-permute-start.1 = (bf16[512,768]{1,0:T(8,128)(2,1)}, bf16[512,768]{1,0:T(8,128)(2,1)}, u32[]{:S(2)}, u32[]{:S(2)}) collective-permute-start(bf16[512,768]{1,0:T(8,128)(2,1)} %get-tuple-element.116), channel_id=1, source_target_pairs={{4,8},{12,16},{20,24},{8,4},{16,12},{24,20},{5,9},{13,17},{21,25},... | collective-permute-start | bytes 2359304 | tf_op jit(solution)/shard_map/ppermute | solution.py:331
  10.7 11.4 %copy-start.7 = (s32[64,9]{0,1:T(8,128)S(1)}, s32[64,9]{0,1:T(8,128)}, u32[]{:S(2)}) copy-start(s32[64,9]{0,1:T(8,128)} %param.14) | copy-start | bytes 6916
  17.4 20.9 %collective-permute-start.3 = (bf16[512,768]{1,0:T(8,128)(2,1)}, bf16[512,768]{1,0:T(8,128)(2,1)}, u32[]{:S(2)}, u32[]{:S(2)}) collective-permute-start(bf16[512,768]{1,0:T(8,128)(2,1)} %collective-permute-done.2.outer_v), channel_id=1, source_target_pairs={{28,16},{0,12},{29,17},{1,13},{30,18},{2,14},{31,19},{3,15}} | collective-permute-start | bytes 2359304 | tf_op jit(solution)/shard_map/ppermute | solution.py:333
  23.4 82.7 %all-to-all-start = ((bf16[8,4,8,16,768]{4,3,2,1,0:T(8,128)(2,1)}), bf16[8,4,8,16,768]{4,3,2,1,0:T(8,128)(2,1)}, u32[]{:S(2)}, u32[]{:S(2)}) async-start(bf16[8,4,8,16,768]{4,3,2,1,0:T(8,128)(2,1)} %pack.1), calls=%async_computation | async-start | bytes 12582912 | tf_op jit(solution)/shard_map/all_to_all | solution.py:337
  28.2 10.1 %copy-start.8 = (bf16[2,512,768]{2,1,0:T(8,128)(2,1)}, bf16[2,512,768]{2,1,0:T(8,128)(2,1)S(1)}, u32[]{:S(2)}) copy-start(bf16[2,512,768]{2,1,0:T(8,128)(2,1)S(1)} %collective-permute-done.inner_kv) | copy-start | bytes 4718596
  88.9 27.9 %collective-permute-start.5 = (bf16[512,768]{1,0:T(8,128)(2,1)}, bf16[512,768]{1,0:T(8,128)(2,1)S(1)}, u32[]{:S(2)}, u32[]{:S(2)}) collective-permute-start(bf16[512,768]{1,0:T(8,128)(2,1)} %get-tuple-element.72), channel_id=1, source_target_pairs={{4,8},{12,16},{20,24},{8,4},{16,12},{24,20},{5,9},{13,17},{21,25},... | collective-permute-start | bytes 2359304 | tf_op jit(solution)/shard_map/ppermute | solution.py:331
  89.6 53.7 %collective-permute-start.6 = (bf16[512,768]{1,0:T(8,128)(2,1)}, bf16[512,768]{1,0:T(8,128)(2,1)}, u32[]{:S(2)}, u32[]{:S(2)}) collective-permute-start(bf16[512,768]{1,0:T(8,128)(2,1)} %get-tuple-element.85), channel_id=1, source_target_pairs={{4,8},{20,24},{8,4},{24,20},{12,28},{16,0},{5,9},{21,25},{9,5},{25... | collective-permute-start | bytes 2359304 | tf_op jit(solution)/shard_map/ppermute | solution.py:330
  90.9 25.9 %collective-permute-start.4 = (bf16[2,512,768]{2,1,0:T(8,128)(2,1)}, bf16[2,512,768]{2,1,0:T(8,128)(2,1)S(1)}, u32[]{:S(2)}, u32[]{:S(2)}) collective-permute-start(bf16[2,512,768]{2,1,0:T(8,128)(2,1)} %get-tuple-element.71), channel_id=1, source_target_pairs={{0,4},{4,0},{8,12},{12,8},{16,20},{20,16},{24,28},{28,24},{1,5},{5... | collective-permute-start | bytes 4718600 | tf_op jit(solution)/shard_map/ppermute | solution.py:332
  116.8 1.1 copy-start.5
  118.0 64.5 %all-to-all-start.1 = ((bf16[8,4,8,16,256]{4,3,2,1,0:T(8,128)(2,1)}), bf16[8,4,8,16,256]{4,3,2,1,0:T(8,128)(2,1)S(1)}, u32[]{:S(2)}, u32[]{:S(2)}) async-start(bf16[8,4,8,16,256]{4,3,2,1,0:T(8,128)(2,1)} %col_heads.2.earlier), calls=%async_computation.1 | async-start | bytes 4194304 | tf_op jit(solution)/shard_map/all_to_all | solution.py:337
  143.3 32.5 %collective-permute-start.7 = (bf16[512,768]{1,0:T(8,128)(2,1)}, bf16[512,768]{1,0:T(8,128)(2,1)}, u32[]{:S(2)}, u32[]{:S(2)}) collective-permute-start(bf16[512,768]{1,0:T(8,128)(2,1)} %collective-permute-done.6), channel_id=1, source_target_pairs={{28,16},{0,12},{29,17},{1,13},{30,18},{2,14},{31,19},{3,15}} | collective-permute-start | bytes 2359304 | tf_op jit(solution)/shard_map/ppermute | solution.py:333
  147.9 25.0 %collective-permute-start.8 = (bf16[4,8,16,512]{3,2,1,0:T(8,128)(2,1)}, bf16[4,8,16,512]{3,2,1,0:T(8,128)(2,1)S(1)}, u32[]{:S(2)}, u32[]{:S(2)}) collective-permute-start(bf16[4,8,16,512]{3,2,1,0:T(8,128)(2,1)} %get-tuple-element.89), channel_id=1, source_target_pairs={{0,8},{4,12},{8,0},{12,4},{16,24},{20,28},{24,16},{28,20},{1,9},{5... | collective-permute-start | bytes 1572872 | tf_op jit(solution)/shard_map/ppermute | solution.py:383
  148.0 27.9 %collective-permute-start.11 = (bf16[4,8,16,512]{3,2,1,0:T(8,128)(2,1)}, bf16[4,8,16,512]{3,2,1,0:T(8,128)(2,1)}, u32[]{:S(2)}, u32[]{:S(2)}) collective-permute-start(bf16[4,8,16,512]{3,2,1,0:T(8,128)(2,1)} %get-tuple-element.93), channel_id=1, source_target_pairs={{0,4},{4,0},{8,12},{12,8},{16,20},{20,16},{24,28},{28,24},{1,5},{5... | collective-permute-start | bytes 1572872 | tf_op jit(solution)/shard_map/ppermute | solution.py:383
  148.0 38.5 %collective-permute-start.12 = (bf16[4,8,16,512]{3,2,1,0:T(8,128)(2,1)}, bf16[4,8,16,512]{3,2,1,0:T(8,128)(2,1)}, u32[]{:S(2)}, u32[]{:S(2)}) collective-permute-start(bf16[4,8,16,512]{3,2,1,0:T(8,128)(2,1)} %get-tuple-element.95), channel_id=1, source_target_pairs={{0,12},{4,8},{8,4},{12,0},{16,28},{20,24},{24,20},{28,16},{1,13},{... | collective-permute-start | bytes 1572872 | tf_op jit(solution)/shard_map/ppermute | solution.py:383
  150.1 36.4 %collective-permute-start.13 = (bf16[4,8,16,512]{3,2,1,0:T(8,128)(2,1)}, bf16[4,8,16,512]{3,2,1,0:T(8,128)(2,1)}, u32[]{:S(2)}, u32[]{:S(2)}) collective-permute-start(bf16[4,8,16,512]{3,2,1,0:T(8,128)(2,1)} %get-tuple-element.96), channel_id=1, source_target_pairs={{0,16},{4,20},{8,24},{12,28},{16,0},{20,4},{24,8},{28,12},{1,17},{... | collective-permute-start | bytes 1572872 | tf_op jit(solution)/shard_map/ppermute | solution.py:383
  173.0 5.6 %copy-start.6 = (bf16[4,8,16,512]{3,2,1,0:T(8,128)(2,1)}, bf16[4,8,16,512]{3,2,1,0:T(8,128)(2,1)S(1)}, u32[]{:S(2)}) copy-start(bf16[4,8,16,512]{3,2,1,0:T(8,128)(2,1)S(1)} %collective-permute-done.8.refs_2_) | copy-start | bytes 1572868
  173.0 32.5 %collective-permute-start.14 = (bf16[4,8,16,512]{3,2,1,0:T(8,128)(2,1)}, bf16[4,8,16,512]{3,2,1,0:T(8,128)(2,1)}, u32[]{:S(2)}, u32[]{:S(2)}) collective-permute-start(bf16[4,8,16,512]{3,2,1,0:T(8,128)(2,1)} %get-tuple-element.97), channel_id=1, source_target_pairs={{0,20},{4,16},{8,28},{12,24},{16,4},{20,0},{24,12},{28,8},{1,21},{... | collective-permute-start | bytes 1572872 | tf_op jit(solution)/shard_map/ppermute | solution.py:383
  175.8 32.6 %collective-permute-start.9 = (bf16[4,8,16,512]{3,2,1,0:T(8,128)(2,1)}, bf16[4,8,16,512]{3,2,1,0:T(8,128)(2,1)}, u32[]{:S(2)}, u32[]{:S(2)}) collective-permute-start(bf16[4,8,16,512]{3,2,1,0:T(8,128)(2,1)} %get-tuple-element.90), channel_id=1, source_target_pairs={{0,24},{4,28},{8,16},{12,20},{16,8},{20,12},{24,0},{28,4},{1,25},{... | collective-permute-start | bytes 1572872 | tf_op jit(solution)/shard_map/ppermute | solution.py:386
  175.9 32.6 %collective-permute-start.10 = (bf16[4,8,16,512]{3,2,1,0:T(8,128)(2,1)}, bf16[4,8,16,512]{3,2,1,0:T(8,128)(2,1)}, u32[]{:S(2)}, u32[]{:S(2)}) collective-permute-start(bf16[4,8,16,512]{3,2,1,0:T(8,128)(2,1)} %get-tuple-element.91), channel_id=1, source_target_pairs={{0,28},{4,24},{8,20},{12,16},{16,12},{20,8},{24,4},{28,0},{1,29},{... | collective-permute-start | bytes 1572872 | tf_op jit(solution)/shard_map/ppermute | solution.py:386
  176.6 2.6 %copy-start.1 = (f32[1024,768]{1,0:T(8,128)S(1)}, f32[1024,768]{1,0:T(8,128)}, u32[]{:S(2)}) copy-start(f32[1024,768]{1,0:T(8,128)} %get-tuple-element.69) | copy-start | bytes 9437188
  176.6 3.6 %copy-start.2 = (f32[1024,768]{1,0:T(8,128)S(1)}, f32[1024,768]{1,0:T(8,128)}, u32[]{:S(2)}) copy-start(f32[1024,768]{1,0:T(8,128)} %get-tuple-element.75) | copy-start | bytes 9437188
  182.5 1.3 copy-start

commit v8 on v7

--- a/solution.py
+++ b/solution.py
@@ -327,10 +327,11 @@
     step = CHIPS_APART
     first = [(i, i + step) for i, _ in far] + [(j, j - step) for _, j in far]
     second = [(i + step, j) for i, j in far] + [(j - step, i) for i, j in far]
-    outer_v = lax.ppermute(outer_v, "ctx", near + back(near) + first)
+    hop = lax.ppermute(outer_v, "ctx", first)
     outer_k = lax.ppermute(outer_k, "ctx", across + back(across))
+    outer_v = lax.ppermute(outer_v, "ctx", near + back(near))
     inner = lax.ppermute(inner, "ctx", [(i, i ^ 1) for i in range(n)])
-    return inner, outer_k, outer_v, lambda passed: lax.ppermute(passed, "ctx", second)
+    return inner, outer_k, outer_v, hop, lambda passed: lax.ppermute(passed, "ctx", second)
 
 
 def exchanged(x):
@@ -354,13 +355,12 @@
     inner_at, outer_at = (1 - odd) * (tokens - rim), odd * (tokens - rim)
     rim_of = lambda x, at: lax.dynamic_slice_in_dim(x, at, rim, 0)
     cols = [col_query, col_key, col_value, col_cotangent]
-    outer_v = rim_of(row_value, outer_at)
-    outer_v, key, value, cols = lax.optimization_barrier((outer_v, row_key, row_value, cols))
-    outer_k = rim_of(key, outer_at)
-    inner = jnp.stack([rim_of(key, inner_at), rim_of(value, inner_at)])
-    inner, outer_k, outer_v, second_hop = swapped(inner, outer_k, outer_v)
-    sent, outer_v = lax.optimization_barrier((packed(cols, n), outer_v))
-    halos = [inner, outer_k, outer_v, second_hop(outer_v)]
+    inner = jnp.stack([rim_of(row_key, inner_at), rim_of(row_value, inner_at)])
+    outer_k, outer_v = rim_of(row_key, outer_at), rim_of(row_value, outer_at)
+    inner, outer_k, outer_v, cols = lax.optimization_barrier((inner, outer_k, outer_v, cols))
+    inner, outer_k, outer_v, hop, second_hop = swapped(inner, outer_k, outer_v)
+    sent, hop = lax.optimization_barrier((packed(cols, n), hop))
+    halos = [inner, outer_k, outer_v, second_hop(hop)]
     moved = exchanged(sent)
 
     is_far = (side == 0) | (side == CHIPS_APART - 1)
@@ -368,16 +368,16 @@
     row_output, row_dquery, own_k, own_v, *sides = row_attention(
         place, row_mask, row_query, row_key, row_value, row_cotangent, halos, band
     )
-    inner, outer_k, outer_v, second_hop = swapped(*sides)
+    inner, outer_k, outer_v, hop, second_hop = swapped(*sides)
 
     heads = col_query.shape[1] // HEAD_DIM
     half = heads // 3
     where = me.reshape(1)
     partners = [[(i, i ^ k) for i in range(n)] for k in range(n)]
     first = col_attention(where, col_mask, moved, row_output, 0, half, False)
-    first, inner, outer_k = lax.optimization_barrier((first, inner, outer_k))
+    first, inner, hop = lax.optimization_barrier((first, inner, hop))
     second = col_attention(where, col_mask, moved, first, half, heads - half, True)
-    second, outer_v = lax.optimization_barrier((second, outer_v))
+    second, outer_k, outer_v = lax.optimization_barrier((second, outer_k, outer_v))
     first = exchanged(first)
     arrived = [second[0]] + [
         lax.ppermute(second[k], "ctx", partners[k]) for k in range(1, n - 2)
@@ -391,7 +391,7 @@
             where, [arrived[k] for k in some], some, half * HEAD_DIM, col_feat, col_results
         )
 
-    outer_v = jnp.where(is_far, second_hop(outer_v), outer_v)
+    outer_v = jnp.where(is_far, second_hop(hop), outer_v)
     row_grads = []
     for own, near, across in ((own_k, inner[0], outer_k), (own_v, inner[1], outer_v)):
         lo = jnp.where(odd == 1, near, across).astype(own.dtype)

time: 211 us -> 216 us (1.024)
  starting transfers between devices: 38.4 us -> 45.3 us
  waiting for transfers between devices: 64.3 us -> 61.9 us
    all_to_all x2, waiting for transfers between devices: 11.1 us -> 5.59 us  [exchanged(): return lax.all_to_all(x, 'ctx', 0, 0, tiled=True)]
    ppermute x2, starting transfers between devices: 7.86 us -> 11.3 us  [swapped(): inner = lax.ppermute(inner, 'ctx', [(i, i ^ 1) for i in range(n)])]
    ppermute x2 -> x4, waiting for transfers between devices: 1.21 us -> 3.69 us  [the longest x2 3.69 us: swapped(): hop = lax.ppermute(outer_v, 'ctx', first)]
    ppermute x2 -> x4, starting transfers between devices: 2.57 us -> 4.86 us  [the longest x2 2.58 us: swapped(): hop = lax.ppermute(outer_v, 'ctx', first)]
    unnamed x19 -> x17, local copies, waits for them, and re-layouts: 4.76 us -> 5.21 us
  transfers between devices with their start and end apart: 17 -> 19, of which waited for: 5 -> 5; matrix products, arithmetic and copies ran while one was open for 3% -> 3% of each run, Pallas kernels for 44% -> 43%
where the time goes in v8:
time: 216 us; the launch traced here: 215 us
  Pallas kernels  93.7 us (43%)
  waiting for transfers between devices  61.9 us (29%)
  starting transfers between devices  45.3 us (21%)
  local copies, waits for them, and re-layouts  7.26 us (3%)
  other arithmetic  5.93 us (3%)
    pallas_call x1, Pallas kernels, row_attention(): pl.pallas_call(functools.partial(row_kernel, band), grid=(heads,), in_spe...  50.6 us
    ppermute x5, waiting for transfers between devices, body(): lax.ppermute(second[k], 'ctx', partners[k])  41.3 us
    pallas_call x2, Pallas kernels, col_attention(): pl.pallas_call(functools.partial(col_kernel, n_parts), grid=(heads, cols...  30 us
    all_to_all x2, starting transfers between devices, exchanged(): return lax.all_to_all(x, 'ctx', 0, 0, tiled=True)  11.4 us
    ppermute x2, waiting for transfers between devices, swapped(): lax.ppermute(passed, 'ctx', second)  11.3 us
    ppermute x2, starting transfers between devices, swapped(): inner = lax.ppermute(inner, 'ctx', [(i, i ^ 1) for i in range(n)])  11.3 us
    ppermute x2, starting transfers between devices, swapped(): lax.ppermute(passed, 'ctx', second)  8.55 us
    pallas_call x3, Pallas kernels, unpacked(): pl.pallas_call(functools.partial(unpack_kernel, partners, start), in_spec...  7.61 us
  transfers between devices with their start and end apart: 19, of which 5 were waited for; matrix products, arithmetic and copies ran while one was open for 3% of the time, Pallas kernels for 43%

profile of v8, /device:TPU:0, one launch (start us, length us, event | category | flops | bytes accessed | tf_op | source)
XLA Modules:
  0.0 215.1 jit_solution(1393003257473620100)
XLA Ops:
  0.7 2.1 constant_dynamic-slice_fusion
  2.7 0.1 pad_maximum_fusion
  2.9 1.3 collective-permute-start.3
  4.2 0.7 collective-permute-start
  4.9 1.6 collective-permute-start.2
  6.5 1.5 collective-permute-start.1
  8.0 0.0 copy-start.6
  8.0 5.5 %pack.1 = bf16[8,4,8,16,768]{4,3,2,1,0:T(8,128)(2,1)} custom-call(bf16[8,128,768]{2,1,0:T(8,128)(2,1)} %bitcast.26, bf16[8,128,768]{2,1,0:T(8,128)(2,1)} %bitcast.27, bf16[8,128,768]{2,1,0:T(8,128)(2,1)} %bitcast.28, bf16[8,128,768]{2,1,0:T(8,128)(2,1)} %bitcast.29), custom_call_target="tpu_custom_call" | custom-call | bytes 12582912 | tf_op jit(solution)/shard_map/pack/pallas_call | solution.py:252
  13.5 3.7 %collective-permute-done.3 = bf16[512,768]{1,0:T(8,128)(2,1)} collective-permute-done((bf16[512,768]{1,0:T(8,128)(2,1)S(1)}, bf16[512,768]{1,0:T(8,128)(2,1)}, u32[]{:S(2)}, u32[]{:S(2)}) %collective-permute-start.3) | collective-permute-done | bytes 786464 | tf_op jit(solution)/shard_map/ppermute | solution.py:330
  17.2 3.9 %collective-permute-start.4 = (bf16[512,768]{1,0:T(8,128)(2,1)}, bf16[512,768]{1,0:T(8,128)(2,1)}, u32[]{:S(2)}, u32[]{:S(2)}) collective-permute-start(bf16[512,768]{1,0:T(8,128)(2,1)} %collective-permute-done.3), channel_id=1, source_target_pairs={{28,16},{0,12},{29,17},{1,13},{30,18},{2,14},{31,19},{3,15}} | collective-permute-start | bytes 2359304 | tf_op jit(solution)/shard_map/ppermute | solution.py:334
  21.1 0.0 copy-done.6
  21.1 0.7 copy.26.mask
  21.8 0.6 pad_add_fusion.place
  22.4 4.8 %all-to-all-start = ((bf16[8,4,8,16,768]{4,3,2,1,0:T(8,128)(2,1)}), bf16[8,4,8,16,768]{4,3,2,1,0:T(8,128)(2,1)}, u32[]{:S(2)}, u32[]{:S(2)}) async-start(bf16[8,4,8,16,768]{4,3,2,1,0:T(8,128)(2,1)} %pack.1), calls=%async_computation | async-start | bytes 12582912 | tf_op jit(solution)/shard_map/all_to_all | solution.py:338
  27.2 0.0 collective-permute-done.1.outer_k
  27.2 0.0 collective-permute-done.2.outer_v
  27.2 0.0 collective-permute-done.inner_kv
  27.2 11.3 %collective-permute-done.4.far_v = bf16[512,768]{1,0:T(8,128)(2,1)} collective-permute-done((bf16[512,768]{1,0:T(8,128)(2,1)}, bf16[512,768]{1,0:T(8,128)(2,1)}, u32[]{:S(2)}, u32[]{:S(2)}) %collective-permute-start.4) | collective-permute-done | bytes 786464 | tf_op jit(solution)/shard_map/ppermute | solution.py:334
  38.5 50.6 %row_heads.1 = (bf16[1024,768]{1,0:T(8,128)(2,1)}, bf16[1024,768]{1,0:T(8,128)(2,1)}, f32[1024,768]{1,0:T(8,128)}, f32[1024,768]{1,0:T(8,128)}, bf16[2,512,768]{...) custom-call(s32[3]{0:T(128)} %pad_add_fusion.place, s32[64,9]{1,0:T(8,128)} %copy.26.mask, ...), custom_call_target="tpu_custom_call" | custom-call | flops 241591910400 | bytes 23592960 | tf_op jit(solution)/shard_map/row_heads/pallas_call | solution.py:121
  89.1 0.7 collective-permute-start.8
  89.8 1.3 collective-permute-start.6
  91.1 1.6 collective-permute-start.7
  92.7 10.5 %collective-permute-start.5 = (bf16[2,512,768]{2,1,0:T(8,128)(2,1)}, bf16[2,512,768]{2,1,0:T(8,128)(2,1)S(1)}, u32[]{:S(2)}, u32[]{:S(2)}) collective-permute-start(bf16[2,512,768]{2,1,0:T(8,128)(2,1)} %get-tuple-element.72), channel_id=1, source_target_pairs={{0,4},{4,0},{8,12},{12,8},{16,20},{20,16},{24,28},{28,24},{1,5},{5... | collective-permute-start | bytes 4718600 | tf_op jit(solution)/shard_map/ppermute | solution.py:333
  103.2 5.6 %all-to-all-done.x = bf16[8,4,8,16,768]{4,3,2,1,0:T(8,128)(2,1)} async-done(((bf16[8,4,8,16,768]{4,3,2,1,0:T(8,128)(2,1)}), bf16[8,4,8,16,768]{4,3,2,1,0:T(8,128)(2,1)}, u32[]{:S(2)}, u32[]{:S(2)}) %all-to-all-start) | async-done | bytes 6291488 | tf_op jit(solution)/shard_map/all_to_all | solution.py:338
  108.8 10.7 %col_heads.2.earlier = bf16[8,4,8,16,256]{4,3,2,1,0:T(8,128)(2,1)} custom-call(s32[1]{0:T(128)} %bitcast.9.me, s32[64,64]{1,0:T(8,128)} %mask.4, bf16[8,4,8,16,768]{4,3,2,1,0:T(8,128)(2,1)} %all-to-all-done.x, bf16[1024,768]{1,0:T(8,128)(2,1)} %get-tuple-element.52.earlier), custom_call_target="tpu_custom_call" | custom-call | flops 32212254720 | bytes 12582912 | tf_op jit(solution)/shard_map/col_heads/pallas_call | solution.py:203
  119.5 0.0 collective-permute-done.6
  119.5 0.0 copy-start.7
  119.5 0.0 collective-permute-done.5
  119.5 0.0 copy-start.3
  119.5 0.9 copy-done.7
  120.4 0.5 copy-done.3
  120.9 6.6 %all-to-all-start.1 = ((bf16[8,4,8,16,256]{4,3,2,1,0:T(8,128)(2,1)}), bf16[8,4,8,16,256]{4,3,2,1,0:T(8,128)(2,1)S(1)}, u32[]{:S(2)}, u32[]{:S(2)}) async-start(bf16[8,4,8,16,256]{4,3,2,1,0:T(8,128)(2,1)} %col_heads.2.earlier), calls=%async_computation.1 | async-start | bytes 4194304 | tf_op jit(solution)/shard_map/all_to_all | solution.py:338
  127.5 4.6 %collective-permute-start.9 = (bf16[512,768]{1,0:T(8,128)(2,1)}, bf16[512,768]{1,0:T(8,128)(2,1)}, u32[]{:S(2)}, u32[]{:S(2)}) collective-permute-start(bf16[512,768]{1,0:T(8,128)(2,1)} %copy-done.7), channel_id=1, source_target_pairs={{28,16},{0,12},{29,17},{1,13},{30,18},{2,14},{31,19},{3,15}} | collective-permute-start | bytes 2359304 | tf_op jit(solution)/shard_map/ppermute | solution.py:334
  132.1 19.4 %col_heads.3 = (bf16[4,8,16,512]{3,2,1,0:T(8,128)(2,1)}, bf16[4,8,16,512]{3,2,1,0:T(8,128)(2,1)}, bf16[4,8,16,512]{3,2,1,0:T(8,128)(2,1)}, bf16[4,8,16,512]{3,2,...) custom-call(s32[1]{0:T(128)} %bitcast.9.me, ...), custom_call_target="tpu_custom_call" | custom-call | flops 64424509440 | bytes 12582912 | tf_op jit(solution)/shard_map/col_heads/pallas_call | solution.py:203
  151.5 0.0 collective-permute-done.7
  151.5 0.0 collective-permute-done.8
  151.5 0.1 collective-permute-start.10
  151.6 0.1 collective-permute-start.13
  151.7 2.0 collective-permute-start.14
  153.7 0.3 collective-permute-start.15
  154.0 22.5 %collective-permute-done.10.refs_2_ = bf16[4,8,16,512]{3,2,1,0:T(8,128)(2,1)S(1)} collective-permute-done((bf16[4,8,16,512]{3,2,1,0:T(8,128)(2,1)}, bf16[4,8,16,512]{3,2,1,0:T(8,128)(2,1)S(1)}, u32[]{:S(2)}, u32[]{:S(2)}) %collective-permute-start.10) | collective-permute-done | bytes 524320 | tf_op jit(solution)/shard_map/ppermute | solution.py:383
  176.6 2.9 %collective-permute-start.16 = (bf16[4,8,16,512]{3,2,1,0:T(8,128)(2,1)}, bf16[4,8,16,512]{3,2,1,0:T(8,128)(2,1)}, u32[]{:S(2)}, u32[]{:S(2)}) collective-permute-start(bf16[4,8,16,512]{3,2,1,0:T(8,128)(2,1)} %get-tuple-element.99), channel_id=1, source_target_pairs={{0,20},{4,16},{8,28},{12,24},{16,4},{20,0},{24,12},{28,8},{1,21},{... | collective-permute-start | bytes 1572872 | tf_op jit(solution)/shard_map/ppermute | solution.py:383
  179.4 0.0 collective-permute-done.9
  179.4 0.0 collective-permute-start.11
  179.4 2.2 %bitcast_select_fusion.1 = (bf16[512,768]{1,0:T(8,128)(2,1)S(1)}, bf16[512,768]{1,0:T(8,128)(2,1)S(1)}, bf16[512,768]{1,0:T(8,128)(2,1)S(1)}, bf16[512,768]{1,0:T(8,128)(2,1)S(1)}) fusion(pred[]{:T(512)S(6)} %eq.17, bf16[2,512,768]{2,1,0:T(8,128)(2,1)} %copy-done.3, bf16[512,768]{1,0:T(8,128)(2,1)} %collective-permute-done.9, ...), kind=kLoop, calls=%fused_computation.4 | loop fusion | flops 1966080 | bytes 7077890 | tf_op jit(solution)/shard_map/jit(_where)/select_n | solution.py:397
  181.7 0.0 copy-done.4
  181.7 0.0 collective-permute-done.13.refs_1_
  181.7 0.8 collective-permute-start.12
  182.5 0.0 copy-done.2
  182.5 1.5 add_convert_fusion.1
  183.9 1.0 copy-done.1
  184.9 1.5 add_convert_fusion
  186.4 0.0 all-to-all-done.1.refs_0_
  186.4 1.3 copy-done
  187.8 2.6 %unpack.3 = (bf16[8,128,768]{2,1,0:T(8,128)(2,1)}, bf16[8,128,768]{2,1,0:T(8,128)(2,1)}, bf16[8,128,768]{2,1,0:T(8,128)(2,1)}, bf16[8,128,768]{2,1,0:T(8,128)(2,1)}) custom-call(s32[1]{0:T(128)} %bitcast.9.me, bf16[8,4,8,16,256]{4,3,2,1,0:T(8,128)(2,1)} %copy-done), custom_call_target="tpu_custom_call" | custom-call | bytes 4194304 | tf_op jit(solution)/shard_map/unpack/pallas_call | solution.py:300
  190.3 0.0 collective-permute-done.14.refs_3_
  190.4 0.0 collective-permute-done.15.refs_4_
  190.4 18.7 %collective-permute-done.16.refs_5_ = bf16[4,8,16,512]{3,2,1,0:T(8,128)(2,1)} collective-permute-done((bf16[4,8,16,512]{3,2,1,0:T(8,128)(2,1)}, bf16[4,8,16,512]{3,2,1,0:T(8,128)(2,1)}, u32[]{:S(2)}, u32[]{:S(2)}) %collective-permute-start.16) | collective-permute-done | bytes 524320 | tf_op jit(solution)/shard_map/ppermute | solution.py:383
  209.1 2.9 %unpack.4 = (bf16[8,128,768]{2,1,0:T(8,128)(2,1)}, bf16[8,128,768]{2,1,0:T(8,128)(2,1)}, bf16[8,128,768]{2,1,0:T(8,128)(2,1)}, bf16[8,128,768]{2,1,0:T(8,128)(2,1)}) custom-call(s32[1]{0:T(128)} %bitcast.9.me, bf16[4,8,16,512]{3,2,1,0:T(8,128)(2,1)} %get-tuple-element.94.refs_0_, ...), custom_call_target="tpu_custom_call", output_to_operand_aliasing={{0}: (7, {}), {1}: (8, {}), {2}: (9, {}), {3}: (10, {})} | custom-call | bytes 6291456 | tf_op jit(solution)/shard_map/unpack/pallas_call | solution.py:300
  212.0 0.0 collective-permute-done.11.refs_0_
  212.0 0.0 collective-permute-done.12.refs_1_
  212.1 0.0 copy-start.5
  212.1 0.8 copy-done.5
  212.8 2.1 unpack.5
  (4 shorter events, 0.0 us)
Async XLA Ops:
  2.9 14.3 %collective-permute-start.3 = (bf16[512,768]{1,0:T(8,128)(2,1)S(1)}, bf16[512,768]{1,0:T(8,128)(2,1)}, u32[]{:S(2)}, u32[]{:S(2)}) collective-permute-start(bf16[512,768]{1,0:T(8,128)(2,1)S(1)} %get-tuple-element.62), channel_id=1, source_target_pairs={{12,28},{16,0},{13,29},{17,1},{14,30},{18,2},{15,31},{19,3}} | collective-permute-start | bytes 2359304 | tf_op jit(solution)/shard_map/ppermute | solution.py:330
  4.2 23.0 %collective-permute-start = (bf16[2,512,768]{2,1,0:T(8,128)(2,1)S(1)}, bf16[2,512,768]{2,1,0:T(8,128)(2,1)}, u32[]{:S(2)}, u32[]{:S(2)}) collective-permute-start(bf16[2,512,768]{2,1,0:T(8,128)(2,1)S(1)} %pad_maximum_fusion), channel_id=1, source_target_pairs={{0,4},{4,0},{8,12},{12,8},{16,20},{20,16},{24,28},{28,24},{1,5},{5... | collective-permute-start | bytes 4718600 | tf_op jit(solution)/shard_map/ppermute | solution.py:333
  4.9 22.3 %collective-permute-start.2 = (bf16[512,768]{1,0:T(8,128)(2,1)S(1)}, bf16[512,768]{1,0:T(8,128)(2,1)}, u32[]{:S(2)}, u32[]{:S(2)}) collective-permute-start(bf16[512,768]{1,0:T(8,128)(2,1)S(1)} %get-tuple-element.62), channel_id=1, source_target_pairs={{4,8},{20,24},{8,4},{24,20},{5,9},{21,25},{9,5},{25,21},{6,10},{22... | collective-permute-start | bytes 2359304 | tf_op jit(solution)/shard_map/ppermute | solution.py:332
  6.5 20.7 %collective-permute-start.1 = (bf16[512,768]{1,0:T(8,128)(2,1)S(1)}, bf16[512,768]{1,0:T(8,128)(2,1)}, u32[]{:S(2)}, u32[]{:S(2)}) collective-permute-start(bf16[512,768]{1,0:T(8,128)(2,1)S(1)} %get-tuple-element.61), channel_id=1, source_target_pairs={{4,8},{12,16},{20,24},{8,4},{16,12},{24,20},{5,9},{13,17},{21,25},... | collective-permute-start | bytes 2359304 | tf_op jit(solution)/shard_map/ppermute | solution.py:331
  8.0 13.1 %copy-start.6 = (s32[64,9]{0,1:T(8,128)S(1)}, s32[64,9]{0,1:T(8,128)}, u32[]{:S(2)}) copy-start(s32[64,9]{0,1:T(8,128)} %param.14) | copy-start | bytes 6916
  17.2 21.3 %collective-permute-start.4 = (bf16[512,768]{1,0:T(8,128)(2,1)}, bf16[512,768]{1,0:T(8,128)(2,1)}, u32[]{:S(2)}, u32[]{:S(2)}) collective-permute-start(bf16[512,768]{1,0:T(8,128)(2,1)} %collective-permute-done.3), channel_id=1, source_target_pairs={{28,16},{0,12},{29,17},{1,13},{30,18},{2,14},{31,19},{3,15}} | collective-permute-start | bytes 2359304 | tf_op jit(solution)/shard_map/ppermute | solution.py:334
  22.4 86.4 %all-to-all-start = ((bf16[8,4,8,16,768]{4,3,2,1,0:T(8,128)(2,1)}), bf16[8,4,8,16,768]{4,3,2,1,0:T(8,128)(2,1)}, u32[]{:S(2)}, u32[]{:S(2)}) async-start(bf16[8,4,8,16,768]{4,3,2,1,0:T(8,128)(2,1)} %pack.1), calls=%async_computation | async-start | bytes 12582912 | tf_op jit(solution)/shard_map/all_to_all | solution.py:338
  89.1 62.4 %collective-permute-start.8 = (bf16[512,768]{1,0:T(8,128)(2,1)}, bf16[512,768]{1,0:T(8,128)(2,1)S(1)}, u32[]{:S(2)}, u32[]{:S(2)}) collective-permute-start(bf16[512,768]{1,0:T(8,128)(2,1)} %get-tuple-element.73), channel_id=1, source_target_pairs={{4,8},{20,24},{8,4},{24,20},{5,9},{21,25},{9,5},{25,21},{6,10},{22... | collective-permute-start | bytes 2359304 | tf_op jit(solution)/shard_map/ppermute | solution.py:332
  89.8 29.6 %collective-permute-start.6 = (bf16[512,768]{1,0:T(8,128)(2,1)}, bf16[512,768]{1,0:T(8,128)(2,1)S(1)}, u32[]{:S(2)}, u32[]{:S(2)}) collective-permute-start(bf16[512,768]{1,0:T(8,128)(2,1)} %get-tuple-element.73), channel_id=1, source_target_pairs={{12,28},{16,0},{13,29},{17,1},{14,30},{18,2},{15,31},{19,3}} | collective-permute-start | bytes 2359304 | tf_op jit(solution)/shard_map/ppermute | solution.py:330
  91.1 60.4 %collective-permute-start.7 = (bf16[512,768]{1,0:T(8,128)(2,1)}, bf16[512,768]{1,0:T(8,128)(2,1)}, u32[]{:S(2)}, u32[]{:S(2)}) collective-permute-start(bf16[512,768]{1,0:T(8,128)(2,1)} %get-tuple-element.84), channel_id=1, source_target_pairs={{4,8},{12,16},{20,24},{8,4},{16,12},{24,20},{5,9},{13,17},{21,25},... | collective-permute-start | bytes 2359304 | tf_op jit(solution)/shard_map/ppermute | solution.py:331
  92.7 26.8 %collective-permute-start.5 = (bf16[2,512,768]{2,1,0:T(8,128)(2,1)}, bf16[2,512,768]{2,1,0:T(8,128)(2,1)S(1)}, u32[]{:S(2)}, u32[]{:S(2)}) collective-permute-start(bf16[2,512,768]{2,1,0:T(8,128)(2,1)} %get-tuple-element.72), channel_id=1, source_target_pairs={{0,4},{4,0},{8,12},{12,8},{16,20},{20,16},{24,28},{28,24},{1,5},{5... | collective-permute-start | bytes 4718600 | tf_op jit(solution)/shard_map/ppermute | solution.py:333
  119.5 0.9 copy-start.7
  119.5 1.4 copy-start.3
  120.9 65.5 %all-to-all-start.1 = ((bf16[8,4,8,16,256]{4,3,2,1,0:T(8,128)(2,1)}), bf16[8,4,8,16,256]{4,3,2,1,0:T(8,128)(2,1)S(1)}, u32[]{:S(2)}, u32[]{:S(2)}) async-start(bf16[8,4,8,16,256]{4,3,2,1,0:T(8,128)(2,1)} %col_heads.2.earlier), calls=%async_computation.1 | async-start | bytes 4194304 | tf_op jit(solution)/shard_map/all_to_all | solution.py:338
  127.5 51.9 %collective-permute-start.9 = (bf16[512,768]{1,0:T(8,128)(2,1)}, bf16[512,768]{1,0:T(8,128)(2,1)}, u32[]{:S(2)}, u32[]{:S(2)}) collective-permute-start(bf16[512,768]{1,0:T(8,128)(2,1)} %copy-done.7), channel_id=1, source_target_pairs={{28,16},{0,12},{29,17},{1,13},{30,18},{2,14},{31,19},{3,15}} | collective-permute-start | bytes 2359304 | tf_op jit(solution)/shard_map/ppermute | solution.py:334
  151.5 25.0 %collective-permute-start.10 = (bf16[4,8,16,512]{3,2,1,0:T(8,128)(2,1)}, bf16[4,8,16,512]{3,2,1,0:T(8,128)(2,1)S(1)}, u32[]{:S(2)}, u32[]{:S(2)}) collective-permute-start(bf16[4,8,16,512]{3,2,1,0:T(8,128)(2,1)} %get-tuple-element.91), channel_id=1, source_target_pairs={{0,8},{4,12},{8,0},{12,4},{16,24},{20,28},{24,16},{28,20},{1,9},{5... | collective-permute-start | bytes 1572872 | tf_op jit(solution)/shard_map/ppermute | solution.py:383
  151.6 30.1 %collective-permute-start.13 = (bf16[4,8,16,512]{3,2,1,0:T(8,128)(2,1)}, bf16[4,8,16,512]{3,2,1,0:T(8,128)(2,1)}, u32[]{:S(2)}, u32[]{:S(2)}) collective-permute-start(bf16[4,8,16,512]{3,2,1,0:T(8,128)(2,1)} %get-tuple-element.95), channel_id=1, source_target_pairs={{0,4},{4,0},{8,12},{12,8},{16,20},{20,16},{24,28},{28,24},{1,5},{5... | collective-permute-start | bytes 1572872 | tf_op jit(solution)/shard_map/ppermute | solution.py:383
  151.7 38.7 %collective-permute-start.14 = (bf16[4,8,16,512]{3,2,1,0:T(8,128)(2,1)}, bf16[4,8,16,512]{3,2,1,0:T(8,128)(2,1)}, u32[]{:S(2)}, u32[]{:S(2)}) collective-permute-start(bf16[4,8,16,512]{3,2,1,0:T(8,128)(2,1)} %get-tuple-element.97), channel_id=1, source_target_pairs={{0,12},{4,8},{8,4},{12,0},{16,28},{20,24},{24,20},{28,16},{1,13},{... | collective-permute-start | bytes 1572872 | tf_op jit(solution)/shard_map/ppermute | solution.py:383
  153.7 36.6 %collective-permute-start.15 = (bf16[4,8,16,512]{3,2,1,0:T(8,128)(2,1)}, bf16[4,8,16,512]{3,2,1,0:T(8,128)(2,1)}, u32[]{:S(2)}, u32[]{:S(2)}) collective-permute-start(bf16[4,8,16,512]{3,2,1,0:T(8,128)(2,1)} %get-tuple-element.98), channel_id=1, source_target_pairs={{0,16},{4,20},{8,24},{12,28},{16,0},{20,4},{24,8},{28,12},{1,17},{... | collective-permute-start | bytes 1572872 | tf_op jit(solution)/shard_map/ppermute | solution.py:383
  176.6 5.1 %copy-start.4 = (bf16[4,8,16,512]{3,2,1,0:T(8,128)(2,1)}, bf16[4,8,16,512]{3,2,1,0:T(8,128)(2,1)S(1)}, u32[]{:S(2)}) copy-start(bf16[4,8,16,512]{3,2,1,0:T(8,128)(2,1)S(1)} %collective-permute-done.10.refs_2_) | copy-start | bytes 1572868
  176.6 32.5 %collective-permute-start.16 = (bf16[4,8,16,512]{3,2,1,0:T(8,128)(2,1)}, bf16[4,8,16,512]{3,2,1,0:T(8,128)(2,1)}, u32[]{:S(2)}, u32[]{:S(2)}) collective-permute-start(bf16[4,8,16,512]{3,2,1,0:T(8,128)(2,1)} %get-tuple-element.99), channel_id=1, source_target_pairs={{0,20},{4,16},{8,28},{12,24},{16,4},{20,0},{24,12},{28,8},{1,21},{... | collective-permute-start | bytes 1572872 | tf_op jit(solution)/shard_map/ppermute | solution.py:383
  179.4 32.6 %collective-permute-start.11 = (bf16[4,8,16,512]{3,2,1,0:T(8,128)(2,1)}, bf16[4,8,16,512]{3,2,1,0:T(8,128)(2,1)}, u32[]{:S(2)}, u32[]{:S(2)}) collective-permute-start(bf16[4,8,16,512]{3,2,1,0:T(8,128)(2,1)} %get-tuple-element.92), channel_id=1, source_target_pairs={{0,24},{4,28},{8,16},{12,20},{16,8},{20,12},{24,0},{28,4},{1,25},{... | collective-permute-start | bytes 1572872 | tf_op jit(solution)/shard_map/ppermute | solution.py:386
  179.4 3.0 %copy-start.2 = (f32[1024,768]{1,0:T(8,128)S(1)}, f32[1024,768]{1,0:T(8,128)}, u32[]{:S(2)}) copy-start(f32[1024,768]{1,0:T(8,128)} %get-tuple-element.70) | copy-start | bytes 9437188
  181.7 30.3 %collective-permute-start.12 = (bf16[4,8,16,512]{3,2,1,0:T(8,128)(2,1)}, bf16[4,8,16,512]{3,2,1,0:T(8,128)(2,1)S(1)}, u32[]{:S(2)}, u32[]{:S(2)}) collective-permute-start(bf16[4,8,16,512]{3,2,1,0:T(8,128)(2,1)} %get-tuple-element.93), channel_id=1, source_target_pairs={{0,28},{4,24},{8,20},{12,16},{16,12},{20,8},{24,4},{28,0},{1,29},{... | collective-permute-start | bytes 1572872 | tf_op jit(solution)/shard_map/ppermute | solution.py:386
  182.5 2.5 %copy-start.1 = (f32[1024,768]{1,0:T(8,128)S(1)}, f32[1024,768]{1,0:T(8,128)}, u32[]{:S(2)}) copy-start(f32[1024,768]{1,0:T(8,128)} %get-tuple-element.86) | copy-start | bytes 9437188
  186.4 1.3 copy-start
  212.1 0.8 copy-start.5

commit v9 on v7

--- a/solution.py
+++ b/solution.py
@@ -333,6 +333,14 @@
     return inner, outer_k, outer_v, lambda passed: lax.ppermute(passed, "ctx", second)
 
 
+def handed_back(inner, outer_k, outer_v):
+    n = lax.axis_size("ctx")
+    across = [(i, i + 1) for i in range(1, n - 1, 2)]
+    pairs = across + [(j, i) for i, j in across]
+    inner = lax.ppermute(inner, "ctx", [(i, i ^ 1) for i in range(n)])
+    return inner, lax.ppermute(outer_k, "ctx", pairs), lax.ppermute(outer_v, "ctx", pairs)
+
+
 def exchanged(x):
     return lax.all_to_all(x, "ctx", 0, 0, tiled=True)
 
@@ -353,11 +361,10 @@
     side = me % CHIPS_APART
     inner_at, outer_at = (1 - odd) * (tokens - rim), odd * (tokens - rim)
     rim_of = lambda x, at: lax.dynamic_slice_in_dim(x, at, rim, 0)
+    inner = jnp.stack([rim_of(row_key, inner_at), rim_of(row_value, inner_at)])
+    outer_k, outer_v = rim_of(row_key, outer_at), rim_of(row_value, outer_at)
     cols = [col_query, col_key, col_value, col_cotangent]
-    outer_v = rim_of(row_value, outer_at)
-    outer_v, key, value, cols = lax.optimization_barrier((outer_v, row_key, row_value, cols))
-    outer_k = rim_of(key, outer_at)
-    inner = jnp.stack([rim_of(key, inner_at), rim_of(value, inner_at)])
+    inner, outer_k, outer_v, cols = lax.optimization_barrier((inner, outer_k, outer_v, cols))
     inner, outer_k, outer_v, second_hop = swapped(inner, outer_k, outer_v)
     sent, outer_v = lax.optimization_barrier((packed(cols, n), outer_v))
     halos = [inner, outer_k, outer_v, second_hop(outer_v)]
@@ -368,10 +375,10 @@
     row_output, row_dquery, own_k, own_v, *sides = row_attention(
         place, row_mask, row_query, row_key, row_value, row_cotangent, halos, band
     )
-    inner, outer_k, outer_v, second_hop = swapped(*sides)
+    inner, outer_k, outer_v = handed_back(*sides)
 
     heads = col_query.shape[1] // HEAD_DIM
-    half = heads // 3
+    half = heads // 2
     where = me.reshape(1)
     partners = [[(i, i ^ k) for i in range(n)] for k in range(n)]
     first = col_attention(where, col_mask, moved, row_output, 0, half, False)
@@ -382,7 +389,7 @@
     arrived = [second[0]] + [
         lax.ppermute(second[k], "ctx", partners[k]) for k in range(1, n - 2)
     ]
-    *last, arrived[2] = lax.optimization_barrier((second[n - 2], second[n - 1], arrived[2]))
+    *last, arrived[1] = lax.optimization_barrier((second[n - 2], second[n - 1], arrived[1]))
     arrived += [lax.ppermute(part, "ctx", pairs) for part, pairs in zip(last, partners[n - 2 :])]
     col_feat = col_query.shape[1]
     col_results = unpacked(where, first, None, 0, col_feat, [])
@@ -391,7 +398,6 @@
             where, [arrived[k] for k in some], some, half * HEAD_DIM, col_feat, col_results
         )
 
-    outer_v = jnp.where(is_far, second_hop(outer_v), outer_v)
     row_grads = []
     for own, near, across in ((own_k, inner[0], outer_k), (own_v, inner[1], outer_v)):
         lo = jnp.where(odd == 1, near, across).astype(own.dtype)

time: 211 us -> 205 us (0.972)
  the two profiles are of different devices: /device:TPU:0 before, /device:TPU:11 now
where the time goes in v9:
time: 205 us; the launch traced here: 201 us
  Pallas kernels  93.6 us (46%)
  waiting for transfers between devices  50.1 us (24%)
  starting transfers between devices  43 us (21%)
  local copies, waits for them, and re-layouts  7.66 us (4%)
  other arithmetic  5.88 us (3%)
    pallas_call x1, Pallas kernels, row_attention(): pl.pallas_call(functools.partial(row_kernel, band), grid=(heads,), in_spe...  50.6 us
    pallas_call x2, Pallas kernels, col_attention(): pl.pallas_call(functools.partial(col_kernel, n_parts), grid=(heads, cols...  29.9 us
    ppermute x5, waiting for transfers between devices, body(): lax.ppermute(second[k], 'ctx', partners[k])  21.8 us
    all_to_all x2, starting transfers between devices, exchanged(): return lax.all_to_all(x, 'ctx', 0, 0, tiled=True)  20.2 us
    ppermute x2, waiting for transfers between devices, body(): lax.ppermute(part, 'ctx', pairs)  13.9 us
    ppermute x1, waiting for transfers between devices, swapped(): lax.ppermute(passed, 'ctx', second)  8.18 us
    pallas_call x3, Pallas kernels, unpacked(): pl.pallas_call(functools.partial(unpack_kernel, partners, start), in_spec...  7.58 us
    unnamed x17, local copies, waits for them, and re-layouts  5.61 us
  transfers between devices with their start and end apart: 16, of which 7 were waited for; matrix products, arithmetic and copies ran while one was open for 3% of the time, Pallas kernels for 46%

profile of v9, /device:TPU:11, one launch (start us, length us, event | category | flops | bytes accessed | tf_op | source)
XLA Modules:
  0.0 201.3 jit_solution(1395273750752087084)
XLA Ops:
  0.7 2.1 %constant_dynamic-slice_fusion = (bf16[512,768]{1,0:T(8,128)(2,1)S(1)}, bf16[1,512,768]{2,1,0:T(8,128)(2,1)S(1)}, bf16[1,512,768]{2,1,0:T(8,128)(2,1)S(1)}, bf16[512,768]{1,0:T(8,128)(2,1)S(1)}) fusion(bf16[1024,768]{1,0:T(8,128)(2,1)} %v.1, s32[]{:T(128)S(6)} %select_n.42, s32[]{:T(128)S(6)} %select_n.41, bf16[1024,768]{1,0:T(8,128)(2,1)} %k.1), kind=kLoop, calls=%fused_computation.9 | loop fusion | bytes 6291464 | tf_op jit(solution)/shard_map/dynamic_slice | solution.py:363
  2.7 0.1 pad_maximum_fusion
  2.9 4.1 %collective-permute-start.2 = (bf16[512,768]{1,0:T(8,128)(2,1)S(1)}, bf16[512,768]{1,0:T(8,128)(2,1)}, u32[]{:S(2)}, u32[]{:S(2)}) collective-permute-start(bf16[512,768]{1,0:T(8,128)(2,1)S(1)} %get-tuple-element.65), channel_id=1, source_target_pairs={{4,8},{20,24},{8,4},{24,20},{12,28},{16,0},{5,9},{21,25},{9,5},{25... | collective-permute-start | bytes 2359304 | tf_op jit(solution)/shard_map/ppermute | solution.py:330
  6.9 0.0 collective-permute-start
  6.9 3.2 %collective-permute-start.1 = (bf16[512,768]{1,0:T(8,128)(2,1)S(1)}, bf16[512,768]{1,0:T(8,128)(2,1)}, u32[]{:S(2)}, u32[]{:S(2)}) collective-permute-start(bf16[512,768]{1,0:T(8,128)(2,1)S(1)} %get-tuple-element.60), channel_id=1, source_target_pairs={{4,8},{12,16},{20,24},{8,4},{16,12},{24,20},{5,9},{13,17},{21,25},... | collective-permute-start | bytes 2359304 | tf_op jit(solution)/shard_map/ppermute | solution.py:331
  10.1 0.0 copy-start.6
  10.1 5.5 %pack.1 = bf16[8,4,8,16,768]{4,3,2,1,0:T(8,128)(2,1)} custom-call(bf16[8,128,768]{2,1,0:T(8,128)(2,1)} %bitcast.26, bf16[8,128,768]{2,1,0:T(8,128)(2,1)} %bitcast.27, bf16[8,128,768]{2,1,0:T(8,128)(2,1)} %bitcast.28, bf16[8,128,768]{2,1,0:T(8,128)(2,1)} %bitcast.29), custom_call_target="tpu_custom_call" | custom-call | bytes 12582912 | tf_op jit(solution)/shard_map/pack/pallas_call | solution.py:252
  15.6 0.0 collective-permute-done.2.outer_v
  15.6 1.3 collective-permute-start.3
  16.9 0.0 copy-done.6
  16.9 0.7 copy.26.mask
  17.7 0.6 pad_add_fusion.place
  18.2 9.0 %all-to-all-start = ((bf16[8,4,8,16,768]{4,3,2,1,0:T(8,128)(2,1)}), bf16[8,4,8,16,768]{4,3,2,1,0:T(8,128)(2,1)}, u32[]{:S(2)}, u32[]{:S(2)}) async-start(bf16[8,4,8,16,768]{4,3,2,1,0:T(8,128)(2,1)} %pack.1), calls=%async_computation | async-start | bytes 12582912 | tf_op jit(solution)/shard_map/all_to_all | solution.py:345
  27.2 2.5 %collective-permute-done.1.outer_k = bf16[512,768]{1,0:T(8,128)(2,1)} collective-permute-done((bf16[512,768]{1,0:T(8,128)(2,1)S(1)}, bf16[512,768]{1,0:T(8,128)(2,1)}, u32[]{:S(2)}, u32[]{:S(2)}) %collective-permute-start.1) | collective-permute-done | bytes 786464 | tf_op jit(solution)/shard_map/ppermute | solution.py:331
  29.7 0.0 collective-permute-done.inner_kv
  29.7 8.2 %collective-permute-done.3.far_v = bf16[512,768]{1,0:T(8,128)(2,1)S(1)} collective-permute-done((bf16[512,768]{1,0:T(8,128)(2,1)}, bf16[512,768]{1,0:T(8,128)(2,1)S(1)}, u32[]{:S(2)}, u32[]{:S(2)}) %collective-permute-start.3) | collective-permute-done | bytes 786464 | tf_op jit(solution)/shard_map/ppermute | solution.py:333
  37.9 0.0 copy-start.7
  37.9 0.9 copy-done.7
  38.8 50.6 %row_heads.1 = (bf16[1024,768]{1,0:T(8,128)(2,1)}, bf16[1024,768]{1,0:T(8,128)(2,1)}, f32[1024,768]{1,0:T(8,128)}, f32[1024,768]{1,0:T(8,128)}, bf16[2,512,768]{...) custom-call(s32[3]{0:T(128)} %pad_add_fusion.place, s32[64,9]{1,0:T(8,128)} %copy.26.mask, ...), custom_call_target="tpu_custom_call" | custom-call | flops 241591910400 | bytes 23592960 | tf_op jit(solution)/shard_map/row_heads/pallas_call | solution.py:121
  89.4 1.9 collective-permute-start.5
  91.3 4.5 %collective-permute-start.6 = (bf16[512,768]{1,0:T(8,128)(2,1)}, bf16[512,768]{1,0:T(8,128)(2,1)}, u32[]{:S(2)}, u32[]{:S(2)}) collective-permute-start(bf16[512,768]{1,0:T(8,128)(2,1)} %get-tuple-element.85), channel_id=1, source_target_pairs={{4,8},{12,16},{20,24},{8,4},{16,12},{24,20},{5,9},{13,17},{21,25},... | collective-permute-start | bytes 2359304 | tf_op jit(solution)/shard_map/ppermute | solution.py:341
  95.9 0.1 collective-permute-start.4
  95.9 0.7 all-to-all-done.x
  96.6 14.8 %col_heads.2.earlier = bf16[8,4,8,16,384]{4,3,2,1,0:T(8,128)(2,1)} custom-call(s32[1]{0:T(128)} %bitcast.9.me, s32[64,64]{1,0:T(8,128)} %mask.4, bf16[8,4,8,16,768]{4,3,2,1,0:T(8,128)(2,1)} %all-to-all-done.x, bf16[1024,768]{1,0:T(8,128)(2,1)} %get-tuple-element.51.earlier), custom_call_target="tpu_custom_call" | custom-call | flops 48318382080 | bytes 12582912 | tf_op jit(solution)/shard_map/col_heads/pallas_call | solution.py:203
  111.4 3.1 %collective-permute-done.5 = bf16[512,768]{1,0:T(8,128)(2,1)S(1)} collective-permute-done((bf16[512,768]{1,0:T(8,128)(2,1)}, bf16[512,768]{1,0:T(8,128)(2,1)S(1)}, u32[]{:S(2)}, u32[]{:S(2)}) %collective-permute-start.5) | collective-permute-done | bytes 786464 | tf_op jit(solution)/shard_map/ppermute | solution.py:341
  114.5 0.0 copy-start.4
  114.5 0.0 collective-permute-done.4
  114.5 0.0 copy-start.3
  114.5 0.9 copy-done.4
  115.4 0.5 copy-done.3
  115.9 11.2 %all-to-all-start.1 = ((bf16[8,4,8,16,384]{4,3,2,1,0:T(8,128)(2,1)}), bf16[8,4,8,16,384]{4,3,2,1,0:T(8,128)(2,1)S(1)}, u32[]{:S(2)}, u32[]{:S(2)}) async-start(bf16[8,4,8,16,384]{4,3,2,1,0:T(8,128)(2,1)} %col_heads.2.earlier), calls=%async_computation.1 | async-start | bytes 6291456 | tf_op jit(solution)/shard_map/all_to_all | solution.py:345
  127.2 15.1 %col_heads.3 = (bf16[4,8,16,384]{3,2,1,0:T(8,128)(2,1)}, bf16[4,8,16,384]{3,2,1,0:T(8,128)(2,1)}, bf16[4,8,16,384]{3,2,1,0:T(8,128)(2,1)}, bf16[4,8,16,384]{3,2,...) custom-call(s32[1]{0:T(128)} %bitcast.9.me, ...), custom_call_target="tpu_custom_call" | custom-call | flops 48318382080 | bytes 12582912 | tf_op jit(solution)/shard_map/col_heads/pallas_call | solution.py:203
  142.3 0.0 collective-permute-done.6
  142.3 0.4 collective-permute-start.7
  142.7 0.0 collective-permute-start.10
  142.7 1.8 collective-permute-start.11
  144.5 1.2 collective-permute-start.12
  145.7 0.5 collective-permute-start.13
  146.2 0.0 copy-start.2
  146.2 2.2 %bitcast_select_fusion.1 = (bf16[512,768]{1,0:T(8,128)(2,1)S(1)}, bf16[512,768]{1,0:T(8,128)(2,1)S(1)}, bf16[512,768]{1,0:T(8,128)(2,1)S(1)}, bf16[512,768]{1,0:T(8,128)(2,1)S(1)}) fusion(bf16[512,768]{1,0:T(8,128)(2,1)} %collective-permute-done.6, pred[]{:T(512)S(6)} %eq.17, bf16[2,512,768]{2,1,0:T(8,128)(2,1)} %copy-done.3, bf16[512,768]{1,0:T(8,128)(2,1)} %copy-done.4), kind=kLoop, calls=%fused_computation.4 | loop fusion | flops 1572864 | bytes 6291457 | tf_op jit(solution)/shard_map/jit(_where)/select_n | solution.py:403
  148.4 0.0 collective-permute-done.7.refs_1_
  148.4 0.0 copy-start.5
  148.4 1.3 collective-permute-start.8
  149.7 21.8 %collective-permute-done.10.refs_2_ = bf16[4,8,16,384]{3,2,1,0:T(8,128)(2,1)} collective-permute-done((bf16[4,8,16,384]{3,2,1,0:T(8,128)(2,1)}, bf16[4,8,16,384]{3,2,1,0:T(8,128)(2,1)}, u32[]{:S(2)}, u32[]{:S(2)}) %collective-permute-start.10) | collective-permute-done | bytes 393248 | tf_op jit(solution)/shard_map/ppermute | solution.py:390
  171.5 2.6 %collective-permute-start.9 = (bf16[4,8,16,384]{3,2,1,0:T(8,128)(2,1)}, bf16[4,8,16,384]{3,2,1,0:T(8,128)(2,1)}, u32[]{:S(2)}, u32[]{:S(2)}) collective-permute-start(bf16[4,8,16,384]{3,2,1,0:T(8,128)(2,1)} %get-tuple-element.91), channel_id=1, source_target_pairs={{0,28},{4,24},{8,20},{12,16},{16,12},{20,8},{24,4},{28,0},{1,29},{... | collective-permute-start | bytes 1179656 | tf_op jit(solution)/shard_map/ppermute | solution.py:393
  174.1 0.0 copy-done.2
  174.1 0.0 copy-start.1
  174.1 1.5 add_convert_fusion.1
  175.5 0.0 copy-done.5
  175.5 1.0 copy-done.1
  176.5 1.5 add_convert_fusion
  178.0 0.0 all-to-all-done.1.refs_0_
  178.0 0.0 copy-start
  178.0 1.6 copy-done
  179.6 3.0 %unpack.3 = (bf16[8,128,768]{2,1,0:T(8,128)(2,1)}, bf16[8,128,768]{2,1,0:T(8,128)(2,1)}, bf16[8,128,768]{2,1,0:T(8,128)(2,1)}, bf16[8,128,768]{2,1,0:T(8,128)(2,1)}) custom-call(s32[1]{0:T(128)} %bitcast.9.me, bf16[8,4,8,16,384]{4,3,2,1,0:T(8,128)(2,1)} %copy-done), custom_call_target="tpu_custom_call" | custom-call | bytes 6291456 | tf_op jit(solution)/shard_map/unpack/pallas_call | solution.py:300
  182.6 0.0 collective-permute-done.11.refs_3_
  182.6 0.0 collective-permute-done.12.refs_4_
  182.7 0.0 collective-permute-done.13.refs_5_
  182.7 2.6 %unpack.4 = (bf16[8,128,768]{2,1,0:T(8,128)(2,1)}, bf16[8,128,768]{2,1,0:T(8,128)(2,1)}, bf16[8,128,768]{2,1,0:T(8,128)(2,1)}, bf16[8,128,768]{2,1,0:T(8,128)(2,1)}) custom-call(s32[1]{0:T(128)} %bitcast.9.me, bf16[4,8,16,384]{3,2,1,0:T(8,128)(2,1)} %get-tuple-element.92.refs_0_, ...), custom_call_target="tpu_custom_call", output_to_operand_aliasing={{0}: (7, {}), {1}: (8, {}), {2}: (9, {}), {3}: (10, {})} | custom-call | bytes 4718592 | tf_op jit(solution)/shard_map/unpack/pallas_call | solution.py:300
  185.3 12.8 %collective-permute-done.8.refs_0_ = bf16[4,8,16,384]{3,2,1,0:T(8,128)(2,1)} collective-permute-done((bf16[4,8,16,384]{3,2,1,0:T(8,128)(2,1)}, bf16[4,8,16,384]{3,2,1,0:T(8,128)(2,1)}, u32[]{:S(2)}, u32[]{:S(2)}) %collective-permute-start.8) | collective-permute-done | bytes 393248 | tf_op jit(solution)/shard_map/ppermute | solution.py:393
  198.1 1.1 collective-permute-done.9.refs_1_
  199.2 1.9 unpack.5
Async XLA Ops:
  2.9 12.7 %collective-permute-start.2 = (bf16[512,768]{1,0:T(8,128)(2,1)S(1)}, bf16[512,768]{1,0:T(8,128)(2,1)}, u32[]{:S(2)}, u32[]{:S(2)}) collective-permute-start(bf16[512,768]{1,0:T(8,128)(2,1)S(1)} %get-tuple-element.65), channel_id=1, source_target_pairs={{4,8},{20,24},{8,4},{24,20},{12,28},{16,0},{5,9},{21,25},{9,5},{25... | collective-permute-start | bytes 2359304 | tf_op jit(solution)/shard_map/ppermute | solution.py:330
  6.9 22.8 %collective-permute-start = (bf16[2,512,768]{2,1,0:T(8,128)(2,1)S(1)}, bf16[2,512,768]{2,1,0:T(8,128)(2,1)}, u32[]{:S(2)}, u32[]{:S(2)}) collective-permute-start(bf16[2,512,768]{2,1,0:T(8,128)(2,1)S(1)} %pad_maximum_fusion), channel_id=1, source_target_pairs={{0,4},{4,0},{8,12},{12,8},{16,20},{20,16},{24,28},{28,24},{1,5},{5... | collective-permute-start | bytes 4718600 | tf_op jit(solution)/shard_map/ppermute | solution.py:332
  6.9 22.8 %collective-permute-start.1 = (bf16[512,768]{1,0:T(8,128)(2,1)S(1)}, bf16[512,768]{1,0:T(8,128)(2,1)}, u32[]{:S(2)}, u32[]{:S(2)}) collective-permute-start(bf16[512,768]{1,0:T(8,128)(2,1)S(1)} %get-tuple-element.60), channel_id=1, source_target_pairs={{4,8},{12,16},{20,24},{8,4},{16,12},{24,20},{5,9},{13,17},{21,25},... | collective-permute-start | bytes 2359304 | tf_op jit(solution)/shard_map/ppermute | solution.py:331
  10.1 6.8 %copy-start.6 = (s32[64,9]{0,1:T(8,128)S(1)}, s32[64,9]{0,1:T(8,128)}, u32[]{:S(2)}) copy-start(s32[64,9]{0,1:T(8,128)} %param.14) | copy-start | bytes 6916
  15.6 22.3 %collective-permute-start.3 = (bf16[512,768]{1,0:T(8,128)(2,1)}, bf16[512,768]{1,0:T(8,128)(2,1)S(1)}, u32[]{:S(2)}, u32[]{:S(2)}) collective-permute-start(bf16[512,768]{1,0:T(8,128)(2,1)} %collective-permute-done.2.outer_v), channel_id=1, source_target_pairs={{28,16},{0,12},{29,17},{1,13},{30,18},{2,14},{31,19},{3,15}} | collective-permute-start | bytes 2359304 | tf_op jit(solution)/shard_map/ppermute | solution.py:333
  18.2 78.4 %all-to-all-start = ((bf16[8,4,8,16,768]{4,3,2,1,0:T(8,128)(2,1)}), bf16[8,4,8,16,768]{4,3,2,1,0:T(8,128)(2,1)}, u32[]{:S(2)}, u32[]{:S(2)}) async-start(bf16[8,4,8,16,768]{4,3,2,1,0:T(8,128)(2,1)} %pack.1), calls=%async_computation | async-start | bytes 12582912 | tf_op jit(solution)/shard_map/all_to_all | solution.py:345
  37.9 0.9 copy-start.7
  89.4 25.1 %collective-permute-start.5 = (bf16[512,768]{1,0:T(8,128)(2,1)}, bf16[512,768]{1,0:T(8,128)(2,1)S(1)}, u32[]{:S(2)}, u32[]{:S(2)}) collective-permute-start(bf16[512,768]{1,0:T(8,128)(2,1)} %get-tuple-element.72), channel_id=1, source_target_pairs={{4,8},{12,16},{20,24},{8,4},{16,12},{24,20},{5,9},{13,17},{21,25},... | collective-permute-start | bytes 2359304 | tf_op jit(solution)/shard_map/ppermute | solution.py:341
  91.3 50.9 %collective-permute-start.6 = (bf16[512,768]{1,0:T(8,128)(2,1)}, bf16[512,768]{1,0:T(8,128)(2,1)}, u32[]{:S(2)}, u32[]{:S(2)}) collective-permute-start(bf16[512,768]{1,0:T(8,128)(2,1)} %get-tuple-element.85), channel_id=1, source_target_pairs={{4,8},{12,16},{20,24},{8,4},{16,12},{24,20},{5,9},{13,17},{21,25},... | collective-permute-start | bytes 2359304 | tf_op jit(solution)/shard_map/ppermute | solution.py:341
  95.9 18.7 %collective-permute-start.4 = (bf16[2,512,768]{2,1,0:T(8,128)(2,1)}, bf16[2,512,768]{2,1,0:T(8,128)(2,1)S(1)}, u32[]{:S(2)}, u32[]{:S(2)}) collective-permute-start(bf16[2,512,768]{2,1,0:T(8,128)(2,1)} %get-tuple-element.71), channel_id=1, source_target_pairs={{0,4},{4,0},{8,12},{12,8},{16,20},{20,16},{24,28},{28,24},{1,5},{5... | collective-permute-start | bytes 4718600 | tf_op jit(solution)/shard_map/ppermute | solution.py:340
  114.5 0.9 copy-start.4
  114.5 1.4 copy-start.3
  115.9 62.1 %all-to-all-start.1 = ((bf16[8,4,8,16,384]{4,3,2,1,0:T(8,128)(2,1)}), bf16[8,4,8,16,384]{4,3,2,1,0:T(8,128)(2,1)S(1)}, u32[]{:S(2)}, u32[]{:S(2)}) async-start(bf16[8,4,8,16,384]{4,3,2,1,0:T(8,128)(2,1)} %col_heads.2.earlier), calls=%async_computation.1 | async-start | bytes 6291456 | tf_op jit(solution)/shard_map/all_to_all | solution.py:345
  142.3 6.1 %collective-permute-start.7 = (bf16[4,8,16,384]{3,2,1,0:T(8,128)(2,1)}, bf16[4,8,16,384]{3,2,1,0:T(8,128)(2,1)S(1)}, u32[]{:S(2)}, u32[]{:S(2)}) collective-permute-start(bf16[4,8,16,384]{3,2,1,0:T(8,128)(2,1)} %get-tuple-element.89), channel_id=1, source_target_pairs={{0,4},{4,0},{8,12},{12,8},{16,20},{20,16},{24,28},{28,24},{1,5},{5... | collective-permute-start | bytes 1179656 | tf_op jit(solution)/shard_map/ppermute | solution.py:390
  142.7 28.8 %collective-permute-start.10 = (bf16[4,8,16,384]{3,2,1,0:T(8,128)(2,1)}, bf16[4,8,16,384]{3,2,1,0:T(8,128)(2,1)}, u32[]{:S(2)}, u32[]{:S(2)}) collective-permute-start(bf16[4,8,16,384]{3,2,1,0:T(8,128)(2,1)} %get-tuple-element.94), channel_id=1, source_target_pairs={{0,8},{4,12},{8,0},{12,4},{16,24},{20,28},{24,16},{28,20},{1,9},{5... | collective-permute-start | bytes 1179656 | tf_op jit(solution)/shard_map/ppermute | solution.py:390
  142.7 39.9 %collective-permute-start.11 = (bf16[4,8,16,384]{3,2,1,0:T(8,128)(2,1)}, bf16[4,8,16,384]{3,2,1,0:T(8,128)(2,1)}, u32[]{:S(2)}, u32[]{:S(2)}) collective-permute-start(bf16[4,8,16,384]{3,2,1,0:T(8,128)(2,1)} %get-tuple-element.95), channel_id=1, source_target_pairs={{0,12},{4,8},{8,4},{12,0},{16,28},{20,24},{24,20},{28,16},{1,13},{... | collective-permute-start | bytes 1179656 | tf_op jit(solution)/shard_map/ppermute | solution.py:390
  144.5 38.1 %collective-permute-start.12 = (bf16[4,8,16,384]{3,2,1,0:T(8,128)(2,1)}, bf16[4,8,16,384]{3,2,1,0:T(8,128)(2,1)}, u32[]{:S(2)}, u32[]{:S(2)}) collective-permute-start(bf16[4,8,16,384]{3,2,1,0:T(8,128)(2,1)} %get-tuple-element.96), channel_id=1, source_target_pairs={{0,16},{4,20},{8,24},{12,28},{16,0},{20,4},{24,8},{28,12},{1,17},{... | collective-permute-start | bytes 1179656 | tf_op jit(solution)/shard_map/ppermute | solution.py:390
  145.7 37.0 %collective-permute-start.13 = (bf16[4,8,16,384]{3,2,1,0:T(8,128)(2,1)}, bf16[4,8,16,384]{3,2,1,0:T(8,128)(2,1)}, u32[]{:S(2)}, u32[]{:S(2)}) collective-permute-start(bf16[4,8,16,384]{3,2,1,0:T(8,128)(2,1)} %get-tuple-element.97), channel_id=1, source_target_pairs={{0,20},{4,16},{8,28},{12,24},{16,4},{20,0},{24,12},{28,8},{1,21},{... | collective-permute-start | bytes 1179656 | tf_op jit(solution)/shard_map/ppermute | solution.py:390
  146.2 27.9 %copy-start.2 = (f32[1024,768]{1,0:T(8,128)S(1)}, f32[1024,768]{1,0:T(8,128)}, u32[]{:S(2)}) copy-start(f32[1024,768]{1,0:T(8,128)} %get-tuple-element.69) | copy-start | bytes 9437188
  148.4 27.1 %copy-start.5 = (bf16[4,8,16,384]{3,2,1,0:T(8,128)(2,1)}, bf16[4,8,16,384]{3,2,1,0:T(8,128)(2,1)S(1)}, u32[]{:S(2)}) copy-start(bf16[4,8,16,384]{3,2,1,0:T(8,128)(2,1)S(1)} %collective-permute-done.7.refs_1_) | copy-start | bytes 1179652
  148.4 49.7 %collective-permute-start.8 = (bf16[4,8,16,384]{3,2,1,0:T(8,128)(2,1)}, bf16[4,8,16,384]{3,2,1,0:T(8,128)(2,1)}, u32[]{:S(2)}, u32[]{:S(2)}) collective-permute-start(bf16[4,8,16,384]{3,2,1,0:T(8,128)(2,1)} %get-tuple-element.90), channel_id=1, source_target_pairs={{0,24},{4,28},{8,16},{12,20},{16,8},{20,12},{24,0},{28,4},{1,25},{... | collective-permute-start | bytes 1179656 | tf_op jit(solution)/shard_map/ppermute | solution.py:393
  171.5 27.7 %collective-permute-start.9 = (bf16[4,8,16,384]{3,2,1,0:T(8,128)(2,1)}, bf16[4,8,16,384]{3,2,1,0:T(8,128)(2,1)}, u32[]{:S(2)}, u32[]{:S(2)}) collective-permute-start(bf16[4,8,16,384]{3,2,1,0:T(8,128)(2,1)} %get-tuple-element.91), channel_id=1, source_target_pairs={{0,28},{4,24},{8,20},{12,16},{16,12},{20,8},{24,4},{28,0},{1,29},{... | collective-permute-start | bytes 1179656 | tf_op jit(solution)/shard_map/ppermute | solution.py:393
  174.1 2.5 %copy-start.1 = (f32[1024,768]{1,0:T(8,128)S(1)}, f32[1024,768]{1,0:T(8,128)}, u32[]{:S(2)}) copy-start(f32[1024,768]{1,0:T(8,128)} %get-tuple-element.75) | copy-start | bytes 9437188
  178.0 1.6 copy-start

commit v10 on v9

--- a/solution.py
+++ b/solution.py
@@ -382,18 +382,17 @@
     where = me.reshape(1)
     partners = [[(i, i ^ k) for i in range(n)] for k in range(n)]
     first = col_attention(where, col_mask, moved, row_output, 0, half, False)
-    first, inner, outer_k = lax.optimization_barrier((first, inner, outer_k))
+    first, inner, outer_v = lax.optimization_barrier((first, inner, outer_v))
     second = col_attention(where, col_mask, moved, first, half, heads - half, True)
-    second, outer_v = lax.optimization_barrier((second, outer_v))
     first = exchanged(first)
     arrived = [second[0]] + [
-        lax.ppermute(second[k], "ctx", partners[k]) for k in range(1, n - 2)
+        lax.ppermute(second[k], "ctx", partners[k]) for k in range(1, n - 1)
     ]
-    *last, arrived[1] = lax.optimization_barrier((second[n - 2], second[n - 1], arrived[1]))
-    arrived += [lax.ppermute(part, "ctx", pairs) for part, pairs in zip(last, partners[n - 2 :])]
+    last, arrived[1] = lax.optimization_barrier((second[n - 1], arrived[1]))
+    arrived.append(lax.ppermute(last, "ctx", partners[n - 1]))
     col_feat = col_query.shape[1]
     col_results = unpacked(where, first, None, 0, col_feat, [])
-    for some in (list(range(n - 2)), [n - 2, n - 1]):
+    for some in (list(range(n - 1)), [n - 1]):
         col_results = unpacked(
             where, [arrived[k] for k in some], some, half * HEAD_DIM, col_feat, col_results
         )

time: 205 us -> 205 us (level)
    ppermute x5 -> x6, waiting for transfers between devices: 21.8 us -> 37.3 us  [body(): lax.ppermute(second[k], 'ctx', partners[k])]
    ppermute x2 -> x1, waiting for transfers between devices: 13.9 us -> 0.01 us  [body(): arrived.append(lax.ppermute(last, 'ctx', partners[n - 1]))]
    ppermute x1, waiting for transfers between devices: 0.01 us -> 3.08 us  [handed_back(): lax.ppermute(outer_v, 'ctx', pairs)]
    ppermute x1, waiting for transfers between devices: 3.08 us -> 0.01 us  [handed_back(): lax.ppermute(outer_k, 'ctx', pairs)]
    ppermute x1, starting transfers between devices: 1.92 us -> 4.54 us  [handed_back(): lax.ppermute(outer_k, 'ctx', pairs)]
    ppermute x1, starting transfers between devices: 4.54 us -> 1.92 us  [handed_back(): lax.ppermute(outer_v, 'ctx', pairs)]
    ppermute x5 -> x6, starting transfers between devices: 3.92 us -> 5.15 us  [body(): lax.ppermute(second[k], 'ctx', partners[k])]
  transfers between devices with their start and end apart: 16 -> 16, of which waited for: 7 -> 6; matrix products, arithmetic and copies ran while one was open for 3% -> 3% of each run, Pallas kernels for 46% -> 45%
where the time goes in v10:
time: 205 us; the launch traced here: 203 us
  Pallas kernels  93.6 us (46%)
  waiting for transfers between devices  51.7 us (25%)
  starting transfers between devices  43 us (21%)
  local copies, waits for them, and re-layouts  7.66 us (4%)
  other arithmetic  5.88 us (3%)
    pallas_call x1, Pallas kernels, row_attention(): pl.pallas_call(functools.partial(row_kernel, band), grid=(heads,), in_spe...  50.6 us
    ppermute x6, waiting for transfers between devices, body(): lax.ppermute(second[k], 'ctx', partners[k])  37.3 us
    pallas_call x2, Pallas kernels, col_attention(): pl.pallas_call(functools.partial(col_kernel, n_parts), grid=(heads, cols...  29.9 us
    all_to_all x2, starting transfers between devices, exchanged(): return lax.all_to_all(x, 'ctx', 0, 0, tiled=True)  20.2 us
    ppermute x1, waiting for transfers between devices, swapped(): lax.ppermute(passed, 'ctx', second)  8.18 us
    pallas_call x3, Pallas kernels, unpacked(): pl.pallas_call(functools.partial(unpack_kernel, partners, start), in_spec...  7.58 us
    unnamed x17, local copies, waits for them, and re-layouts  5.61 us
    pallas_call x1, Pallas kernels, packed(): pl.pallas_call(functools.partial(pack_kernel, n), in_specs=[pl.BlockSpec(...  5.46 us
  transfers between devices with their start and end apart: 16, of which 6 were waited for; matrix products, arithmetic and copies ran while one was open for 3% of the time, Pallas kernels for 45%

profile of v10, /device:TPU:11, one launch (start us, length us, event | category | flops | bytes accessed | tf_op | source)
XLA Modules:
  0.0 202.8 jit_solution(17026458009349417972)
XLA Ops:
  0.7 2.1 %constant_dynamic-slice_fusion = (bf16[512,768]{1,0:T(8,128)(2,1)S(1)}, bf16[1,512,768]{2,1,0:T(8,128)(2,1)S(1)}, bf16[1,512,768]{2,1,0:T(8,128)(2,1)S(1)}, bf16[512,768]{1,0:T(8,128)(2,1)S(1)}) fusion(bf16[1024,768]{1,0:T(8,128)(2,1)} %v.1, s32[]{:T(128)S(6)} %select_n.42, s32[]{:T(128)S(6)} %select_n.41, bf16[1024,768]{1,0:T(8,128)(2,1)} %k.1), kind=kLoop, calls=%fused_computation.9 | loop fusion | bytes 6291464 | tf_op jit(solution)/shard_map/dynamic_slice | solution.py:363
  2.7 0.1 pad_maximum_fusion
  2.9 4.1 %collective-permute-start.2 = (bf16[512,768]{1,0:T(8,128)(2,1)S(1)}, bf16[512,768]{1,0:T(8,128)(2,1)}, u32[]{:S(2)}, u32[]{:S(2)}) collective-permute-start(bf16[512,768]{1,0:T(8,128)(2,1)S(1)} %get-tuple-element.55), channel_id=1, source_target_pairs={{4,8},{20,24},{8,4},{24,20},{12,28},{16,0},{5,9},{21,25},{9,5},{25... | collective-permute-start | bytes 2359304 | tf_op jit(solution)/shard_map/ppermute | solution.py:330
  6.9 0.0 collective-permute-start
  6.9 3.2 %collective-permute-start.1 = (bf16[512,768]{1,0:T(8,128)(2,1)S(1)}, bf16[512,768]{1,0:T(8,128)(2,1)}, u32[]{:S(2)}, u32[]{:S(2)}) collective-permute-start(bf16[512,768]{1,0:T(8,128)(2,1)S(1)} %get-tuple-element.50), channel_id=1, source_target_pairs={{4,8},{12,16},{20,24},{8,4},{16,12},{24,20},{5,9},{13,17},{21,25},... | collective-permute-start | bytes 2359304 | tf_op jit(solution)/shard_map/ppermute | solution.py:331
  10.1 0.0 copy-start.6
  10.1 5.5 %pack.1 = bf16[8,4,8,16,768]{4,3,2,1,0:T(8,128)(2,1)} custom-call(bf16[8,128,768]{2,1,0:T(8,128)(2,1)} %bitcast.26, bf16[8,128,768]{2,1,0:T(8,128)(2,1)} %bitcast.27, bf16[8,128,768]{2,1,0:T(8,128)(2,1)} %bitcast.28, bf16[8,128,768]{2,1,0:T(8,128)(2,1)} %bitcast.29), custom_call_target="tpu_custom_call" | custom-call | bytes 12582912 | tf_op jit(solution)/shard_map/pack/pallas_call | solution.py:252
  15.6 0.0 collective-permute-done.2.outer_v
  15.6 1.3 collective-permute-start.3
  16.9 0.0 copy-done.6
  16.9 0.7 copy.26.mask
  17.7 0.6 pad_add_fusion.place
  18.2 9.0 %all-to-all-start = ((bf16[8,4,8,16,768]{4,3,2,1,0:T(8,128)(2,1)}), bf16[8,4,8,16,768]{4,3,2,1,0:T(8,128)(2,1)}, u32[]{:S(2)}, u32[]{:S(2)}) async-start(bf16[8,4,8,16,768]{4,3,2,1,0:T(8,128)(2,1)} %pack.1), calls=%async_computation | async-start | bytes 12582912 | tf_op jit(solution)/shard_map/all_to_all | solution.py:345
  27.2 2.5 %collective-permute-done.1.outer_k = bf16[512,768]{1,0:T(8,128)(2,1)} collective-permute-done((bf16[512,768]{1,0:T(8,128)(2,1)S(1)}, bf16[512,768]{1,0:T(8,128)(2,1)}, u32[]{:S(2)}, u32[]{:S(2)}) %collective-permute-start.1) | collective-permute-done | bytes 786464 | tf_op jit(solution)/shard_map/ppermute | solution.py:331
  29.7 0.0 collective-permute-done.inner_kv
  29.7 8.2 %collective-permute-done.3.far_v = bf16[512,768]{1,0:T(8,128)(2,1)S(1)} collective-permute-done((bf16[512,768]{1,0:T(8,128)(2,1)}, bf16[512,768]{1,0:T(8,128)(2,1)S(1)}, u32[]{:S(2)}, u32[]{:S(2)}) %collective-permute-start.3) | collective-permute-done | bytes 786464 | tf_op jit(solution)/shard_map/ppermute | solution.py:333
  37.9 0.0 copy-start.7
  37.9 0.9 copy-done.7
  38.8 50.6 %row_heads.1 = (bf16[1024,768]{1,0:T(8,128)(2,1)}, bf16[1024,768]{1,0:T(8,128)(2,1)}, f32[1024,768]{1,0:T(8,128)}, f32[1024,768]{1,0:T(8,128)}, bf16[2,512,768]{...) custom-call(s32[3]{0:T(128)} %pad_add_fusion.place, s32[64,9]{1,0:T(8,128)} %copy.26.mask, ...), custom_call_target="tpu_custom_call" | custom-call | flops 241591910400 | bytes 23592960 | tf_op jit(solution)/shard_map/row_heads/pallas_call | solution.py:121
  89.4 1.9 collective-permute-start.5
  91.3 4.5 %collective-permute-start.6 = (bf16[512,768]{1,0:T(8,128)(2,1)}, bf16[512,768]{1,0:T(8,128)(2,1)}, u32[]{:S(2)}, u32[]{:S(2)}) collective-permute-start(bf16[512,768]{1,0:T(8,128)(2,1)} %get-tuple-element.64), channel_id=1, source_target_pairs={{4,8},{12,16},{20,24},{8,4},{16,12},{24,20},{5,9},{13,17},{21,25},... | collective-permute-start | bytes 2359304 | tf_op jit(solution)/shard_map/ppermute | solution.py:341
  95.9 0.1 collective-permute-start.4
  95.9 0.7 all-to-all-done.x
  96.6 14.8 %col_heads.2.earlier = bf16[8,4,8,16,384]{4,3,2,1,0:T(8,128)(2,1)} custom-call(s32[1]{0:T(128)} %bitcast.9.me, s32[64,64]{1,0:T(8,128)} %mask.4, bf16[8,4,8,16,768]{4,3,2,1,0:T(8,128)(2,1)} %all-to-all-done.x, bf16[1024,768]{1,0:T(8,128)(2,1)} %get-tuple-element.41.earlier), custom_call_target="tpu_custom_call" | custom-call | flops 48318382080 | bytes 12582912 | tf_op jit(solution)/shard_map/col_heads/pallas_call | solution.py:203
  111.4 3.1 %collective-permute-done.5 = bf16[512,768]{1,0:T(8,128)(2,1)S(1)} collective-permute-done((bf16[512,768]{1,0:T(8,128)(2,1)}, bf16[512,768]{1,0:T(8,128)(2,1)S(1)}, u32[]{:S(2)}, u32[]{:S(2)}) %collective-permute-start.5) | collective-permute-done | bytes 786464 | tf_op jit(solution)/shard_map/ppermute | solution.py:341
  114.5 0.0 copy-start.4
  114.5 0.0 collective-permute-done.4
  114.5 0.0 copy-start.3
  114.5 0.9 copy-done.4
  115.4 0.5 copy-done.3
  115.9 11.2 %all-to-all-start.1 = ((bf16[8,4,8,16,384]{4,3,2,1,0:T(8,128)(2,1)}), bf16[8,4,8,16,384]{4,3,2,1,0:T(8,128)(2,1)S(1)}, u32[]{:S(2)}, u32[]{:S(2)}) async-start(bf16[8,4,8,16,384]{4,3,2,1,0:T(8,128)(2,1)} %col_heads.2.earlier), calls=%async_computation.1 | async-start | bytes 6291456 | tf_op jit(solution)/shard_map/all_to_all | solution.py:345
  127.2 15.1 %col_heads.3 = (bf16[4,8,16,384]{3,2,1,0:T(8,128)(2,1)}, bf16[4,8,16,384]{3,2,1,0:T(8,128)(2,1)}, bf16[4,8,16,384]{3,2,1,0:T(8,128)(2,1)}, bf16[4,8,16,384]{3,2,...) custom-call(s32[1]{0:T(128)} %bitcast.9.me, ...), custom_call_target="tpu_custom_call" | custom-call | flops 48318382080 | bytes 12582912 | tf_op jit(solution)/shard_map/col_heads/pallas_call | solution.py:203
  142.2 0.4 collective-permute-start.7
  142.6 0.0 collective-permute-start.9
  142.6 1.8 collective-permute-start.10
  144.4 1.2 collective-permute-start.11
  145.6 0.0 collective-permute-done.6
  145.7 0.5 collective-permute-start.12
  146.1 0.0 copy-start.2
  146.1 2.2 %bitcast_select_fusion.1 = (bf16[512,768]{1,0:T(8,128)(2,1)S(1)}, bf16[512,768]{1,0:T(8,128)(2,1)S(1)}, bf16[512,768]{1,0:T(8,128)(2,1)S(1)}, bf16[512,768]{1,0:T(8,128)(2,1)S(1)}) fusion(bf16[512,768]{1,0:T(8,128)(2,1)} %copy-done.4, pred[]{:T(512)S(6)} %eq.17, bf16[2,512,768]{2,1,0:T(8,128)(2,1)} %copy-done.3, bf16[512,768]{1,0:T(8,128)(2,1)} %collective-permute-done.6), kind=kLoop, calls=%fused_computation.4 | loop fusion | flops 1572864 | bytes 6291457 | tf_op jit(solution)/shard_map/jit(_where)/select_n | solution.py:402
  148.3 0.0 collective-permute-done.7.refs_1_
  148.4 0.0 copy-start.5
  148.4 1.3 collective-permute-start.13
  149.6 21.9 %collective-permute-done.9.refs_2_ = bf16[4,8,16,384]{3,2,1,0:T(8,128)(2,1)} collective-permute-done((bf16[4,8,16,384]{3,2,1,0:T(8,128)(2,1)}, bf16[4,8,16,384]{3,2,1,0:T(8,128)(2,1)}, u32[]{:S(2)}, u32[]{:S(2)}) %collective-permute-start.9) | collective-permute-done | bytes 393248 | tf_op jit(solution)/shard_map/ppermute | solution.py:389
  171.5 2.6 %collective-permute-start.8 = (bf16[4,8,16,384]{3,2,1,0:T(8,128)(2,1)}, bf16[4,8,16,384]{3,2,1,0:T(8,128)(2,1)}, u32[]{:S(2)}, u32[]{:S(2)}) collective-permute-start(bf16[4,8,16,384]{3,2,1,0:T(8,128)(2,1)} %get-tuple-element.70), channel_id=1, source_target_pairs={{0,28},{4,24},{8,20},{12,16},{16,12},{20,8},{24,4},{28,0},{1,29},{... | collective-permute-start | bytes 1179656 | tf_op jit(solution)/shard_map/ppermute | solution.py:392
  174.1 0.0 copy-done.2
  174.1 0.0 copy-start.1
  174.1 1.5 add_convert_fusion.1
  175.5 0.0 copy-done.5
  175.5 1.0 copy-done.1
  176.5 1.5 add_convert_fusion
  178.0 0.0 all-to-all-done.1.refs_0_
  178.0 0.0 copy-start
  178.0 1.6 copy-done
  179.6 3.0 %unpack.3 = (bf16[8,128,768]{2,1,0:T(8,128)(2,1)}, bf16[8,128,768]{2,1,0:T(8,128)(2,1)}, bf16[8,128,768]{2,1,0:T(8,128)(2,1)}, bf16[8,128,768]{2,1,0:T(8,128)(2,1)}) custom-call(s32[1]{0:T(128)} %bitcast.9.me, bf16[8,4,8,16,384]{4,3,2,1,0:T(8,128)(2,1)} %copy-done), custom_call_target="tpu_custom_call" | custom-call | bytes 6291456 | tf_op jit(solution)/shard_map/unpack/pallas_call | solution.py:300
  182.6 0.0 collective-permute-done.10.refs_3_
  182.6 0.0 collective-permute-done.11.refs_4_
  182.7 0.0 collective-permute-done.12.refs_5_
  182.7 15.4 %collective-permute-done.13.refs_6_ = bf16[4,8,16,384]{3,2,1,0:T(8,128)(2,1)} collective-permute-done((bf16[4,8,16,384]{3,2,1,0:T(8,128)(2,1)}, bf16[4,8,16,384]{3,2,1,0:T(8,128)(2,1)}, u32[]{:S(2)}, u32[]{:S(2)}) %collective-permute-start.13) | collective-permute-done | bytes 393248 | tf_op jit(solution)/shard_map/ppermute | solution.py:389
  198.1 2.8 %unpack.4 = (bf16[8,128,768]{2,1,0:T(8,128)(2,1)}, bf16[8,128,768]{2,1,0:T(8,128)(2,1)}, bf16[8,128,768]{2,1,0:T(8,128)(2,1)}, bf16[8,128,768]{2,1,0:T(8,128)(2,1)}) custom-call(s32[1]{0:T(128)} %bitcast.9.me, bf16[4,8,16,384]{3,2,1,0:T(8,128)(2,1)} %get-tuple-element.71.refs_0_, ...), custom_call_target="tpu_custom_call", output_to_operand_aliasing={{0}: (8, {}), {1}: (9, {}), {2}: (10, {}), {3}: (11, {})} | custom-call | bytes 5505024 | tf_op jit(solution)/shard_map/unpack/pallas_call | solution.py:300
  200.9 0.0 collective-permute-done.8.refs_0_
  200.9 1.8 unpack.5
Async XLA Ops:
  2.9 12.7 %collective-permute-start.2 = (bf16[512,768]{1,0:T(8,128)(2,1)S(1)}, bf16[512,768]{1,0:T(8,128)(2,1)}, u32[]{:S(2)}, u32[]{:S(2)}) collective-permute-start(bf16[512,768]{1,0:T(8,128)(2,1)S(1)} %get-tuple-element.55), channel_id=1, source_target_pairs={{4,8},{20,24},{8,4},{24,20},{12,28},{16,0},{5,9},{21,25},{9,5},{25... | collective-permute-start | bytes 2359304 | tf_op jit(solution)/shard_map/ppermute | solution.py:330
  6.9 22.8 %collective-permute-start = (bf16[2,512,768]{2,1,0:T(8,128)(2,1)S(1)}, bf16[2,512,768]{2,1,0:T(8,128)(2,1)}, u32[]{:S(2)}, u32[]{:S(2)}) collective-permute-start(bf16[2,512,768]{2,1,0:T(8,128)(2,1)S(1)} %pad_maximum_fusion), channel_id=1, source_target_pairs={{0,4},{4,0},{8,12},{12,8},{16,20},{20,16},{24,28},{28,24},{1,5},{5... | collective-permute-start | bytes 4718600 | tf_op jit(solution)/shard_map/ppermute | solution.py:332
  6.9 22.8 %collective-permute-start.1 = (bf16[512,768]{1,0:T(8,128)(2,1)S(1)}, bf16[512,768]{1,0:T(8,128)(2,1)}, u32[]{:S(2)}, u32[]{:S(2)}) collective-permute-start(bf16[512,768]{1,0:T(8,128)(2,1)S(1)} %get-tuple-element.50), channel_id=1, source_target_pairs={{4,8},{12,16},{20,24},{8,4},{16,12},{24,20},{5,9},{13,17},{21,25},... | collective-permute-start | bytes 2359304 | tf_op jit(solution)/shard_map/ppermute | solution.py:331
  10.1 6.8 %copy-start.6 = (s32[64,9]{0,1:T(8,128)S(1)}, s32[64,9]{0,1:T(8,128)}, u32[]{:S(2)}) copy-start(s32[64,9]{0,1:T(8,128)} %param.14) | copy-start | bytes 6916
  15.6 22.3 %collective-permute-start.3 = (bf16[512,768]{1,0:T(8,128)(2,1)}, bf16[512,768]{1,0:T(8,128)(2,1)S(1)}, u32[]{:S(2)}, u32[]{:S(2)}) collective-permute-start(bf16[512,768]{1,0:T(8,128)(2,1)} %collective-permute-done.2.outer_v), channel_id=1, source_target_pairs={{28,16},{0,12},{29,17},{1,13},{30,18},{2,14},{31,19},{3,15}} | collective-permute-start | bytes 2359304 | tf_op jit(solution)/shard_map/ppermute | solution.py:333
  18.2 78.4 %all-to-all-start = ((bf16[8,4,8,16,768]{4,3,2,1,0:T(8,128)(2,1)}), bf16[8,4,8,16,768]{4,3,2,1,0:T(8,128)(2,1)}, u32[]{:S(2)}, u32[]{:S(2)}) async-start(bf16[8,4,8,16,768]{4,3,2,1,0:T(8,128)(2,1)} %pack.1), calls=%async_computation | async-start | bytes 12582912 | tf_op jit(solution)/shard_map/all_to_all | solution.py:345
  37.9 0.9 copy-start.7
  89.4 25.1 %collective-permute-start.5 = (bf16[512,768]{1,0:T(8,128)(2,1)}, bf16[512,768]{1,0:T(8,128)(2,1)S(1)}, u32[]{:S(2)}, u32[]{:S(2)}) collective-permute-start(bf16[512,768]{1,0:T(8,128)(2,1)} %get-tuple-element.62), channel_id=1, source_target_pairs={{4,8},{12,16},{20,24},{8,4},{16,12},{24,20},{5,9},{13,17},{21,25},... | collective-permute-start | bytes 2359304 | tf_op jit(solution)/shard_map/ppermute | solution.py:341
  91.3 54.3 %collective-permute-start.6 = (bf16[512,768]{1,0:T(8,128)(2,1)}, bf16[512,768]{1,0:T(8,128)(2,1)}, u32[]{:S(2)}, u32[]{:S(2)}) collective-permute-start(bf16[512,768]{1,0:T(8,128)(2,1)} %get-tuple-element.64), channel_id=1, source_target_pairs={{4,8},{12,16},{20,24},{8,4},{16,12},{24,20},{5,9},{13,17},{21,25},... | collective-permute-start | bytes 2359304 | tf_op jit(solution)/shard_map/ppermute | solution.py:341
  95.9 18.7 %collective-permute-start.4 = (bf16[2,512,768]{2,1,0:T(8,128)(2,1)}, bf16[2,512,768]{2,1,0:T(8,128)(2,1)S(1)}, u32[]{:S(2)}, u32[]{:S(2)}) collective-permute-start(bf16[2,512,768]{2,1,0:T(8,128)(2,1)} %get-tuple-element.61), channel_id=1, source_target_pairs={{0,4},{4,0},{8,12},{12,8},{16,20},{20,16},{24,28},{28,24},{1,5},{5... | collective-permute-start | bytes 4718600 | tf_op jit(solution)/shard_map/ppermute | solution.py:340
  114.5 0.9 copy-start.4
  114.5 1.4 copy-start.3
  115.9 62.1 %all-to-all-start.1 = ((bf16[8,4,8,16,384]{4,3,2,1,0:T(8,128)(2,1)}), bf16[8,4,8,16,384]{4,3,2,1,0:T(8,128)(2,1)S(1)}, u32[]{:S(2)}, u32[]{:S(2)}) async-start(bf16[8,4,8,16,384]{4,3,2,1,0:T(8,128)(2,1)} %col_heads.2.earlier), calls=%async_computation.1 | async-start | bytes 6291456 | tf_op jit(solution)/shard_map/all_to_all | solution.py:345
  142.2 6.1 %collective-permute-start.7 = (bf16[4,8,16,384]{3,2,1,0:T(8,128)(2,1)}, bf16[4,8,16,384]{3,2,1,0:T(8,128)(2,1)S(1)}, u32[]{:S(2)}, u32[]{:S(2)}) collective-permute-start(bf16[4,8,16,384]{3,2,1,0:T(8,128)(2,1)} %get-tuple-element.69), channel_id=1, source_target_pairs={{0,4},{4,0},{8,12},{12,8},{16,20},{20,16},{24,28},{28,24},{1,5},{5... | collective-permute-start | bytes 1179656 | tf_op jit(solution)/shard_map/ppermute | solution.py:389
  142.6 28.8 %collective-permute-start.9 = (bf16[4,8,16,384]{3,2,1,0:T(8,128)(2,1)}, bf16[4,8,16,384]{3,2,1,0:T(8,128)(2,1)}, u32[]{:S(2)}, u32[]{:S(2)}) collective-permute-start(bf16[4,8,16,384]{3,2,1,0:T(8,128)(2,1)} %get-tuple-element.73), channel_id=1, source_target_pairs={{0,8},{4,12},{8,0},{12,4},{16,24},{20,28},{24,16},{28,20},{1,9},{5... | collective-permute-start | bytes 1179656 | tf_op jit(solution)/shard_map/ppermute | solution.py:389
  142.6 40.0 %collective-permute-start.10 = (bf16[4,8,16,384]{3,2,1,0:T(8,128)(2,1)}, bf16[4,8,16,384]{3,2,1,0:T(8,128)(2,1)}, u32[]{:S(2)}, u32[]{:S(2)}) collective-permute-start(bf16[4,8,16,384]{3,2,1,0:T(8,128)(2,1)} %get-tuple-element.74), channel_id=1, source_target_pairs={{0,12},{4,8},{8,4},{12,0},{16,28},{20,24},{24,20},{28,16},{1,13},{... | collective-permute-start | bytes 1179656 | tf_op jit(solution)/shard_map/ppermute | solution.py:389
  144.4 38.2 %collective-permute-start.11 = (bf16[4,8,16,384]{3,2,1,0:T(8,128)(2,1)}, bf16[4,8,16,384]{3,2,1,0:T(8,128)(2,1)}, u32[]{:S(2)}, u32[]{:S(2)}) collective-permute-start(bf16[4,8,16,384]{3,2,1,0:T(8,128)(2,1)} %get-tuple-element.75), channel_id=1, source_target_pairs={{0,16},{4,20},{8,24},{12,28},{16,0},{20,4},{24,8},{28,12},{1,17},{... | collective-permute-start | bytes 1179656 | tf_op jit(solution)/shard_map/ppermute | solution.py:389
  145.7 37.0 %collective-permute-start.12 = (bf16[4,8,16,384]{3,2,1,0:T(8,128)(2,1)}, bf16[4,8,16,384]{3,2,1,0:T(8,128)(2,1)}, u32[]{:S(2)}, u32[]{:S(2)}) collective-permute-start(bf16[4,8,16,384]{3,2,1,0:T(8,128)(2,1)} %get-tuple-element.76), channel_id=1, source_target_pairs={{0,20},{4,16},{8,28},{12,24},{16,4},{20,0},{24,12},{28,8},{1,21},{... | collective-permute-start | bytes 1179656 | tf_op jit(solution)/shard_map/ppermute | solution.py:389
  146.1 27.9 %copy-start.2 = (f32[1024,768]{1,0:T(8,128)S(1)}, f32[1024,768]{1,0:T(8,128)}, u32[]{:S(2)}) copy-start(f32[1024,768]{1,0:T(8,128)} %get-tuple-element.59) | copy-start | bytes 9437188
  148.4 27.2 %copy-start.5 = (bf16[4,8,16,384]{3,2,1,0:T(8,128)(2,1)}, bf16[4,8,16,384]{3,2,1,0:T(8,128)(2,1)S(1)}, u32[]{:S(2)}) copy-start(bf16[4,8,16,384]{3,2,1,0:T(8,128)(2,1)S(1)} %collective-permute-done.7.refs_1_) | copy-start | bytes 1179652
  148.4 49.7 %collective-permute-start.13 = (bf16[4,8,16,384]{3,2,1,0:T(8,128)(2,1)}, bf16[4,8,16,384]{3,2,1,0:T(8,128)(2,1)}, u32[]{:S(2)}, u32[]{:S(2)}) collective-permute-start(bf16[4,8,16,384]{3,2,1,0:T(8,128)(2,1)} %get-tuple-element.77), channel_id=1, source_target_pairs={{0,24},{4,28},{8,16},{12,20},{16,8},{20,12},{24,0},{28,4},{1,25},{... | collective-permute-start | bytes 1179656 | tf_op jit(solution)/shard_map/ppermute | solution.py:389
  171.5 29.4 %collective-permute-start.8 = (bf16[4,8,16,384]{3,2,1,0:T(8,128)(2,1)}, bf16[4,8,16,384]{3,2,1,0:T(8,128)(2,1)}, u32[]{:S(2)}, u32[]{:S(2)}) collective-permute-start(bf16[4,8,16,384]{3,2,1,0:T(8,128)(2,1)} %get-tuple-element.70), channel_id=1, source_target_pairs={{0,28},{4,24},{8,20},{12,16},{16,12},{20,8},{24,4},{28,0},{1,29},{... | collective-permute-start | bytes 1179656 | tf_op jit(solution)/shard_map/ppermute | solution.py:392
  174.1 2.5 %copy-start.1 = (f32[1024,768]{1,0:T(8,128)S(1)}, f32[1024,768]{1,0:T(8,128)}, u32[]{:S(2)}) copy-start(f32[1024,768]{1,0:T(8,128)} %get-tuple-element.65) | copy-start | bytes 9437188
  178.0 1.6 copy-start
